TPU v7x, 32 devices: a whole 2x2x4 slice. The times are simulated.
32 devices in a mesh: region: 8 (over y, x, core), tile: 4 (over z).
Axes of the slice: x: 2, y: 2, z: 4, core: 2. Of those that a mesh axis runs over, the one named last changes fastest.
Arguments:
- params: float32 [256, 59, 128], P(('region', 'tile')), may hold values from -6 to 6
- first_moment: float32 [256, 59, 128], P(('region', 'tile')), may hold values from -0.006 to 0.006
- second_moment: float32 [256, 59, 128], P(('region', 'tile')), may hold values from 1e-09 to 2e-05
- view_basis: float32 [16], replicated, may hold values from -1.5 to 1.5
- target: float32 [32, 3, 1024], P(('region', 'tile')), may hold values from 0 to 1
- tile_blocks: int32 [32, 4], P(('region', 'tile')), may hold values from 0 to 31, as said below
- moving: int32 [32, 4], P(('region', 'tile')), may hold values from 0 to 7, as said below
Outputs:
- new_params: float32 [256, 59, 128], P(('region', 'tile'))
- new_first: float32 [256, 59, 128], P(('region', 'tile'))
- new_second: float32 [256, 59, 128], P(('region', 'tile'))
- image: float32 [32, 3, 1024], P(('region', 'tile'))
Inputs may be any that keep to these rules, and one draw needn't show every extreme that they name: `tile_blocks`: row i lists the blocks of the tile of device i front to back, as ids within that device's region; it names exactly one block of each of the region's 4 devices, the device at tile index k owning ids k * 8 to (k + 1) * 8 - 1. `moving`: row i names 4 different blocks of device i, counted from 0 within the device.
All inputs are finite; a program needn't handle non-finite values.
Results may differ from a plain program's by a relative error of at most 0.0003.
Values sent between devices are 32-bit elements; how exact they have to be, the bound alone decides.
No kernel may reach another device: no remote copies, remote signals or barrier semaphores. Data moves between devices by JAX's collectives and lax.ppermute only.
A program may use at most 64 MiB of HBM per device.

v0:
```python
import jax
import jax.numpy as jnp
from jax import lax
from jax.sharding import PartitionSpec as P

SH = 16
TILE_SIDE = 32
PIX = 1024


beta_one = 0.9
beta_two = 0.999
adam_eps = 1e-08
adam_step = 10.0
highest = lax.Precision.HIGHEST


def shifted(shard, axis, by):
    peers = lax.axis_size(axis)
    return lax.ppermute(shard, axis, [(i, (i + by) % peers) for i in range(peers)])


def step_rates():
    return jnp.concatenate(
        [
            jnp.full((3,), 0.002, jnp.float32),
            jnp.full((3,), 0.005, jnp.float32),
            jnp.full((4,), 0.001, jnp.float32),
            jnp.full((1,), 0.05, jnp.float32),
            jnp.full((3 * SH,), 0.0025, jnp.float32),
        ]
    )


def project(values, view_basis):
    side = float(TILE_SIDE)
    mean_x = 0.5 * side + 0.375 * side * jnp.tanh(values[..., 0, :])
    mean_y = 0.5 * side + 0.375 * side * jnp.tanh(values[..., 1, :])
    zoom_factor = 3.0 / (1.0 + jax.nn.softplus(values[..., 2, :]))
    extent = side / 32.0 * 1.5 * jnp.exp(jnp.tanh(values[..., 3:6, :]))
    extent_sq = extent * extent
    rotation = values[..., 6:10, :]
    rot_norm = jnp.sqrt(jnp.sum(rotation * rotation, axis=-2, keepdims=True))
    rotation = rotation / jnp.maximum(rot_norm, 1.0)
    quat_w = rotation[..., 0, :]
    quat_x = rotation[..., 1, :]
    quat_y = rotation[..., 2, :]
    quat_z = rotation[..., 3, :]
    upper_row = [
        1.0 - 2.0 * (quat_y * quat_y + quat_z * quat_z),
        2.0 * (quat_x * quat_y - quat_w * quat_z),
        2.0 * (quat_x * quat_z + quat_w * quat_y),
    ]
    lower_row = [
        2.0 * (quat_x * quat_y + quat_w * quat_z),
        1.0 - 2.0 * (quat_x * quat_x + quat_z * quat_z),
        2.0 * (quat_y * quat_z - quat_w * quat_x),
    ]
    zoom_sq = zoom_factor * zoom_factor
    cov_xx = (
        zoom_sq
        * (
            upper_row[0] * upper_row[0] * extent_sq[..., 0, :]
            + upper_row[1] * upper_row[1] * extent_sq[..., 1, :]
            + upper_row[2] * upper_row[2] * extent_sq[..., 2, :]
        )
        + 0.3
    )
    cov_yy = (
        zoom_sq
        * (
            lower_row[0] * lower_row[0] * extent_sq[..., 0, :]
            + lower_row[1] * lower_row[1] * extent_sq[..., 1, :]
            + lower_row[2] * lower_row[2] * extent_sq[..., 2, :]
        )
        + 0.3
    )
    cov_xy = zoom_sq * (
        upper_row[0] * lower_row[0] * extent_sq[..., 0, :]
        + upper_row[1] * lower_row[1] * extent_sq[..., 1, :]
        + upper_row[2] * lower_row[2] * extent_sq[..., 2, :]
    )
    determinant = cov_xx * cov_yy - cov_xy * cov_xy
    opacity = 0.99 * jax.nn.sigmoid(values[..., 10, :] - 4.0)
    harmonics = values[..., 11:, :].reshape(values.shape[:-2] + (3, SH, values.shape[-1]))
    colours = jax.nn.sigmoid(
        jnp.einsum("...ckg,k->...cg", harmonics, view_basis, precision=highest)
    )
    return jnp.stack(
        [
            mean_x,
            mean_y,
            cov_yy / determinant,
            -cov_xy / determinant,
            cov_xx / determinant,
            opacity,
            colours[..., 0, :],
            colours[..., 1, :],
            colours[..., 2, :],
        ],
        axis=-2,
    )


def composite(splat_list, wanted):
    width = splat_list.shape[2]
    pixels = jnp.arange(PIX)
    centre_x = (pixels % TILE_SIDE).astype(jnp.float32) + 0.5
    centre_y = (pixels // TILE_SIDE).astype(jnp.float32) + 0.5
    strict = (jnp.arange(width)[:, None] < jnp.arange(width)[None, :]).astype(jnp.float32)
    inclusive_mask = (jnp.arange(width)[:, None] <= jnp.arange(width)[None, :]).astype(jnp.float32)

    def footprint(splats):
        offset_x = centre_x[:, None] - splats[0][None, :]
        offset_y = centre_y[:, None] - splats[1][None, :]
        exponent = -0.5 * (
            splats[2] * offset_x * offset_x
            + 2.0 * splats[3] * offset_x * offset_y
            + splats[4] * offset_y * offset_y
        )
        spread = jnp.exp(exponent)
        alphas = splats[5] * spread
        log_keep = jnp.log1p(-alphas)
        return (offset_x, offset_y, spread, alphas, log_keep)

    def forward(running, splats):
        log_trans, colour_sum = running
        offset_x, offset_y, spread, alphas, log_keep = footprint(splats)
        log_here = log_trans[:, None] + jnp.dot(log_keep, strict, precision=highest)
        weight = alphas * jnp.exp(log_here)
        colour_sum = colour_sum + jnp.dot(weight, splats[6:9].T, precision=highest)
        return ((log_trans + jnp.sum(log_keep, axis=1), colour_sum), None)

    initial = (jnp.zeros((PIX,), jnp.float32), jnp.zeros((PIX, 3), jnp.float32))
    (_, colour_sum), _ = lax.scan(forward, initial, splat_list)
    errors = 2.0 * (colour_sum - wanted.T)
    totals = jnp.sum(errors * colour_sum, axis=1)

    def backward(running, splats):
        log_trans, before = running
        offset_x, offset_y, spread, alphas, log_keep = footprint(splats)
        log_here = log_trans[:, None] + jnp.dot(log_keep, strict, precision=highest)
        trans = jnp.exp(log_here)
        weight = alphas * trans
        shading = jnp.dot(errors, splats[6:9], precision=highest)
        covered = before[:, None] + jnp.dot(weight * shading, inclusive_mask, precision=highest)
        d_alpha = trans * shading - (totals[:, None] - covered) / (1.0 - alphas)
        d_exponent = d_alpha * alphas
        d_colour = jnp.dot(errors.T, weight, precision=highest)
        gradient = jnp.stack(
            [
                jnp.sum(d_exponent * (splats[2] * offset_x + splats[3] * offset_y), axis=0),
                jnp.sum(d_exponent * (splats[3] * offset_x + splats[4] * offset_y), axis=0),
                jnp.sum(-0.5 * offset_x * offset_x * d_exponent, axis=0),
                jnp.sum(-offset_x * offset_y * d_exponent, axis=0),
                jnp.sum(-0.5 * offset_y * offset_y * d_exponent, axis=0),
                jnp.sum(d_alpha * spread, axis=0),
                d_colour[0],
                d_colour[1],
                d_colour[2],
            ]
        )
        return ((log_trans + jnp.sum(log_keep, axis=1), covered[:, -1]), gradient)

    _, splat_grads = lax.scan(
        backward, (jnp.zeros((PIX,), jnp.float32), jnp.zeros((PIX,), jnp.float32)), splat_list
    )
    return (colour_sum.T, splat_grads)


def on_device(params, first_moment, second_moment, view_basis, target, tile_blocks, moving):
    per_device = params.shape[0]
    projected = project(params, view_basis)
    listed = tile_blocks[0]
    region_blocks = lax.all_gather(projected, "tile", axis=0, tiled=True)
    splat_list = jnp.take(region_blocks, listed, axis=0)
    picture, splat_grads = composite(splat_list, target[0])
    region_count = lax.axis_size("tile") * per_device
    onehot = (listed[:, None] == jnp.arange(region_count)[None, :]).astype(jnp.float32)
    dense_grads = jnp.einsum("lr,lkg->rkg", onehot, splat_grads, precision=highest)
    proj_grads = lax.psum_scatter(dense_grads, "tile", scatter_dimension=0, tiled=True)
    _, pullback = jax.vjp(lambda values: project(values, view_basis), params)
    gradient = pullback(proj_grads)[0]
    rates = step_rates()[:, None]
    moment_one = beta_one * first_moment + (1.0 - beta_one) * gradient
    moment_two = beta_two * second_moment + (1.0 - beta_two) * gradient * gradient
    stepped = params - rates * (moment_one / (1.0 - beta_one**adam_step)) / (
        jnp.sqrt(moment_two / (1.0 - beta_two**adam_step)) + adam_eps
    )
    leaving_ids = moving[0]
    incoming = shifted(
        (
            jnp.take(stepped, leaving_ids, axis=0),
            jnp.take(moment_one, leaving_ids, axis=0),
            jnp.take(moment_two, leaving_ids, axis=0),
        ),
        "region",
        1,
    )
    new_params = stepped.at[leaving_ids].set(incoming[0])
    new_first = moment_one.at[leaving_ids].set(incoming[1])
    new_second = moment_two.at[leaving_ids].set(incoming[2])
    return (new_params, new_first, new_second, picture[None])


def solution(mesh):
    in_specs = (
        P(("region", "tile"), None, None),
        P(("region", "tile"), None, None),
        P(("region", "tile"), None, None),
        P(),
        P(("region", "tile"), None, None),
        P(("region", "tile"), None),
        P(("region", "tile"), None),
    )
    out_specs = (
        P(("region", "tile"), None, None),
        P(("region", "tile"), None, None),
        P(("region", "tile"), None, None),
        P(("region", "tile"), None, None),
    )
    return jax.shard_map(
        on_device, mesh=mesh, in_specs=in_specs, out_specs=out_specs, check_vma=False
    )
```

profile of v0, /device:TPU:0, one launch (start us, length us, event | category | flops | bytes accessed | tf_op | source)
XLA Modules:
  0.0 99.5 jit_solution(8393477302530917290)
XLA Ops:
  11.3 15.2 %all_gather.3 = f32[32,9,128]{2,0,1:T(8,128)S(1)} all-gather(f32[8,9,128]{2,0,1:T(8,128)S(1)} %constant_dynamic-update-slice_fusion), channel_id=1, replica_groups=mesh['region'=8,'tile'=4] {'tile'}, dimensions={0}, use_global_device_ids=true | all-gather | bytes 184320 | tf_op jit(solution)/shard_map/all_gather | solution.py:175
  27.2 9.0 %while.28 = (s32[]{:T(128)}, f32[1024]{0:T(1024)S(1)}, f32[1024,3]{0,1:T(4,128)S(1)}, f32[4,9,128]{2,1,0:T(8,128)S(1)}, s32[]{:T(128)}, /*index=5*/s32[]{:T(128)}, s32[]{}, s32[]{}, s32[]{}, s32[]{}, /*index=10*/s32[]{}, s32[]{}) while((s32[]{:T(128)}, f32[1024]{0:T(1024)S(1)}, f32[1024,3]{0,1:T(4,128)S(1)}, ...), condition=%wide.region_3.4_spmd.clone, body=%wide.region_1.3_spmd.clone.sunk | while | flops 211475584 | bytes 1140968 | solution.py:135
  27.8 1.1 %fusion.161 = f32[1024,128]{1,0:T(8,128)S(1)} fusion(f32[1024]{0:T(1024)S(1)} %get-tuple-element.376, f32[128]{0:T(128)S(1)} %get-tuple-element.367, f32[128]{0:T(128)S(1)} %get-tuple-element.368, f32[1024]{0:T(1024)S(1)} %get-tuple-element.369, f32[128]{0:T(128)S(1)} %get-tuple-element.370, f32[128]{0:T(128)S(1)} %get-tuple-element.371, ...), kind=kOutput, calls=%fused_computation.16.clone.1 | convolution fusion | flops 204898304 | bytes 539648 | tf_op jit(solution)/shard_map/while/body/eval_jaxpr/dot_general | solution.py:129
  30.1 1.1 %fusion.161 = f32[1024,128]{1,0:T(8,128)S(1)} fusion(f32[1024]{0:T(1024)S(1)} %get-tuple-element.376, f32[128]{0:T(128)S(1)} %get-tuple-element.367, f32[128]{0:T(128)S(1)} %get-tuple-element.368, f32[1024]{0:T(1024)S(1)} %get-tuple-element.369, f32[128]{0:T(128)S(1)} %get-tuple-element.370, f32[128]{0:T(128)S(1)} %get-tuple-element.371, ...), kind=kOutput, calls=%fused_computation.16.clone.1 | convolution fusion | flops 204898304 | bytes 539648 | tf_op jit(solution)/shard_map/while/body/eval_jaxpr/dot_general | solution.py:129
  32.3 1.1 %fusion.161 = f32[1024,128]{1,0:T(8,128)S(1)} fusion(f32[1024]{0:T(1024)S(1)} %get-tuple-element.376, f32[128]{0:T(128)S(1)} %get-tuple-element.367, f32[128]{0:T(128)S(1)} %get-tuple-element.368, f32[1024]{0:T(1024)S(1)} %get-tuple-element.369, f32[128]{0:T(128)S(1)} %get-tuple-element.370, f32[128]{0:T(128)S(1)} %get-tuple-element.371, ...), kind=kOutput, calls=%fused_computation.16.clone.1 | convolution fusion | flops 204898304 | bytes 539648 | tf_op jit(solution)/shard_map/while/body/eval_jaxpr/dot_general | solution.py:129
  34.6 1.1 %fusion.161 = f32[1024,128]{1,0:T(8,128)S(1)} fusion(f32[1024]{0:T(1024)S(1)} %get-tuple-element.376, f32[128]{0:T(128)S(1)} %get-tuple-element.367, f32[128]{0:T(128)S(1)} %get-tuple-element.368, f32[1024]{0:T(1024)S(1)} %get-tuple-element.369, f32[128]{0:T(128)S(1)} %get-tuple-element.370, f32[128]{0:T(128)S(1)} %get-tuple-element.371, ...), kind=kOutput, calls=%fused_computation.16.clone.1 | convolution fusion | flops 204898304 | bytes 539648 | tf_op jit(solution)/shard_map/while/body/eval_jaxpr/dot_general | solution.py:129
  36.3 20.6 %while.29 = (s32[]{:T(128)}, f32[1024]{0:T(1024)S(1)}, f32[1024]{0:T(1024)S(1)}, f32[4,9,128]{2,0,1:T(4,128)S(1)}, f32[4,9,128]{2,1,0:T(8,128)S(1)}, /*index=5*/...) while((s32[]{:T(128)}, f32[1024]{0:T(1024)S(1)}, ...), condition=%wide.region_13.14_spmd.clone, body=%wide.region_5.13_spmd.clone.sunk | while | flops 423183744 | bytes 3303176 | solution.py:165
  36.4 1.0 fusion.167
  37.3 1.0 %convolution_bitcast_fusion.4 = f32[1024,128]{1,0:T(8,128)S(1)} fusion(f32[1024,3]{0,1:T(4,128)S(1)} %get-tuple-element.472, f32[4,9,128]{2,1,0:T(8,128)S(1)} %get-tuple-element.471, s32[]{:T(128)} %get-tuple-element.452, s32[]{:T(128)S(6)} %add.964), kind=kOutput, calls=%fused_computation.79.clone.1 | convolution fusion | flops 4718592 | bytes 542728 | tf_op jit(solution)/shard_map/while/body/eval_jaxpr/dot_general | solution.py:145
  38.3 1.8 %fusion.168 = (f32[128]{0:T(128)S(1)}, f32[128]{0:T(128)S(1)}, f32[128]{0:T(128)S(1)}, f32[128]{0:T(128)S(1)}, f32[128]{0:T(128)S(1)}, /*index=5*/f32[128]{0:T(128)S(1)}, f32[1024]{0:T(1024)S(1)}, f32[1024,128]{1,0:T(8,128)S(1)}) fusion(f32[128]{0:T(128)S(1)} %get-tuple-element.384, f32[1024]{0:T(1024)S(1)} %get-tuple-element.385, ...), kind=kOutput, calls=%fused_computation.98.clone.1 | convolution fusion | flops 208828672 | bytes 1600000 | tf_op jit(solution)/shard_map/while/body/eval_jaxpr/dot_general | solution.py:146
  41.5 1.0 fusion.167
  42.5 1.0 %convolution_bitcast_fusion.4 = f32[1024,128]{1,0:T(8,128)S(1)} fusion(f32[1024,3]{0,1:T(4,128)S(1)} %get-tuple-element.472, f32[4,9,128]{2,1,0:T(8,128)S(1)} %get-tuple-element.471, s32[]{:T(128)} %get-tuple-element.452, s32[]{:T(128)S(6)} %add.964), kind=kOutput, calls=%fused_computation.79.clone.1 | convolution fusion | flops 4718592 | bytes 542728 | tf_op jit(solution)/shard_map/while/body/eval_jaxpr/dot_general | solution.py:145
  43.5 1.8 %fusion.168 = (f32[128]{0:T(128)S(1)}, f32[128]{0:T(128)S(1)}, f32[128]{0:T(128)S(1)}, f32[128]{0:T(128)S(1)}, f32[128]{0:T(128)S(1)}, /*index=5*/f32[128]{0:T(128)S(1)}, f32[1024]{0:T(1024)S(1)}, f32[1024,128]{1,0:T(8,128)S(1)}) fusion(f32[128]{0:T(128)S(1)} %get-tuple-element.384, f32[1024]{0:T(1024)S(1)} %get-tuple-element.385, ...), kind=kOutput, calls=%fused_computation.98.clone.1 | convolution fusion | flops 208828672 | bytes 1600000 | tf_op jit(solution)/shard_map/while/body/eval_jaxpr/dot_general | solution.py:146
  46.6 1.0 fusion.167
  47.6 1.0 %convolution_bitcast_fusion.4 = f32[1024,128]{1,0:T(8,128)S(1)} fusion(f32[1024,3]{0,1:T(4,128)S(1)} %get-tuple-element.472, f32[4,9,128]{2,1,0:T(8,128)S(1)} %get-tuple-element.471, s32[]{:T(128)} %get-tuple-element.452, s32[]{:T(128)S(6)} %add.964), kind=kOutput, calls=%fused_computation.79.clone.1 | convolution fusion | flops 4718592 | bytes 542728 | tf_op jit(solution)/shard_map/while/body/eval_jaxpr/dot_general | solution.py:145
  48.6 1.8 %fusion.168 = (f32[128]{0:T(128)S(1)}, f32[128]{0:T(128)S(1)}, f32[128]{0:T(128)S(1)}, f32[128]{0:T(128)S(1)}, f32[128]{0:T(128)S(1)}, /*index=5*/f32[128]{0:T(128)S(1)}, f32[1024]{0:T(1024)S(1)}, f32[1024,128]{1,0:T(8,128)S(1)}) fusion(f32[128]{0:T(128)S(1)} %get-tuple-element.384, f32[1024]{0:T(1024)S(1)} %get-tuple-element.385, ...), kind=kOutput, calls=%fused_computation.98.clone.1 | convolution fusion | flops 208828672 | bytes 1600000 | tf_op jit(solution)/shard_map/while/body/eval_jaxpr/dot_general | solution.py:146
  51.8 1.0 fusion.167
  52.8 1.0 %convolution_bitcast_fusion.4 = f32[1024,128]{1,0:T(8,128)S(1)} fusion(f32[1024,3]{0,1:T(4,128)S(1)} %get-tuple-element.472, f32[4,9,128]{2,1,0:T(8,128)S(1)} %get-tuple-element.471, s32[]{:T(128)} %get-tuple-element.452, s32[]{:T(128)S(6)} %add.964), kind=kOutput, calls=%fused_computation.79.clone.1 | convolution fusion | flops 4718592 | bytes 542728 | tf_op jit(solution)/shard_map/while/body/eval_jaxpr/dot_general | solution.py:145
  53.8 1.8 %fusion.168 = (f32[128]{0:T(128)S(1)}, f32[128]{0:T(128)S(1)}, f32[128]{0:T(128)S(1)}, f32[128]{0:T(128)S(1)}, f32[128]{0:T(128)S(1)}, /*index=5*/f32[128]{0:T(128)S(1)}, f32[1024]{0:T(1024)S(1)}, f32[1024,128]{1,0:T(8,128)S(1)}) fusion(f32[128]{0:T(128)S(1)} %get-tuple-element.384, f32[1024]{0:T(1024)S(1)} %get-tuple-element.385, ...), kind=kOutput, calls=%fused_computation.98.clone.1 | convolution fusion | flops 208828672 | bytes 1600000 | tf_op jit(solution)/shard_map/while/body/eval_jaxpr/dot_general | solution.py:146
  56.9 1.0 %fusion.122 = f32[32,9,128]{2,0,1:T(8,128)} fusion(f32[4,9,128]{2,0,1:T(4,128)S(1)} %get-tuple-element.100, s32[4]{0:T(128)S(1)} %bitcast.135), kind=kOutput, calls=%fused_computation.272 | convolution fusion | flops 1769600 | bytes 165904 | tf_op jit(solution)/shard_map/lr,lkg->rkg/dot_general | solution.py:180
  59.1 19.5 %reduce-scatter.2.cloned.1.call-done = f32[8,9,128]{2,0,1:T(8,128)} async-done(((f32[32,9,128]{2,0,1:T(8,128)}), f32[8,9,128]{2,0,1:T(8,128)}) %reduce-scatter.2.cloned.1.call-update) | async-done | bytes 36880 | tf_op jit(solution)/shard_map/reduce_scatter | solution.py:181
  82.9 1.6 %collective-permute-start.1 = (f32[4,59,128]{2,1,0:T(8,128)S(1)}, f32[4,59,128]{2,1,0:T(8,128)S(1)}, u32[]{:S(2)}, u32[]{:S(2)}) collective-permute-start(f32[4,59,128]{2,1,0:T(8,128)S(1)} %get-tuple-element.274), channel_id=1, source_target_pairs={{0,4},{4,8},{8,12},{12,16},{16,20},{20,24},{24,28},{28,0},{1,5},{5... | collective-permute-start | bytes 362504 | tf_op jit(solution)/shard_map/ppermute | solution.py:20
  84.5 3.6 %collective-permute-done.2 = f32[4,59,128]{2,1,0:T(8,128)S(1)} collective-permute-done((f32[4,59,128]{2,1,0:T(8,128)S(1)}, f32[4,59,128]{2,1,0:T(8,128)S(1)}, u32[]{:S(2)}, u32[]{:S(2)}) %collective-permute-start.2) | collective-permute-done | bytes 120864 | tf_op jit(solution)/shard_map/ppermute | solution.py:20
  88.8 0.8 copy.41
  (140 shorter events, 23.6 us)
Async XLA Ops:
  7.2 3.0 %copy-start = (f32[8,59,128]{2,0,1:T(8,128)S(1)}, f32[8,59,128]{2,0,1:T(8,128)}, u32[]{:S(2)}) copy-start(f32[8,59,128]{2,0,1:T(8,128)} %param.13) | copy-start | bytes 724996
  7.2 71.5 %reduce-scatter.2.cloned.1.call-start = ((), (), s32[]{:S(2)}) async-start(), calls=%async_computation.1 | async-start | bytes 184320 | tf_op jit(solution)/shard_map/reduce_scatter | solution.py:181
  9.4 0.7 copy-start.6
  10.1 0.9 slice-start
  10.3 0.8 copy-start.5
  27.2 9.0 %copy-start.4 = (f32[1,3,1024]{2,0,1:T(1,128)S(1)}, f32[1,3,1024]{2,0,1:T(1,128)}, u32[]{:S(2)}) copy-start(f32[1,3,1024]{2,0,1:T(1,128)} %param.17) | copy-start | bytes 36868
  57.9 0.7 copy-start.8
  78.7 0.8 copy-start.3
  79.6 0.9 copy-start.1
  79.6 1.1 %copy-start.2 = (f32[8,59,128]{2,0,1:T(8,128)S(1)}, f32[8,59,128]{2,0,1:T(8,128)}, u32[]{:S(2)}) copy-start(f32[8,59,128]{2,0,1:T(8,128)} %param.15) | copy-start | bytes 724996
  79.8 0.8 copy-start.7
  82.8 5.3 %collective-permute-start.2 = (f32[4,59,128]{2,1,0:T(8,128)S(1)}, f32[4,59,128]{2,1,0:T(8,128)S(1)}, u32[]{:S(2)}, u32[]{:S(2)}) collective-permute-start(f32[4,59,128]{2,1,0:T(8,128)S(1)} %get-tuple-element.273), channel_id=1, source_target_pairs={{0,4},{4,8},{8,12},{12,16},{16,20},{20,24},{24,28},{28,0},{1,5},{5... | collective-permute-start | bytes 362504 | tf_op jit(solution)/shard_map/ppermute | solution.py:20
  82.9 6.8 %collective-permute-start.1 = (f32[4,59,128]{2,1,0:T(8,128)S(1)}, f32[4,59,128]{2,1,0:T(8,128)S(1)}, u32[]{:S(2)}, u32[]{:S(2)}) collective-permute-start(f32[4,59,128]{2,1,0:T(8,128)S(1)} %get-tuple-element.274), channel_id=1, source_target_pairs={{0,4},{4,8},{8,12},{12,16},{16,20},{20,24},{24,28},{28,0},{1,5},{5... | collective-permute-start | bytes 362504 | tf_op jit(solution)/shard_map/ppermute | solution.py:20
  84.5 6.7 %collective-permute-start = (f32[4,59,128]{2,1,0:T(8,128)S(1)}, f32[4,59,128]{2,1,0:T(8,128)S(1)}, u32[]{:S(2)}, u32[]{:S(2)}) collective-permute-start(f32[4,59,128]{2,1,0:T(8,128)S(1)} %get-tuple-element.275), channel_id=1, source_target_pairs={{0,4},{4,8},{8,12},{12,16},{16,20},{20,24},{24,28},{28,0},{1,5},{5... | collective-permute-start | bytes 362504 | tf_op jit(solution)/shard_map/ppermute | solution.py:20
Sparse Core Ops, SparseCore 0:
  58.0 20.6 reduce-scatter.1
where the time goes:
time: 99.8 us; the launch traced here: 99.5 us
  matrix products  25.5 us (26%)
  waiting for transfers between devices  23.2 us (23%)
  blocking collectives  15.2 us (15%)
  between operations  14.4 us (14%)
  local copies, waits for them, and re-layouts  12.6 us (13%)
  other arithmetic  6.27 us (6%)
  starting transfers between devices  1.75 us (2%)
    reduce_scatter x1, waiting for transfers between devices, on_device(): lax.psum_scatter(dense_grads, 'tile', scatter_dimension=0, tiled=True)  19.5 us
    all_gather x1, blocking collectives, on_device(): region_blocks = lax.all_gather(projected, 'tile', axis=0, tiled=True)  15.2 us
    dot_general x4, matrix products, backward(): jnp.dot(weight * shading, inclusive_mask, precision=highest)  7.1 us
    unnamed x21, local copies, waits for them, and re-layouts  4.67 us
    dot_general x4, matrix products, forward(): log_here = log_trans[:, None] + jnp.dot(log_keep, strict, precision=highest)  4.21 us
    dot_general x4, matrix products, backward(): shading = jnp.dot(errors, splats[6:9], precision=highest)  4.01 us
    dot_general x4, matrix products, backward(): log_here = log_trans[:, None] + jnp.dot(log_keep, strict, precision=highest)  3.89 us
    ppermute x3, waiting for transfers between devices, shifted(): lax.ppermute(shard, axis, [(i, (i + by) % peers) for i in range(peers)])  3.62 us
  transfers between devices with their start and end apart: 4, of which 2 were waited for; matrix products, arithmetic and copies ran while one was open for 4% of the time, Pallas kernels for 0%

commit v1 on v0

v1 whole, which is shorter than its diff:
```python
import functools
import math
import jax
import jax.numpy as jnp
import numpy as np
from jax import lax
from jax.experimental import pallas as pl
from jax.experimental.pallas import tpu as pltpu
from jax.sharding import PartitionSpec as P

SH = 16
TILE_SIDE = 32
NPROJ = 9
GRADS = 16
HALF = TILE_SIDE / 2.0

beta_one = 0.9
beta_two = 0.999
adam_eps = 1e-08
adam_step = 10.0
LOG2E = math.log2(math.e)


def rate_of(row):
    if row < 3:
        return 0.002
    if row < 6:
        return 0.005
    if row < 10:
        return 0.001
    if row < 11:
        return 0.05
    return 0.0025


def sigmoid(x):
    return 1.0 / (1.0 + jnp.exp(-x))


def geometry(p):
    v = {}
    v["tx"] = jnp.tanh(p(0))
    v["ty"] = jnp.tanh(p(1))
    depth = p(2)
    softplus = jnp.maximum(depth, 0.0) + jnp.log(1.0 + jnp.exp(-jnp.abs(depth)))
    v["f"] = 3.0 / (1.0 + softplus)
    v["z"] = v["f"] * v["f"]
    v["ts"] = [jnp.tanh(p(3 + k)) for k in range(3)]
    v["e"] = [2.25 * jnp.exp(2.0 * t) for t in v["ts"]]
    q = [p(6 + k) for k in range(4)]
    norm = jnp.sqrt((q[0] * q[0] + q[1] * q[1]) + (q[2] * q[2] + q[3] * q[3]))
    inv = 1.0 / jnp.maximum(norm, 1.0)
    v["norm"] = norm
    v["inv"] = inv
    w, x, y, z = [a * inv for a in q]
    v["q"] = (w, x, y, z)
    U = [1.0 - 2.0 * (y * y + z * z), 2.0 * (x * y - w * z), 2.0 * (x * z + w * y)]
    L = [2.0 * (x * y + w * z), 1.0 - 2.0 * (x * x + z * z), 2.0 * (y * z - w * x)]
    v["U"], v["L"] = U, L
    e = v["e"]
    v["sxx"] = U[0] * U[0] * e[0] + U[1] * U[1] * e[1] + U[2] * U[2] * e[2]
    v["syy"] = L[0] * L[0] * e[0] + L[1] * L[1] * e[1] + L[2] * L[2] * e[2]
    v["sxy"] = U[0] * L[0] * e[0] + U[1] * L[1] * e[1] + U[2] * L[2] * e[2]
    v["xx"] = v["z"] * v["sxx"] + 0.3
    v["yy"] = v["z"] * v["syy"] + 0.3
    v["xy"] = v["z"] * v["sxy"]
    v["idet"] = 1.0 / (v["xx"] * v["yy"] - v["xy"] * v["xy"])
    v["A"] = v["yy"] * v["idet"]
    v["B"] = -v["xy"] * v["idet"]
    v["C"] = v["xx"] * v["idet"]
    v["so"] = sigmoid(p(10) - 4.0)
    return v


def colour(p, c, basis):
    total = p(11 + SH * c) * basis(0)
    for k in range(1, SH):
        total = total + p(11 + SH * c + k) * basis(k)
    return sigmoid(total)


def project_kernel(moving_ref, basis_ref, p_ref, f_ref, s_ref, proj_ref, leave_ref):
    rows, blocks, lanes = p_ref.shape
    moves = leave_ref.shape[1]
    p = lambda i: p_ref[i]
    v = geometry(p)
    proj_ref[0] = 0.375 * TILE_SIDE * v["tx"]
    proj_ref[1] = 0.375 * TILE_SIDE * v["ty"]
    proj_ref[2] = v["A"]
    proj_ref[3] = v["B"]
    proj_ref[4] = v["C"]
    proj_ref[5] = 0.99 * v["so"]
    for c in range(3):
        proj_ref[6 + c] = colour(p, c, lambda k: basis_ref[k])
    slot = lax.broadcasted_iota(jnp.int32, (blocks, lanes), 0)
    pick = jnp.zeros((blocks, lanes), jnp.int32)
    for m in range(moves):
        pick = jnp.where(slot == m, moving_ref[0, m], pick)
    for a, ref in enumerate((p_ref, f_ref, s_ref)):
        for i in range(rows):
            leave_ref[a * rows + i] = jnp.take_along_axis(ref[i], pick, axis=0)[:moves]


def composite_kernel(meta_ref, *refs):
    peers = meta_ref.shape[0] // 2
    sources = refs[:peers]
    target_ref = refs[peers]
    image_ref = refs[peers + 1]
    grad_refs = refs[peers + 2 : 2 * peers + 2]
    pbuf, abuf, wbuf, ebuf, colq, errbuf, gbuf = refs[2 * peers + 2 :]
    lanes = pbuf.shape[2]
    width = colq.shape[1]
    chunks = abuf.shape[0] // width
    for d in range(peers):
        pos = meta_ref[d]
        loc = meta_ref[peers + d]
        for r in range(NPROJ):
            pbuf[pos, pl.ds(r, 1), :] = sources[d][r, pl.ds(loc, 1), :]

    lane = lax.broadcasted_iota(jnp.int32, (8, lanes), 1)
    px = (lane % TILE_SIDE).astype(jnp.float32) + (0.5 - HALF)
    py = (lane // TILE_SIDE).astype(jnp.float32) + (0.5 - HALF)
    step = float(lanes // TILE_SIDE)

    def alphas(j, _):
        block = pbuf[j]
        scale = jnp.concatenate(
            [
                jnp.full((2, lanes), 1.0, jnp.float32),
                jnp.full((1, lanes), -0.5 * LOG2E, jnp.float32),
                jnp.full((1, lanes), -LOG2E, jnp.float32),
                jnp.full((1, lanes), -0.5 * LOG2E, jnp.float32),
                jnp.full((11, lanes), 1.0, jnp.float32),
            ],
            axis=0,
        )
        columns = (block * scale).T
        for u in range(lanes // 8):
            part = columns[u * 8 : (u + 1) * 8]
            wide = lambda k: jnp.broadcast_to(part[:, k : k + 1], (8, lanes))
            row = pl.multiple_of(j * lanes + u * 8, 8)
            dx = px - wide(0)
            ax = wide(2) * dx * dx
            bx = wide(3) * dx
            dy0 = py - wide(1)
            conic = wide(4)
            opacity = wide(5)
            for k in range(3):
                colq[k, pl.ds(row, 8), :] = wide(6 + k)
            for c in range(chunks):
                dy = dy0 + step * c
                power = (conic * dy + bx) * dy + ax
                abuf[pl.ds(c * width + row, 8), :] = opacity * jnp.exp2(power)
        return 0

    lax.fori_loop(0, width // lanes, alphas, 0)

    unroll = 8

    def forward(i, running):
        trans, image = running
        for u in range(unroll):
            g = i * unroll + u
            alpha = abuf[pl.ds(g, chunks, stride=width), :]
            weight = trans * alpha
            trans = trans * (1.0 - alpha)
            wbuf[pl.ds(g, chunks, stride=width), :] = weight
            image = tuple(
                image[k] + weight * jnp.broadcast_to(colq[k, pl.ds(g, 1), :], (chunks, lanes)) for k in range(3)
            )
        return (trans, image)

    zero = jnp.zeros((chunks, lanes), jnp.float32)
    _, image = lax.fori_loop(0, width // unroll, forward, (zero + 1.0, (zero, zero, zero)))
    errors = []
    errbuf[...] = jnp.zeros_like(errbuf)
    for k in range(3):
        image_ref[k] = image[k]
        errors.append(2.0 * (image[k] - target_ref[k]))
        errbuf[k * chunks : (k + 1) * chunks, :] = errors[k]

    def backward(i, behind):
        for u in range(unroll):
            g = width - 1 - (i * unroll + u)
            shade = [errors[k] * jnp.broadcast_to(colq[k, pl.ds(g, 1), :], (chunks, lanes)) for k in range(3)]
            alpha = abuf[pl.ds(g, chunks, stride=width), :]
            weight = wbuf[pl.ds(g, chunks, stride=width), :]
            ahead = (shade[0] + shade[1]) + shade[2] - behind
            behind = behind + alpha * ahead
            ebuf[pl.ds(g, chunks, stride=width), :] = weight * ahead
        return behind

    lax.fori_loop(0, width // unroll, backward, zero)

    which = lax.broadcasted_iota(jnp.int32, (8, lanes), 0)
    dot = functools.partial(
        lax.dot_general,
        dimension_numbers=(((1,), (1,)), ((), ())),
        precision=lax.Precision.HIGHEST,
        preferred_element_type=jnp.float32,
    )
    moments = jnp.zeros((8, width), jnp.float32)
    shades = jnp.zeros((8, width), jnp.float32)
    for c in range(chunks):
        y = py + step * c
        basis = jnp.where(which == 0, 1.0, 0.0)
        for r, value in enumerate((px, y, px * px, px * y, y * y)):
            basis = jnp.where(which == r + 1, value, basis)
        moments = moments + dot(basis, ebuf[c * width : (c + 1) * width, :])
        shades = shades + dot(errbuf[pl.ds(c, 8, stride=chunks), :], wbuf[c * width : (c + 1) * width, :])
    for j in range(width // lanes):
        part = moments[:, j * lanes : (j + 1) * lanes]
        m0, m1x, m1y, mxx, mxy, myy = [part[r : r + 1] for r in range(6)]
        mx, my, ca, cb, cc, op = [pbuf[j, r : r + 1, :] for r in range(6)]
        sx = m1x - mx * m0
        sy = m1y - my * m0
        sxx = mxx - mx * m1x - mx * sx
        sxy = mxy - mx * m1y - my * sx
        syy = myy - my * m1y - my * sy
        gbuf[j, 0:1, :] = ca * sx + cb * sy
        gbuf[j, 1:2, :] = cb * sx + cc * sy
        gbuf[j, 2:3, :] = -0.5 * sxx
        gbuf[j, 3:4, :] = -sxy
        gbuf[j, 4:5, :] = -0.5 * syy
        gbuf[j, 5:6, :] = m0 / op
        gbuf[j, 6:9, :] = shades[0:3, j * lanes : (j + 1) * lanes]
        gbuf[j, 9:16, :] = jnp.zeros((7, lanes), jnp.float32)
    for d in range(peers):
        grad_refs[d][...] = gbuf[meta_ref[d]]
        grad_refs[d][NPROJ : NPROJ + 1, :] = jnp.full((1, lanes), 1, jnp.float32) * meta_ref[peers + d].astype(jnp.float32)


def owner_kernel(moving_ref, *refs):
    sources = refs[:-2]
    dense_ref, leave_ref = refs[-2:]
    _, blocks, lanes = dense_ref.shape
    moves = leave_ref.shape[1]
    slot = lax.broadcasted_iota(jnp.int32, (blocks, lanes), 0)
    slots = slot.astype(jnp.float32)
    pick = jnp.zeros((blocks, lanes), jnp.int32)
    for m in range(moves):
        pick = jnp.where(slot == m, moving_ref[0, m], pick)
    masks = [slots == jnp.broadcast_to(ref[NPROJ : NPROJ + 1, :], (blocks, lanes)) for ref in sources]
    for r in range(NPROJ):
        total = jnp.zeros((blocks, lanes), jnp.float32)
        for mask, ref in zip(masks, sources):
            total = total + jnp.where(mask, jnp.broadcast_to(ref[r : r + 1, :], (blocks, lanes)), 0.0)
        dense_ref[r] = total
        leave_ref[r] = jnp.take_along_axis(total, pick, axis=0)[:moves]


def update_kernel(moving_ref, basis_ref, p_ref, f_ref, s_ref, came_ref, dense_ref, carried_ref, np_ref, nf_ref, ns_ref, ubuf, kbuf):
    rows, blocks, lanes = p_ref.shape
    moves = came_ref.shape[1]
    slot = lax.broadcasted_iota(jnp.int32, (blocks, lanes), 0)
    pick = jnp.zeros((blocks, lanes), jnp.int32)
    taken = jnp.zeros((blocks, lanes), jnp.bool_)
    for m in range(moves):
        here = slot == moving_ref[0, m]
        pick = jnp.where(here, m, pick)
        taken = jnp.logical_or(taken, here)

    def mixed(own, arrived, k):
        kbuf[k, 0:moves, :] = arrived
        return jnp.where(taken, jnp.take_along_axis(kbuf[k], pick, axis=0), own)

    for i in range(rows):
        ubuf[i] = mixed(p_ref[i], came_ref[i], i % 8)
    grads = [mixed(dense_ref[r], carried_ref[r], r % 8) for r in range(NPROJ)]
    p = lambda i: ubuf[i]

    def store(i, grad):
        first = mixed(f_ref[i], came_ref[rows + i], i % 8)
        second = mixed(s_ref[i], came_ref[2 * rows + i], (i + 4) % 8)
        one = beta_one * first + (1.0 - beta_one) * grad
        two = beta_two * second + (1.0 - beta_two) * grad * grad
        nf_ref[i] = one
        ns_ref[i] = two
        scaled = (rate_of(i) / (1.0 - beta_one**adam_step)) * one
        np_ref[i] = p(i) - scaled / (jnp.sqrt(two * (1.0 / (1.0 - beta_two**adam_step))) + adam_eps)

    v = geometry(p)
    gmx, gmy, ga, gb, gc, gop = grads[:6]
    store(0, gmx * (0.375 * TILE_SIDE) * (1.0 - v["tx"] * v["tx"]))
    store(1, gmy * (0.375 * TILE_SIDE) * (1.0 - v["ty"] * v["ty"]))
    gdet = -(ga * v["A"] + gb * v["B"] + gc * v["C"]) * v["idet"]
    gxx = gc * v["idet"] + gdet * v["yy"]
    gyy = ga * v["idet"] + gdet * v["xx"]
    gxy = -gb * v["idet"] - 2.0 * gdet * v["xy"]
    gz = gxx * v["sxx"] + gyy * v["syy"] + gxy * v["sxy"]
    f = v["f"]
    store(2, gz * (-2.0 / 3.0) * f * f * f * sigmoid(p(2)))
    U, L, e = v["U"], v["L"], v["e"]
    gU, gL = [], []
    for k in range(3):
        ge = v["z"] * (gxx * U[k] * U[k] + gyy * L[k] * L[k] + gxy * U[k] * L[k])
        t = v["ts"][k]
        store(3 + k, 2.0 * ge * e[k] * (1.0 - t * t))
        ze = v["z"] * e[k]
        gU.append(ze * (2.0 * gxx * U[k] + gxy * L[k]))
        gL.append(ze * (2.0 * gyy * L[k] + gxy * U[k]))
    w, x, y, z = v["q"]
    gq = [
        2.0 * (z * (gL[0] - gU[1]) + y * gU[2] - x * gL[2]),
        2.0 * (y * (gU[1] + gL[0]) + z * gU[2] - 2.0 * x * gL[1] - w * gL[2]),
        2.0 * (x * (gU[1] + gL[0]) - 2.0 * y * gU[0] + w * gU[2] + z * gL[2]),
        2.0 * (w * (gL[0] - gU[1]) - 2.0 * z * (gU[0] + gL[1]) + x * gU[2] + y * gL[2]),
    ]
    share = jnp.where(v["norm"] > 1.0, 1.0, jnp.where(v["norm"] == 1.0, 0.5, 0.0))
    along = share * (w * gq[0] + x * gq[1] + y * gq[2] + z * gq[3])
    for k, unit in enumerate((w, x, y, z)):
        store(6 + k, (gq[k] - unit * along) * v["inv"])
    store(10, gop * 0.99 * v["so"] * (1.0 - v["so"]))
    for c in range(3):
        shade = colour(p, c, lambda k: basis_ref[k])
        logit = grads[6 + c] * shade * (1.0 - shade)
        for k in range(SH):
            store(11 + SH * c + k, logit * basis_ref[k])


def on_device(params, first_moment, second_moment, view_basis, target, tile_blocks, moving):
    blocks, rows, lanes = params.shape
    peers = lax.axis_size("tile")
    listed = tile_blocks.shape[1]
    moves = moving.shape[1]
    pixels = target.shape[2]
    chunks = pixels // lanes
    width = listed * lanes
    f32 = jnp.float32
    smem = pl.BlockSpec(memory_space=pltpu.SMEM)
    vmem = pl.BlockSpec(memory_space=pltpu.VMEM)
    sds = jax.ShapeDtypeStruct

    me = lax.axis_index("tile")
    partner = jnp.bitwise_xor(me, jnp.arange(peers, dtype=jnp.int32))
    matches = (tile_blocks[0][None, :] // blocks) == partner[:, None]
    pos = jnp.sum(jnp.where(matches, jnp.arange(listed, dtype=jnp.int32)[None, :], 0), axis=1)
    loc = jnp.sum(jnp.where(matches, (tile_blocks[0] % blocks)[None, :], 0), axis=1)
    meta = jnp.concatenate([pos, loc]).astype(jnp.int32)

    turned = [jnp.transpose(a, (1, 0, 2)) for a in (params, first_moment, second_moment)]
    projected, leaving = pl.pallas_call(
        project_kernel,
        out_shape=(sds((NPROJ, blocks, lanes), f32), sds((3 * rows, moves, lanes), f32)),
        in_specs=[smem, smem, vmem, vmem, vmem],
        out_specs=(vmem, vmem),
        name="project",
    )(moving, view_basis, *turned)

    def swapped(value, d):
        return lax.ppermute(value, "tile", [(i, i ^ d) for i in range(peers)])

    regions = lax.axis_size("region")
    onward = lambda value: lax.ppermute(value, "region", [(i, (i + 1) % regions) for i in range(regions)])

    sources = [projected] + [swapped(projected, d) for d in range(1, peers)]
    came = onward(leaving)
    image, *splat_grads = pl.pallas_call(
        composite_kernel,
        out_shape=(sds((3, chunks, lanes), f32),) + (sds((GRADS, lanes), f32),) * peers,
        in_specs=[smem] + [vmem] * (peers + 1),
        out_specs=(vmem,) * (peers + 1),
        scratch_shapes=[
            pltpu.VMEM((listed, GRADS, lanes), f32),
            pltpu.VMEM((chunks * width, lanes), f32),
            pltpu.VMEM((chunks * width, lanes), f32),
            pltpu.VMEM((chunks * width, lanes), f32),
            pltpu.VMEM((3, width, lanes), f32),
            pltpu.VMEM((8 * chunks, lanes), f32),
            pltpu.VMEM((listed, GRADS, lanes), f32),
        ],
        compiler_params=pltpu.CompilerParams(vmem_limit_bytes=(3 * chunks + 3) * width * lanes * 4 + (8 << 20)),
        name="composite",
    )(meta, *sources, target.reshape(3, chunks, lanes))
    arrived = [splat_grads[0]] + [swapped(splat_grads[d], d) for d in range(1, peers)]
    dense, outgoing = pl.pallas_call(
        owner_kernel,
        out_shape=(sds((NPROJ, blocks, lanes), f32), sds((NPROJ, moves, lanes), f32)),
        in_specs=[smem] + [vmem] * peers,
        out_specs=(vmem, vmem),
        name="owner",
    )(moving, *arrived)
    carried = onward(outgoing)
    updated = pl.pallas_call(
        update_kernel,
        out_shape=(sds((rows, blocks, lanes), f32),) * 3,
        in_specs=[smem, smem] + [vmem] * 6,
        out_specs=(vmem,) * 3,
        scratch_shapes=[pltpu.VMEM((rows, blocks, lanes), f32), pltpu.VMEM((8, blocks, lanes), f32)],
        name="update",
    )(moving, view_basis, *turned, came, dense, carried)
    updated = [jnp.transpose(a, (1, 0, 2)) for a in updated]
    return (*updated, image.reshape(1, 3, pixels))


def solution(mesh):
    three = P(("region", "tile"), None, None)
    two = P(("region", "tile"), None)
    return jax.shard_map(
        on_device,
        mesh=mesh,
        in_specs=(three, three, three, P(), three, two, two),
        out_specs=(three, three, three, three),
        check_vma=False,
    )
```

time: 99.8 us -> 45.3 us (0.45)
  matrix products: 25.5 us -> 0 us
  Pallas kernels: 0 us -> 19.8 us
  blocking collectives: 15.2 us -> 0 us
  between operations: 14.4 us -> 0.68 us
  waiting for transfers between devices: 23.2 us -> 11.6 us
  local copies, waits for them, and re-layouts: 12.6 us -> 2.71 us
  starting transfers between devices: 1.75 us -> 10.1 us
  other arithmetic: 6.27 us -> 0.27 us
    dot_general x26 -> x0, matrix products: 25.5 us -> none  [the longest x4 7.1 us: backward(): jnp.dot(weight * shading, inclusive_mask, precision=highest)]
    pallas_call x0 -> x4, Pallas kernels: none -> 19.8 us  [the longest x1 13.9 us: on_device(): pl.pallas_call(composite_kernel, out_shape=(sds((3, chunks, lanes), f32),...]
    reduce_scatter x1 -> x0, waiting for transfers between devices: 19.5 us -> none  [on_device(): lax.psum_scatter(dense_grads, 'tile', scatter_dimension=0, tiled=True)]
    all_gather x1 -> x0, blocking collectives: 15.2 us -> none  [on_device(): region_blocks = lax.all_gather(projected, 'tile', axis=0, tiled=True)]
    ppermute x3 -> x8, starting transfers between devices: 1.71 us -> 10.1 us  [the longest x6 10.1 us: swapped(): return lax.ppermute(value, 'tile', [(i, i ^ d) for i in range(peers)])]
    ppermute x3 -> x8, waiting for transfers between devices: 3.62 us -> 11.6 us  [the longest x6 7.26 us: swapped(): return lax.ppermute(value, 'tile', [(i, i ^ d) for i in range(peers)])]
    reduce_sum x7 -> x1, other arithmetic: 3.08 us -> 0.18 us  [on_device(): jnp.sum(jnp.where(matches, jnp.arange(listed, dtype=jnp.int32)[None, :],...]
    gather x4 -> x0, local copies, waits for them, and re-layouts: 2.22 us -> none  [the longest x1 0.56 us: on_device(): jnp.take(stepped, leaving_ids, axis=0)]
  transfers between devices with their start and end apart: 4 -> 8, of which waited for: 2 -> 5; matrix products, arithmetic and copies ran while one was open for 4% -> 1% of each run, Pallas kernels for 0% -> 34%
where the time goes in v1:
time: 45.3 us; the launch traced here: 45 us
  Pallas kernels  19.8 us (44%)
  waiting for transfers between devices  11.6 us (26%)
  starting transfers between devices  10.1 us (22%)
  local copies, waits for them, and re-layouts  2.71 us (6%)
  between operations  0.68 us (2%)
    pallas_call x1, Pallas kernels, on_device(): pl.pallas_call(composite_kernel, out_shape=(sds((3, chunks, lanes), f32),...  13.9 us
    ppermute x6, starting transfers between devices, swapped(): return lax.ppermute(value, 'tile', [(i, i ^ d) for i in range(peers)])  10.1 us
    ppermute x6, waiting for transfers between devices, swapped(): return lax.ppermute(value, 'tile', [(i, i ^ d) for i in range(peers)])  7.26 us
    ppermute x2, waiting for transfers between devices, on_device(): lax.ppermute(value, 'region', [(i, (i + 1) % regions) for i in range(regi...  4.3 us
    unnamed x18, local copies, waits for them, and re-layouts  2.71 us
    pallas_call x1, Pallas kernels, on_device(): pl.pallas_call(update_kernel, out_shape=(sds((rows, blocks, lanes), f32),...  2.4 us
    pallas_call x1, Pallas kernels, on_device(): pl.pallas_call(project_kernel, out_shape=(sds((NPROJ, blocks, lanes), f32...  2.01 us
    pallas_call x1, Pallas kernels, on_device(): pl.pallas_call(owner_kernel, out_shape=(sds((NPROJ, blocks, lanes), f32),...  1.44 us
  transfers between devices with their start and end apart: 8, of which 5 were waited for; matrix products, arithmetic and copies ran while one was open for 1% of the time, Pallas kernels for 34%

profile of v1, /device:TPU:0, one launch (start us, length us, event | category | flops | bytes accessed | tf_op | source)
XLA Modules:
  0.0 45.0 jit_solution(14607583394443493096)
XLA Ops:
  0.6 2.0 %project.1 = (f32[9,8,128]{2,1,0:T(8,128)}, f32[177,4,128]{2,1,0:T(4,128)}) custom-call(s32[1,4]{1,0:T(1,128)} %moving_ref.5, f32[16]{0:T(128)} %basis_ref.3, f32[59,8,128]{2,1,0:T(8,128)} %bitcast.13, f32[59,8,128]{2,1,0:T(8,128)} %bitcast.15, f32[59,8,128]{2,1,0:T(8,128)} %bitcast.17), custom_call_target="tpu_custom_call" | custom-call | tf_op jit(solution)/shard_map/project/pallas_call | solution.py:342
  2.6 5.0 %collective-permute-start.3 = (f32[9,8,128]{2,1,0:T(8,128)}, f32[9,8,128]{2,1,0:T(8,128)S(1)}, u32[]{:S(2)}, u32[]{:S(2)}) collective-permute-start(f32[9,8,128]{2,1,0:T(8,128)} %get-tuple-element.17.refs_0_), channel_id=1, source_target_pairs={{0,3},{1,2},{2,1},{3,0},{4,7},{5,6},{6,5},{7,4},{8,11},{9,10},{10,... | collective-permute-start | bytes 110600 | tf_op jit(solution)/shard_map/ppermute | solution.py:351
  7.7 0.0 collective-permute-start.2
  7.7 0.6 %collective-permute-start.1 = (f32[9,8,128]{2,1,0:T(8,128)}, f32[9,8,128]{2,1,0:T(8,128)S(1)}, u32[]{:S(2)}, u32[]{:S(2)}) collective-permute-start(f32[9,8,128]{2,1,0:T(8,128)} %get-tuple-element.17.refs_0_), channel_id=1, source_target_pairs={{0,1},{1,0},{2,3},{3,2},{4,5},{5,4},{6,7},{7,6},{8,9},{9,8},{10,11... | collective-permute-start | bytes 110600 | tf_op jit(solution)/shard_map/ppermute | solution.py:351
  8.3 0.0 collective-permute-start
  8.3 0.2 fusion
  8.5 0.1 pad_add_fusion.meta_ref
  8.6 1.2 %collective-permute-done.3.refs_3_ = f32[9,8,128]{2,1,0:T(8,128)S(1)} collective-permute-done((f32[9,8,128]{2,1,0:T(8,128)}, f32[9,8,128]{2,1,0:T(8,128)S(1)}, u32[]{:S(2)}, u32[]{:S(2)}) %collective-permute-start.3) | collective-permute-done | bytes 36896 | tf_op jit(solution)/shard_map/ppermute | solution.py:351
  9.8 2.9 %collective-permute-done.2.refs_2_ = f32[9,8,128]{2,1,0:T(8,128)S(1)} collective-permute-done((f32[9,8,128]{2,1,0:T(8,128)}, f32[9,8,128]{2,1,0:T(8,128)S(1)}, u32[]{:S(2)}, u32[]{:S(2)}) %collective-permute-start.2) | collective-permute-done | bytes 36896 | tf_op jit(solution)/shard_map/ppermute | solution.py:351
  12.8 0.0 collective-permute-done.1.refs_1_
  12.8 0.8 %copy-done = f32[9,8,128]{2,1,0:T(8,128)S(1)} copy-done((f32[9,8,128]{2,1,0:T(8,128)S(1)}, f32[9,8,128]{2,1,0:T(8,128)}, u32[]{:S(2)}) %copy-start) | copy-done | bytes 36888
  13.5 13.9 %composite.1 = (f32[3,8,128]{2,1,0:T(8,128)}, f32[16,128]{1,0:T(8,128)S(1)}, f32[16,128]{1,0:T(8,128)S(1)}, f32[16,128]{1,0:T(8,128)S(1)}, f32[16,128]{1,0:T(8,128)S(1)}) custom-call(s32[8]{0:T(128)S(1)} %pad_add_fusion.meta_ref, f32[9,8,128]{2,1,0:T(8,128)S(1)} %copy-done, f32[9,8,128]{2,1,0:T(8,128)S(1)} %collective-permute-done.1.refs_1_, ...), custom_call_target="tpu_custom_call" | custom-call | tf_op jit(solution)/shard_map/composite/pallas_call | solution.py:358
  27.4 0.0 copy-start.2
  27.5 0.6 %copy-done.2 = f32[16,128]{1,0:T(8,128)} copy-done((f32[16,128]{1,0:T(8,128)}, f32[16,128]{1,0:T(8,128)S(1)}, u32[]{:S(2)}) %copy-start.2) | copy-done | bytes 8216
  28.1 2.1 %collective-permute-start.5 = (f32[16,128]{1,0:T(8,128)S(1)}, f32[16,128]{1,0:T(8,128)S(1)}, u32[]{:S(2)}, u32[]{:S(2)}) collective-permute-start(f32[16,128]{1,0:T(8,128)S(1)} %get-tuple-element.20), channel_id=1, source_target_pairs={{0,2},{1,3},{2,0},{3,1},{4,6},{5,7},{6,4},{7,5},{8,10},{9,11},{10,... | collective-permute-start | bytes 24584 | tf_op jit(solution)/shard_map/ppermute | solution.py:351
  30.1 2.3 %collective-permute-start.6 = (f32[16,128]{1,0:T(8,128)S(1)}, f32[16,128]{1,0:T(8,128)S(1)}, u32[]{:S(2)}, u32[]{:S(2)}) collective-permute-start(f32[16,128]{1,0:T(8,128)S(1)} %get-tuple-element.21), channel_id=1, source_target_pairs={{0,3},{1,2},{2,1},{3,0},{4,7},{5,6},{6,5},{7,4},{8,11},{9,10},{10,... | collective-permute-start | bytes 24584 | tf_op jit(solution)/shard_map/ppermute | solution.py:351
  32.4 0.2 collective-permute-done.5.refs_2_
  32.6 3.0 %collective-permute-done.6.refs_3_ = f32[16,128]{1,0:T(8,128)S(1)} collective-permute-done((f32[16,128]{1,0:T(8,128)S(1)}, f32[16,128]{1,0:T(8,128)S(1)}, u32[]{:S(2)}, u32[]{:S(2)}) %collective-permute-start.6) | collective-permute-done | bytes 8224 | tf_op jit(solution)/shard_map/ppermute | solution.py:351
  35.6 0.6 %copy-done.7 = f32[16,128]{1,0:T(8,128)} copy-done((f32[16,128]{1,0:T(8,128)}, f32[16,128]{1,0:T(8,128)S(1)}, u32[]{:S(2)}) %copy-start.7) | copy-done | bytes 8216
  36.2 1.4 %owner.1 = (f32[9,8,128]{2,1,0:T(8,128)}, f32[9,4,128]{2,1,0:T(4,128)}) custom-call(s32[1,4]{1,0:T(1,128)} %moving_ref.5, f32[16,128]{1,0:T(8,128)} %copy-done.2, f32[16,128]{1,0:T(8,128)} %copy-done.5, f32[16,128]{1,0:T(8,128)} %copy-done.6, f32[16,128]{1,0:T(8,128)} %copy-done.7), custom_call_target="tpu_custom_call" | custom-call | tf_op jit(solution)/shard_map/owner/pallas_call | solution.py:376
  37.6 4.3 %collective-permute-done.7.carried_ref = f32[9,4,128]{2,1,0:T(4,128)S(1)} collective-permute-done((f32[9,4,128]{2,1,0:T(4,128)}, f32[9,4,128]{2,1,0:T(4,128)S(1)}, u32[]{:S(2)}, u32[]{:S(2)}) %collective-permute-start.7) | collective-permute-done | bytes 18464 | tf_op jit(solution)/shard_map/ppermute | solution.py:354
  41.9 0.6 %copy-done.4 = f32[9,4,128]{2,1,0:T(4,128)} copy-done((f32[9,4,128]{2,1,0:T(4,128)}, f32[9,4,128]{2,1,0:T(4,128)S(1)}, u32[]{:S(2)}) %copy-start.4) | copy-done | bytes 18456
  42.5 0.1 copy-done.3
  42.6 2.4 %update.1 = (f32[59,8,128]{2,1,0:T(8,128)}, f32[59,8,128]{2,1,0:T(8,128)}, f32[59,8,128]{2,1,0:T(8,128)}) custom-call(s32[1,4]{1,0:T(1,128)} %moving_ref.5, f32[16]{0:T(128)} %basis_ref.3, f32[59,8,128]{2,1,0:T(8,128)} %bitcast.14, f32[59,8,128]{2,1,0:T(8,128)} %bitcast.16, f32[59,8,128]{2,1,0:T(8,128)} %bitcast.18, f32[177,4,128]{2,1,0:T(4,128)} %copy-done.3, ...), custom_call_target="tpu_custom_call" | custom-call | tf_op jit(solution)/shard_map/update/pallas_call | solution.py:384
  (18 shorter events, 0.0 us)
Async XLA Ops:
  2.6 5.7 %copy-start.8 = (s32[1,4]{1,0:T(1,128)S(1)}, s32[1,4]{1,0:T(1,128)}, u32[]{:S(2)}) copy-start(s32[1,4]{1,0:T(1,128)} %param.12) | copy-start | bytes 52
  2.6 7.2 %collective-permute-start.3 = (f32[9,8,128]{2,1,0:T(8,128)}, f32[9,8,128]{2,1,0:T(8,128)S(1)}, u32[]{:S(2)}, u32[]{:S(2)}) collective-permute-start(f32[9,8,128]{2,1,0:T(8,128)} %get-tuple-element.17.refs_0_), channel_id=1, source_target_pairs={{0,3},{1,2},{2,1},{3,0},{4,7},{5,6},{6,5},{7,4},{8,11},{9,10},{10,... | collective-permute-start | bytes 110600 | tf_op jit(solution)/shard_map/ppermute | solution.py:351
  7.7 5.1 %collective-permute-start.2 = (f32[9,8,128]{2,1,0:T(8,128)}, f32[9,8,128]{2,1,0:T(8,128)S(1)}, u32[]{:S(2)}, u32[]{:S(2)}) collective-permute-start(f32[9,8,128]{2,1,0:T(8,128)} %get-tuple-element.17.refs_0_), channel_id=1, source_target_pairs={{0,2},{1,3},{2,0},{3,1},{4,6},{5,7},{6,4},{7,5},{8,10},{9,11},{10,... | collective-permute-start | bytes 110600 | tf_op jit(solution)/shard_map/ppermute | solution.py:351
  7.7 5.1 %collective-permute-start.1 = (f32[9,8,128]{2,1,0:T(8,128)}, f32[9,8,128]{2,1,0:T(8,128)S(1)}, u32[]{:S(2)}, u32[]{:S(2)}) collective-permute-start(f32[9,8,128]{2,1,0:T(8,128)} %get-tuple-element.17.refs_0_), channel_id=1, source_target_pairs={{0,1},{1,0},{2,3},{3,2},{4,5},{5,4},{6,7},{7,6},{8,9},{9,8},{10,11... | collective-permute-start | bytes 110600 | tf_op jit(solution)/shard_map/ppermute | solution.py:351
  8.3 4.4 %copy-start.1 = (f32[1,3,1024]{2,0,1:T(1,128)S(1)}, f32[1,3,1024]{2,0,1:T(1,128)}, u32[]{:S(2)}) copy-start(f32[1,3,1024]{2,0,1:T(1,128)} %param.11) | copy-start | bytes 36868
  8.3 33.6 %collective-permute-start = (f32[177,4,128]{2,1,0:T(4,128)}, f32[177,4,128]{2,1,0:T(4,128)S(1)}, u32[]{:S(2)}, u32[]{:S(2)}) collective-permute-start(f32[177,4,128]{2,1,0:T(4,128)} %get-tuple-element.16), channel_id=1, source_target_pairs={{0,4},{4,8},{8,12},{12,16},{16,20},{20,24},{24,28},{28,0},{1,5},{5... | collective-permute-start | bytes 1087496 | tf_op jit(solution)/shard_map/ppermute | solution.py:354
  12.8 0.8 %copy-start = (f32[9,8,128]{2,1,0:T(8,128)S(1)}, f32[9,8,128]{2,1,0:T(8,128)}, u32[]{:S(2)}) copy-start(f32[9,8,128]{2,1,0:T(8,128)} %get-tuple-element.17.refs_0_) | copy-start | bytes 110596
  27.4 0.6 %copy-start.2 = (f32[16,128]{1,0:T(8,128)}, f32[16,128]{1,0:T(8,128)S(1)}, u32[]{:S(2)}) copy-start(f32[16,128]{1,0:T(8,128)S(1)} %get-tuple-element.18.refs_0_) | copy-start | bytes 24580
  28.1 4.4 %collective-permute-start.4 = (f32[16,128]{1,0:T(8,128)S(1)}, f32[16,128]{1,0:T(8,128)S(1)}, u32[]{:S(2)}, u32[]{:S(2)}) collective-permute-start(f32[16,128]{1,0:T(8,128)S(1)} %get-tuple-element.19), channel_id=1, source_target_pairs={{0,1},{1,0},{2,3},{3,2},{4,5},{5,4},{6,7},{7,6},{8,9},{9,8},{10,11... | collective-permute-start | bytes 24584 | tf_op jit(solution)/shard_map/ppermute | solution.py:351
  28.1 4.5 %collective-permute-start.5 = (f32[16,128]{1,0:T(8,128)S(1)}, f32[16,128]{1,0:T(8,128)S(1)}, u32[]{:S(2)}, u32[]{:S(2)}) collective-permute-start(f32[16,128]{1,0:T(8,128)S(1)} %get-tuple-element.20), channel_id=1, source_target_pairs={{0,2},{1,3},{2,0},{3,1},{4,6},{5,7},{6,4},{7,5},{8,10},{9,11},{10,... | collective-permute-start | bytes 24584 | tf_op jit(solution)/shard_map/ppermute | solution.py:351
  30.1 5.4 %collective-permute-start.6 = (f32[16,128]{1,0:T(8,128)S(1)}, f32[16,128]{1,0:T(8,128)S(1)}, u32[]{:S(2)}, u32[]{:S(2)}) collective-permute-start(f32[16,128]{1,0:T(8,128)S(1)} %get-tuple-element.21), channel_id=1, source_target_pairs={{0,3},{1,2},{2,1},{3,0},{4,7},{5,6},{6,5},{7,4},{8,11},{9,10},{10,... | collective-permute-start | bytes 24584 | tf_op jit(solution)/shard_map/ppermute | solution.py:351
  32.4 3.1 %copy-start.5 = (f32[16,128]{1,0:T(8,128)}, f32[16,128]{1,0:T(8,128)S(1)}, u32[]{:S(2)}) copy-start(f32[16,128]{1,0:T(8,128)S(1)} %collective-permute-done.4.refs_1_) | copy-start | bytes 24580
  32.6 3.0 %copy-start.6 = (f32[16,128]{1,0:T(8,128)}, f32[16,128]{1,0:T(8,128)S(1)}, u32[]{:S(2)}) copy-start(f32[16,128]{1,0:T(8,128)S(1)} %collective-permute-done.5.refs_2_) | copy-start | bytes 24580
  35.6 0.6 %copy-start.7 = (f32[16,128]{1,0:T(8,128)}, f32[16,128]{1,0:T(8,128)S(1)}, u32[]{:S(2)}) copy-start(f32[16,128]{1,0:T(8,128)S(1)} %collective-permute-done.6.refs_3_) | copy-start | bytes 24580
  37.6 4.3 %collective-permute-start.7 = (f32[9,4,128]{2,1,0:T(4,128)}, f32[9,4,128]{2,1,0:T(4,128)S(1)}, u32[]{:S(2)}, u32[]{:S(2)}) collective-permute-start(f32[9,4,128]{2,1,0:T(4,128)} %get-tuple-element.23), channel_id=1, source_target_pairs={{0,4},{4,8},{8,12},{12,16},{16,20},{20,24},{24,28},{28,0},{1,5},{5... | collective-permute-start | bytes 55304 | tf_op jit(solution)/shard_map/ppermute | solution.py:354
  41.9 0.6 %copy-start.4 = (f32[9,4,128]{2,1,0:T(4,128)}, f32[9,4,128]{2,1,0:T(4,128)S(1)}, u32[]{:S(2)}) copy-start(f32[9,4,128]{2,1,0:T(4,128)S(1)} %collective-permute-done.7.carried_ref) | copy-start | bytes 55300
  41.9 0.7 %copy-start.3 = (f32[177,4,128]{2,1,0:T(4,128)}, f32[177,4,128]{2,1,0:T(4,128)S(1)}, u32[]{:S(2)}) copy-start(f32[177,4,128]{2,1,0:T(4,128)S(1)} %collective-permute-done.came_ref) | copy-start | bytes 1087492

commit v2 on v1

--- a/solution.py
+++ b/solution.py
@@ -107,7 +107,7 @@
     target_ref = refs[peers]
     image_ref = refs[peers + 1]
     grad_refs = refs[peers + 2 : 2 * peers + 2]
-    pbuf, abuf, wbuf, ebuf, colq, errbuf, gbuf = refs[2 * peers + 2 :]
+    pbuf, abuf, wbuf, ebuf, colq, errbuf, gbuf, rbuf = refs[2 * peers + 2 :]
     lanes = pbuf.shape[2]
     width = colq.shape[1]
     chunks = abuf.shape[0] // width
@@ -150,28 +150,27 @@
             for c in range(chunks):
                 dy = dy0 + step * c
                 power = (conic * dy + bx) * dy + ax
-                abuf[pl.ds(c * width + row, 8), :] = opacity * jnp.exp2(power)
+                abuf[pl.ds(row * chunks + c * 8, 8), :] = opacity * jnp.exp2(power)
         return 0
 
     lax.fori_loop(0, width // lanes, alphas, 0)
-
-    unroll = 8
 
     def forward(i, running):
         trans, image = running
-        for u in range(unroll):
-            g = i * unroll + u
-            alpha = abuf[pl.ds(g, chunks, stride=width), :]
+        base = pl.multiple_of(i * (8 * chunks), 8 * chunks)
+        for u in range(8):
+            g = i * 8 + u
+            alpha = abuf[pl.ds(base + u, chunks, stride=8), :]
             weight = trans * alpha
             trans = trans * (1.0 - alpha)
-            wbuf[pl.ds(g, chunks, stride=width), :] = weight
+            wbuf[pl.ds(base + u * chunks, chunks), :] = weight
             image = tuple(
                 image[k] + weight * jnp.broadcast_to(colq[k, pl.ds(g, 1), :], (chunks, lanes)) for k in range(3)
             )
         return (trans, image)
 
     zero = jnp.zeros((chunks, lanes), jnp.float32)
-    _, image = lax.fori_loop(0, width // unroll, forward, (zero + 1.0, (zero, zero, zero)))
+    _, image = lax.fori_loop(0, width // 8, forward, (zero + 1.0, (zero, zero, zero)))
     errors = []
     errbuf[...] = jnp.zeros_like(errbuf)
     for k in range(3):
@@ -180,37 +179,78 @@
         errbuf[k * chunks : (k + 1) * chunks, :] = errors[k]
 
     def backward(i, behind):
-        for u in range(unroll):
-            g = width - 1 - (i * unroll + u)
+        group = width // 8 - 1 - i
+        base = pl.multiple_of(group * (8 * chunks), 8 * chunks)
+        for u in reversed(range(8)):
+            g = group * 8 + u
             shade = [errors[k] * jnp.broadcast_to(colq[k, pl.ds(g, 1), :], (chunks, lanes)) for k in range(3)]
-            alpha = abuf[pl.ds(g, chunks, stride=width), :]
-            weight = wbuf[pl.ds(g, chunks, stride=width), :]
+            alpha = abuf[pl.ds(base + u, chunks, stride=8), :]
+            weight = wbuf[pl.ds(base + u * chunks, chunks), :]
             ahead = (shade[0] + shade[1]) + shade[2] - behind
             behind = behind + alpha * ahead
-            ebuf[pl.ds(g, chunks, stride=width), :] = weight * ahead
+            ebuf[pl.ds(base + u * chunks, chunks), :] = weight * ahead
         return behind
 
-    lax.fori_loop(0, width // unroll, backward, zero)
-
-    which = lax.broadcasted_iota(jnp.int32, (8, lanes), 0)
-    dot = functools.partial(
-        lax.dot_general,
-        dimension_numbers=(((1,), (1,)), ((), ())),
-        precision=lax.Precision.HIGHEST,
-        preferred_element_type=jnp.float32,
-    )
-    moments = jnp.zeros((8, width), jnp.float32)
-    shades = jnp.zeros((8, width), jnp.float32)
-    for c in range(chunks):
-        y = py + step * c
-        basis = jnp.where(which == 0, 1.0, 0.0)
-        for r, value in enumerate((px, y, px * px, px * y, y * y)):
-            basis = jnp.where(which == r + 1, value, basis)
-        moments = moments + dot(basis, ebuf[c * width : (c + 1) * width, :])
-        shades = shades + dot(errbuf[pl.ds(c, 8, stride=chunks), :], wbuf[c * width : (c + 1) * width, :])
+    lax.fori_loop(0, width // 8, backward, zero)
+
+    half = chunks // 2
+
+    def reduce_pixels(u, _):
+        row = pl.multiple_of(u * 8, 8)
+        part = [ebuf[pl.ds(row * chunks + c, 8, stride=chunks), :] for c in range(chunks)]
+        even = [part[c] + part[chunks - 1 - c] for c in range(half)]
+        odd = [part[chunks - 1 - c] - part[c] for c in range(half)]
+        centre = (chunks - 1) / 2.0
+        sums = [
+            sum(even[1:], even[0]),
+            sum([(centre - c) * odd[c] for c in range(1, half)], centre * odd[0]),
+            sum([(centre - c) ** 2 * even[c] for c in range(1, half)], centre**2 * even[0]),
+        ]
+        part = [wbuf[pl.ds(row * chunks + c, 8, stride=chunks), :] for c in range(chunks)]
+        for k in range(3):
+            lit = [part[c] * jnp.broadcast_to(errbuf[pl.ds(k * chunks + c, 1), :], (8, lanes)) for c in range(chunks)]
+            sums.append(((lit[0] + lit[1]) + (lit[2] + lit[3])) + ((lit[4] + lit[5]) + (lit[6] + lit[7])))
+        for i, value in enumerate(sums):
+            rbuf[pl.ds(row, 8), i * lanes : (i + 1) * lanes] = value
+        return 0
+
+    lax.fori_loop(0, width // 8, reduce_pixels, 0)
+
+    which = lax.broadcasted_iota(jnp.int32, (GRADS, lanes), 0)
+    lane = lax.broadcasted_iota(jnp.int32, (GRADS, lanes), 1)
+    bx = (lane % TILE_SIDE).astype(jnp.float32) + (0.5 - HALF)
+    by = (lane // TILE_SIDE).astype(jnp.float32) + (0.5 - step / 2.0)
+    one = jnp.ones_like(bx)
+
+    def table(**entries):
+        out = jnp.zeros_like(bx)
+        for name, value in entries.items():
+            out = jnp.where(which == int(name[1:]), value, out)
+        return out
+
+    basis = jnp.concatenate(
+        [
+            table(r0=one, r1=bx, r2=by, r3=(bx * bx - 0.25) * 0.5, r4=bx * by, r5=by * by),
+            table(r2=step * one, r4=step * bx, r5=2.0 * step * by),
+            table(r5=step * step * one),
+            table(r6=one),
+            table(r7=one),
+            table(r8=one),
+        ],
+        axis=1,
+    ).astype(jnp.bfloat16)
+    whole = rbuf[...]
+    totals = jnp.zeros((width, GRADS), jnp.float32)
+    for _ in range(3):
+        piece = whole.astype(jnp.bfloat16)
+        whole = whole - piece.astype(jnp.float32)
+        totals = totals + lax.dot_general(
+            piece, basis, (((1,), (1,)), ((), ())), preferred_element_type=jnp.float32
+        )
     for j in range(width // lanes):
-        part = moments[:, j * lanes : (j + 1) * lanes]
+        part = totals[j * lanes : (j + 1) * lanes].T
         m0, m1x, m1y, mxx, mxy, myy = [part[r : r + 1] for r in range(6)]
+        mxx = 2.0 * mxx + 0.25 * m0
         mx, my, ca, cb, cc, op = [pbuf[j, r : r + 1, :] for r in range(6)]
         sx = m1x - mx * m0
         sy = m1y - my * m0
@@ -223,7 +263,7 @@
         gbuf[j, 3:4, :] = -sxy
         gbuf[j, 4:5, :] = -0.5 * syy
         gbuf[j, 5:6, :] = m0 / op
-        gbuf[j, 6:9, :] = shades[0:3, j * lanes : (j + 1) * lanes]
+        gbuf[j, 6:9, :] = part[6:9]
         gbuf[j, 9:16, :] = jnp.zeros((7, lanes), jnp.float32)
     for d in range(peers):
         grad_refs[d][...] = gbuf[meta_ref[d]]
@@ -344,6 +384,7 @@
         out_shape=(sds((NPROJ, blocks, lanes), f32), sds((3 * rows, moves, lanes), f32)),
         in_specs=[smem, smem, vmem, vmem, vmem],
         out_specs=(vmem, vmem),
+        compiler_params=pltpu.CompilerParams(vmem_limit_bytes=4 << 20),
         name="project",
     )(moving, view_basis, *turned)
 
@@ -368,8 +409,9 @@
             pltpu.VMEM((3, width, lanes), f32),
             pltpu.VMEM((8 * chunks, lanes), f32),
             pltpu.VMEM((listed, GRADS, lanes), f32),
+            pltpu.VMEM((width, 6 * lanes), f32),
         ],
-        compiler_params=pltpu.CompilerParams(vmem_limit_bytes=(3 * chunks + 3) * width * lanes * 4 + (8 << 20)),
+        compiler_params=pltpu.CompilerParams(vmem_limit_bytes=(3 * chunks + 12) * width * lanes * 4 + (8 << 20)),
         name="composite",
     )(meta, *sources, target.reshape(3, chunks, lanes))
     arrived = [splat_grads[0]] + [swapped(splat_grads[d], d) for d in range(1, peers)]
@@ -378,6 +420,7 @@
         out_shape=(sds((NPROJ, blocks, lanes), f32), sds((NPROJ, moves, lanes), f32)),
         in_specs=[smem] + [vmem] * peers,
         out_specs=(vmem, vmem),
+        compiler_params=pltpu.CompilerParams(vmem_limit_bytes=1 << 20),
         name="owner",
     )(moving, *arrived)
     carried = onward(outgoing)
@@ -387,6 +430,7 @@
         in_specs=[smem, smem] + [vmem] * 6,
         out_specs=(vmem,) * 3,
         scratch_shapes=[pltpu.VMEM((rows, blocks, lanes), f32), pltpu.VMEM((8, blocks, lanes), f32)],
+        compiler_params=pltpu.CompilerParams(vmem_limit_bytes=6 << 20),
         name="update",
     )(moving, view_basis, *turned, came, dense, carried)
     updated = [jnp.transpose(a, (1, 0, 2)) for a in updated]

time: 45.3 us -> 36.4 us (0.80)
  Pallas kernels: 19.8 us -> 10.3 us
  local copies, waits for them, and re-layouts: 2.71 us -> 3.5 us
    pallas_call x1, Pallas kernels: 13.9 us -> 7.41 us  [on_device(): pl.pallas_call(composite_kernel, out_shape=(sds((3, chunks, lanes), f32),...]
    pallas_call x1, Pallas kernels: 2.01 us -> 0.63 us  [on_device(): pl.pallas_call(project_kernel, out_shape=(sds((NPROJ, blocks, lanes), f32...]
    pallas_call x1, Pallas kernels: 1.44 us -> 0.56 us  [on_device(): pl.pallas_call(owner_kernel, out_shape=(sds((NPROJ, blocks, lanes), f32),...]
    unnamed x18 -> x20, local copies, waits for them, and re-layouts: 2.71 us -> 3.5 us
    pallas_call x1, Pallas kernels: 2.4 us -> 1.7 us  [on_device(): pl.pallas_call(update_kernel, out_shape=(sds((rows, blocks, lanes), f32),...]
  transfers between devices with their start and end apart: 8 -> 8, of which waited for: 5 -> 5; matrix products, arithmetic and copies ran while one was open for 1% -> 1% of each run, Pallas kernels for 34% -> 22%
where the time goes in v2:
time: 36.4 us; the launch traced here: 36.2 us
  waiting for transfers between devices  11.2 us (31%)
  Pallas kernels  10.3 us (28%)
  starting transfers between devices  10.3 us (28%)
  local copies, waits for them, and re-layouts  3.5 us (10%)
  between operations  0.73 us (2%)
    ppermute x6, starting transfers between devices, swapped(): return lax.ppermute(value, 'tile', [(i, i ^ d) for i in range(peers)])  10.2 us
    pallas_call x1, Pallas kernels, on_device(): pl.pallas_call(composite_kernel, out_shape=(sds((3, chunks, lanes), f32),...  7.41 us
    ppermute x6, waiting for transfers between devices, swapped(): return lax.ppermute(value, 'tile', [(i, i ^ d) for i in range(peers)])  7.08 us
    ppermute x2, waiting for transfers between devices, on_device(): lax.ppermute(value, 'region', [(i, (i + 1) % regions) for i in range(regi...  4.07 us
    unnamed x20, local copies, waits for them, and re-layouts  3.5 us
    pallas_call x1, Pallas kernels, on_device(): pl.pallas_call(update_kernel, out_shape=(sds((rows, blocks, lanes), f32),...  1.7 us
  transfers between devices with their start and end apart: 8, of which 5 were waited for; matrix products, arithmetic and copies ran while one was open for 1% of the time, Pallas kernels for 22%

profile of v2, /device:TPU:0, one launch (start us, length us, event | category | flops | bytes accessed | tf_op | source)
XLA Modules:
  0.0 36.2 jit_solution(11204034110973612104)
XLA Ops:
  0.7 0.6 %copy-done.7 = s32[1,4]{1,0:T(1,128)S(1)} copy-done((s32[1,4]{1,0:T(1,128)S(1)}, s32[1,4]{1,0:T(1,128)}, u32[]{:S(2)}) %copy-start.7) | copy-done | bytes 40
  1.3 0.0 copy-done.8
  1.3 0.9 %copy-done = f32[8,59,128]{2,0,1:T(8,128)S(1)} copy-done((f32[8,59,128]{2,0,1:T(8,128)S(1)}, f32[8,59,128]{2,0,1:T(8,128)}, u32[]{:S(2)}) %copy-start) | copy-done | bytes 241688
  2.2 0.9 %copy-done.2 = f32[8,59,128]{2,0,1:T(8,128)S(1)} copy-done((f32[8,59,128]{2,0,1:T(8,128)S(1)}, f32[8,59,128]{2,0,1:T(8,128)}, u32[]{:S(2)}) %copy-start.2) | copy-done | bytes 241688
  3.2 0.9 %copy-done.4 = f32[8,59,128]{2,0,1:T(8,128)S(1)} copy-done((f32[8,59,128]{2,0,1:T(8,128)S(1)}, f32[8,59,128]{2,0,1:T(8,128)}, u32[]{:S(2)}) %copy-start.4) | copy-done | bytes 241688
  4.1 0.6 %project.1 = (f32[9,8,128]{2,1,0:T(8,128)S(1)}, f32[177,4,128]{2,1,0:T(4,128)S(1)}) custom-call(s32[1,4]{1,0:T(1,128)S(1)} %copy-done.7, f32[16]{0:T(128)S(1)} %copy-done.8, f32[59,8,128]{2,1,0:T(8,128)S(1)} %bitcast.12, f32[59,8,128]{2,1,0:T(8,128)S(1)} %bitcast.14, f32[59,8,128]{2,1,0:T(8,128)S(1)} %bitcast.16), custom_call_target="tpu_custom_call" | custom-call | tf_op jit(solution)/shard_map/project/pallas_call | solution.py:382
  4.8 0.0 copy-start.9
  4.8 5.1 %collective-permute-start.3 = (f32[9,8,128]{2,1,0:T(8,128)S(1)}, f32[9,8,128]{2,1,0:T(8,128)S(1)}, u32[]{:S(2)}, u32[]{:S(2)}) collective-permute-start(f32[9,8,128]{2,1,0:T(8,128)S(1)} %get-tuple-element.17.refs_0_), channel_id=1, source_target_pairs={{0,3},{1,2},{2,1},{3,0},{4,7},{5,6},{6,5},{7,4},{8,11},{9,10},{10,... | collective-permute-start | bytes 110600 | tf_op jit(solution)/shard_map/ppermute | solution.py:392
  9.9 0.0 collective-permute-start.2
  9.9 0.6 %collective-permute-start.1 = (f32[9,8,128]{2,1,0:T(8,128)S(1)}, f32[9,8,128]{2,1,0:T(8,128)S(1)}, u32[]{:S(2)}, u32[]{:S(2)}) collective-permute-start(f32[9,8,128]{2,1,0:T(8,128)S(1)} %get-tuple-element.17.refs_0_), channel_id=1, source_target_pairs={{0,1},{1,0},{2,3},{3,2},{4,5},{5,4},{6,7},{7,6},{8,9},{9,8},{10,11... | collective-permute-start | bytes 110600 | tf_op jit(solution)/shard_map/ppermute | solution.py:392
  10.6 0.2 fusion
  10.8 0.1 pad_add_fusion.meta_ref
  10.8 1.0 %collective-permute-done.3.refs_3_ = f32[9,8,128]{2,1,0:T(8,128)S(1)} collective-permute-done((f32[9,8,128]{2,1,0:T(8,128)S(1)}, f32[9,8,128]{2,1,0:T(8,128)S(1)}, u32[]{:S(2)}, u32[]{:S(2)}) %collective-permute-start.3) | collective-permute-done | bytes 36896 | tf_op jit(solution)/shard_map/ppermute | solution.py:392
  11.8 2.9 %collective-permute-done.2.refs_2_ = f32[9,8,128]{2,1,0:T(8,128)S(1)} collective-permute-done((f32[9,8,128]{2,1,0:T(8,128)S(1)}, f32[9,8,128]{2,1,0:T(8,128)S(1)}, u32[]{:S(2)}, u32[]{:S(2)}) %collective-permute-start.2) | collective-permute-done | bytes 36896 | tf_op jit(solution)/shard_map/ppermute | solution.py:392
  14.8 7.4 %composite.1 = (f32[3,8,128]{2,1,0:T(8,128)}, f32[16,128]{1,0:T(8,128)S(1)}, f32[16,128]{1,0:T(8,128)S(1)}, f32[16,128]{1,0:T(8,128)S(1)}, f32[16,128]{1,0:T(8,128)S(1)}) custom-call(s32[8]{0:T(128)S(1)} %pad_add_fusion.meta_ref, f32[9,8,128]{2,1,0:T(8,128)S(1)} %get-tuple-element.17.refs_0_, f32[9,8,128]{2,1,0:T(8,128)S(1)} %collective-permute-done.1.refs_1_, ...), custom_call_target="tpu_custom_call" | custom-call | tf_op jit(solution)/shard_map/composite/pallas_call | solution.py:399
  22.2 0.1 collective-permute-start.4
  22.3 2.1 %collective-permute-start.5 = (f32[16,128]{1,0:T(8,128)S(1)}, f32[16,128]{1,0:T(8,128)S(1)}, u32[]{:S(2)}, u32[]{:S(2)}) collective-permute-start(f32[16,128]{1,0:T(8,128)S(1)} %get-tuple-element.20), channel_id=1, source_target_pairs={{0,2},{1,3},{2,0},{3,1},{4,6},{5,7},{6,4},{7,5},{8,10},{9,11},{10,... | collective-permute-start | bytes 24584 | tf_op jit(solution)/shard_map/ppermute | solution.py:392
  24.3 2.3 %collective-permute-start.6 = (f32[16,128]{1,0:T(8,128)S(1)}, f32[16,128]{1,0:T(8,128)S(1)}, u32[]{:S(2)}, u32[]{:S(2)}) collective-permute-start(f32[16,128]{1,0:T(8,128)S(1)} %get-tuple-element.21), channel_id=1, source_target_pairs={{0,3},{1,2},{2,1},{3,0},{4,7},{5,6},{6,5},{7,4},{8,11},{9,10},{10,... | collective-permute-start | bytes 24584 | tf_op jit(solution)/shard_map/ppermute | solution.py:392
  26.6 0.2 collective-permute-done.5.refs_2_
  26.9 2.9 %collective-permute-done.6.refs_3_ = f32[16,128]{1,0:T(8,128)S(1)} collective-permute-done((f32[16,128]{1,0:T(8,128)S(1)}, f32[16,128]{1,0:T(8,128)S(1)}, u32[]{:S(2)}, u32[]{:S(2)}) %collective-permute-start.6) | collective-permute-done | bytes 8224 | tf_op jit(solution)/shard_map/ppermute | solution.py:392
  29.8 0.6 %owner.1 = (f32[9,8,128]{2,1,0:T(8,128)S(1)}, f32[9,4,128]{2,1,0:T(4,128)S(1)}) custom-call(s32[1,4]{1,0:T(1,128)S(1)} %copy-done.7, f32[16,128]{1,0:T(8,128)S(1)} %get-tuple-element.18.refs_0_, f32[16,128]{1,0:T(8,128)S(1)} %collective-permute-done.4.refs_1_, f32[16,128]{1,0:T(8,128)S(1)} %collective-permute-done.5.refs_2_, ...), custom_call_target="tpu_custom_call" | custom-call | tf_op jit(solution)/shard_map/owner/pallas_call | solution.py:418
  30.4 0.1 collective-permute-start.7
  30.4 4.1 %collective-permute-done.7.carried_ref = f32[9,4,128]{2,1,0:T(4,128)S(1)} collective-permute-done((f32[9,4,128]{2,1,0:T(4,128)S(1)}, f32[9,4,128]{2,1,0:T(4,128)S(1)}, u32[]{:S(2)}, u32[]{:S(2)}) %collective-permute-start.7) | collective-permute-done | bytes 18464 | tf_op jit(solution)/shard_map/ppermute | solution.py:395
  34.5 1.7 %update.1 = (f32[59,8,128]{2,1,0:T(8,128)}, f32[59,8,128]{2,1,0:T(8,128)}, f32[59,8,128]{2,1,0:T(8,128)}) custom-call(s32[1,4]{1,0:T(1,128)S(1)} %copy-done.7, f32[16]{0:T(128)S(1)} %copy-done.8, f32[59,8,128]{2,1,0:T(8,128)S(1)} %bitcast.13, f32[59,8,128]{2,1,0:T(8,128)S(1)} %bitcast.15, f32[59,8,128]{2,1,0:T(8,128)S(1)} %bitcast.17, ...), custom_call_target="tpu_custom_call" | custom-call | tf_op jit(solution)/shard_map/update/pallas_call | solution.py:427
  (20 shorter events, 0.0 us)
Async XLA Ops:
  0.6 0.7 %copy-start.7 = (s32[1,4]{1,0:T(1,128)S(1)}, s32[1,4]{1,0:T(1,128)}, u32[]{:S(2)}) copy-start(s32[1,4]{1,0:T(1,128)} %moving_ref.5) | copy-start | bytes 52
  0.6 0.7 %copy-start.8 = (f32[16]{0:T(128)S(1)}, f32[16]{0:T(128)}, u32[]{:S(2)}) copy-start(f32[16]{0:T(128)} %basis_ref.3) | copy-start | bytes 196
  1.3 0.9 %copy-start = (f32[8,59,128]{2,0,1:T(8,128)S(1)}, f32[8,59,128]{2,0,1:T(8,128)}, u32[]{:S(2)}) copy-start(f32[8,59,128]{2,0,1:T(8,128)} %param.7) | copy-start | bytes 724996
  2.2 0.9 %copy-start.2 = (f32[8,59,128]{2,0,1:T(8,128)S(1)}, f32[8,59,128]{2,0,1:T(8,128)}, u32[]{:S(2)}) copy-start(f32[8,59,128]{2,0,1:T(8,128)} %param.8) | copy-start | bytes 724996
  3.2 0.9 %copy-start.4 = (f32[8,59,128]{2,0,1:T(8,128)S(1)}, f32[8,59,128]{2,0,1:T(8,128)}, u32[]{:S(2)}) copy-start(f32[8,59,128]{2,0,1:T(8,128)} %param.9) | copy-start | bytes 724996
  4.1 30.4 %copy-start.1 = (f32[8,59,128]{2,0,1:T(8,128)S(1)}, f32[8,59,128]{2,0,1:T(8,128)}, u32[]{:S(2)}) copy-start(f32[8,59,128]{2,0,1:T(8,128)} %param.7) | copy-start | bytes 724996
  4.1 30.4 %copy-start.3 = (f32[8,59,128]{2,0,1:T(8,128)S(1)}, f32[8,59,128]{2,0,1:T(8,128)}, u32[]{:S(2)}) copy-start(f32[8,59,128]{2,0,1:T(8,128)} %param.8) | copy-start | bytes 724996
  4.1 30.4 %copy-start.5 = (f32[8,59,128]{2,0,1:T(8,128)S(1)}, f32[8,59,128]{2,0,1:T(8,128)}, u32[]{:S(2)}) copy-start(f32[8,59,128]{2,0,1:T(8,128)} %param.9) | copy-start | bytes 724996
  4.8 5.8 %copy-start.9 = (s32[1,4]{1,0:T(1,128)S(1)}, s32[1,4]{1,0:T(1,128)}, u32[]{:S(2)}) copy-start(s32[1,4]{1,0:T(1,128)} %param.12) | copy-start | bytes 52
  4.8 7.1 %collective-permute-start.3 = (f32[9,8,128]{2,1,0:T(8,128)S(1)}, f32[9,8,128]{2,1,0:T(8,128)S(1)}, u32[]{:S(2)}, u32[]{:S(2)}) collective-permute-start(f32[9,8,128]{2,1,0:T(8,128)S(1)} %get-tuple-element.17.refs_0_), channel_id=1, source_target_pairs={{0,3},{1,2},{2,1},{3,0},{4,7},{5,6},{6,5},{7,4},{8,11},{9,10},{10,... | collective-permute-start | bytes 110600 | tf_op jit(solution)/shard_map/ppermute | solution.py:392
  9.9 4.9 %collective-permute-start.2 = (f32[9,8,128]{2,1,0:T(8,128)S(1)}, f32[9,8,128]{2,1,0:T(8,128)S(1)}, u32[]{:S(2)}, u32[]{:S(2)}) collective-permute-start(f32[9,8,128]{2,1,0:T(8,128)S(1)} %get-tuple-element.17.refs_0_), channel_id=1, source_target_pairs={{0,2},{1,3},{2,0},{3,1},{4,6},{5,7},{6,4},{7,5},{8,10},{9,11},{10,... | collective-permute-start | bytes 110600 | tf_op jit(solution)/shard_map/ppermute | solution.py:392
  9.9 4.9 %collective-permute-start.1 = (f32[9,8,128]{2,1,0:T(8,128)S(1)}, f32[9,8,128]{2,1,0:T(8,128)S(1)}, u32[]{:S(2)}, u32[]{:S(2)}) collective-permute-start(f32[9,8,128]{2,1,0:T(8,128)S(1)} %get-tuple-element.17.refs_0_), channel_id=1, source_target_pairs={{0,1},{1,0},{2,3},{3,2},{4,5},{5,4},{6,7},{7,6},{8,9},{9,8},{10,11... | collective-permute-start | bytes 110600 | tf_op jit(solution)/shard_map/ppermute | solution.py:392
  10.5 4.2 %copy-start.6 = (f32[1,3,1024]{2,0,1:T(1,128)S(1)}, f32[1,3,1024]{2,0,1:T(1,128)}, u32[]{:S(2)}) copy-start(f32[1,3,1024]{2,0,1:T(1,128)} %param.11) | copy-start | bytes 36868
  10.5 24.0 %collective-permute-start = (f32[177,4,128]{2,1,0:T(4,128)S(1)}, f32[177,4,128]{2,1,0:T(4,128)S(1)}, u32[]{:S(2)}, u32[]{:S(2)}) collective-permute-start(f32[177,4,128]{2,1,0:T(4,128)S(1)} %get-tuple-element.16), channel_id=1, source_target_pairs={{0,4},{4,8},{8,12},{12,16},{16,20},{20,24},{24,28},{28,0},{1,5},{5... | collective-permute-start | bytes 1087496 | tf_op jit(solution)/shard_map/ppermute | solution.py:395
  22.2 4.5 %collective-permute-start.4 = (f32[16,128]{1,0:T(8,128)S(1)}, f32[16,128]{1,0:T(8,128)S(1)}, u32[]{:S(2)}, u32[]{:S(2)}) collective-permute-start(f32[16,128]{1,0:T(8,128)S(1)} %get-tuple-element.19), channel_id=1, source_target_pairs={{0,1},{1,0},{2,3},{3,2},{4,5},{5,4},{6,7},{7,6},{8,9},{9,8},{10,11... | collective-permute-start | bytes 24584 | tf_op jit(solution)/shard_map/ppermute | solution.py:392
  22.3 4.6 %collective-permute-start.5 = (f32[16,128]{1,0:T(8,128)S(1)}, f32[16,128]{1,0:T(8,128)S(1)}, u32[]{:S(2)}, u32[]{:S(2)}) collective-permute-start(f32[16,128]{1,0:T(8,128)S(1)} %get-tuple-element.20), channel_id=1, source_target_pairs={{0,2},{1,3},{2,0},{3,1},{4,6},{5,7},{6,4},{7,5},{8,10},{9,11},{10,... | collective-permute-start | bytes 24584 | tf_op jit(solution)/shard_map/ppermute | solution.py:392
  24.3 5.4 %collective-permute-start.6 = (f32[16,128]{1,0:T(8,128)S(1)}, f32[16,128]{1,0:T(8,128)S(1)}, u32[]{:S(2)}, u32[]{:S(2)}) collective-permute-start(f32[16,128]{1,0:T(8,128)S(1)} %get-tuple-element.21), channel_id=1, source_target_pairs={{0,3},{1,2},{2,1},{3,0},{4,7},{5,6},{6,5},{7,4},{8,11},{9,10},{10,... | collective-permute-start | bytes 24584 | tf_op jit(solution)/shard_map/ppermute | solution.py:392
  30.4 4.1 %collective-permute-start.7 = (f32[9,4,128]{2,1,0:T(4,128)S(1)}, f32[9,4,128]{2,1,0:T(4,128)S(1)}, u32[]{:S(2)}, u32[]{:S(2)}) collective-permute-start(f32[9,4,128]{2,1,0:T(4,128)S(1)} %get-tuple-element.23), channel_id=1, source_target_pairs={{0,4},{4,8},{8,12},{12,16},{16,20},{20,24},{24,28},{28,0},{1,5},{5... | collective-permute-start | bytes 55304 | tf_op jit(solution)/shard_map/ppermute | solution.py:395

commit v3 on v1

v3 whole, which is shorter than its diff:
```python
import functools
import math
import jax
import jax.numpy as jnp
import numpy as np
from jax import lax
from jax.experimental import pallas as pl
from jax.experimental.pallas import tpu as pltpu
from jax.sharding import PartitionSpec as P

SH = 16
TILE_SIDE = 32
NPROJ = 9
GRADS = 16
HALF = TILE_SIDE / 2.0

beta_one = 0.9
beta_two = 0.999
adam_eps = 1e-08
adam_step = 10.0
LOG2E = math.log2(math.e)


def rate_of(row):
    if row < 3:
        return 0.002
    if row < 6:
        return 0.005
    if row < 10:
        return 0.001
    if row < 11:
        return 0.05
    return 0.0025


def sigmoid(x):
    return 1.0 / (1.0 + jnp.exp(-x))


def geometry(p):
    v = {}
    v["tx"] = jnp.tanh(p(0))
    v["ty"] = jnp.tanh(p(1))
    depth = p(2)
    softplus = jnp.maximum(depth, 0.0) + jnp.log(1.0 + jnp.exp(-jnp.abs(depth)))
    v["f"] = 3.0 / (1.0 + softplus)
    v["z"] = v["f"] * v["f"]
    v["ts"] = [jnp.tanh(p(3 + k)) for k in range(3)]
    v["e"] = [2.25 * jnp.exp(2.0 * t) for t in v["ts"]]
    q = [p(6 + k) for k in range(4)]
    norm = jnp.sqrt((q[0] * q[0] + q[1] * q[1]) + (q[2] * q[2] + q[3] * q[3]))
    inv = 1.0 / jnp.maximum(norm, 1.0)
    v["norm"] = norm
    v["inv"] = inv
    w, x, y, z = [a * inv for a in q]
    v["q"] = (w, x, y, z)
    U = [1.0 - 2.0 * (y * y + z * z), 2.0 * (x * y - w * z), 2.0 * (x * z + w * y)]
    L = [2.0 * (x * y + w * z), 1.0 - 2.0 * (x * x + z * z), 2.0 * (y * z - w * x)]
    v["U"], v["L"] = U, L
    e = v["e"]
    v["sxx"] = U[0] * U[0] * e[0] + U[1] * U[1] * e[1] + U[2] * U[2] * e[2]
    v["syy"] = L[0] * L[0] * e[0] + L[1] * L[1] * e[1] + L[2] * L[2] * e[2]
    v["sxy"] = U[0] * L[0] * e[0] + U[1] * L[1] * e[1] + U[2] * L[2] * e[2]
    v["xx"] = v["z"] * v["sxx"] + 0.3
    v["yy"] = v["z"] * v["syy"] + 0.3
    v["xy"] = v["z"] * v["sxy"]
    v["idet"] = 1.0 / (v["xx"] * v["yy"] - v["xy"] * v["xy"])
    v["A"] = v["yy"] * v["idet"]
    v["B"] = -v["xy"] * v["idet"]
    v["C"] = v["xx"] * v["idet"]
    v["so"] = sigmoid(p(10) - 4.0)
    return v


def colour(p, c, basis):
    total = p(11 + SH * c) * basis(0)
    for k in range(1, SH):
        total = total + p(11 + SH * c + k) * basis(k)
    return sigmoid(total)


def project_kernel(basis_hbm, p_hbm, proj_ref, p_ref, basis_ref, sems):
    head = 11
    copies = [
        pltpu.make_async_copy(p_hbm.at[:head], p_ref.at[:head], sems.at[0]),
        pltpu.make_async_copy(p_hbm.at[head:], p_ref.at[head:], sems.at[1]),
        pltpu.make_async_copy(basis_hbm, basis_ref, sems.at[2]),
    ]
    for copy in copies:
        copy.start()
    p = lambda i: p_ref[i]
    copies[0].wait()
    v = geometry(p)
    proj_ref[0] = 0.375 * TILE_SIDE * v["tx"]
    proj_ref[1] = 0.375 * TILE_SIDE * v["ty"]
    proj_ref[2] = v["A"]
    proj_ref[3] = v["B"]
    proj_ref[4] = v["C"]
    proj_ref[5] = 0.99 * v["so"]
    copies[1].wait()
    copies[2].wait()
    for c in range(3):
        proj_ref[6 + c] = colour(p, c, lambda k: basis_ref[k])


def picks(moving_ref, blocks, lanes):
    slot = lax.broadcasted_iota(jnp.int32, (blocks, lanes), 0)
    source = jnp.zeros((blocks, lanes), jnp.int32)
    taken = jnp.zeros((blocks, lanes), jnp.bool_)
    for m in range(moving_ref.shape[1]):
        here = slot == moving_ref[0, m]
        source = jnp.where(here, m, source)
        taken = jnp.logical_or(taken, here)
    return source, taken


def pack_kernel(moving_ref, p_hbm, f_hbm, s_hbm, leave_ref, state_ref, sems):
    total, moves, lanes = leave_ref.shape
    rows, blocks, _ = p_hbm.shape
    copies = [
        pltpu.make_async_copy(ref, state_ref.at[a * rows : (a + 1) * rows], sems.at[a])
        for a, ref in enumerate((p_hbm, f_hbm, s_hbm))
    ]
    for copy in copies:
        copy.start()
    slot = lax.broadcasted_iota(jnp.int32, (blocks, lanes), 0)
    pick = jnp.zeros((blocks, lanes), jnp.int32)
    for m in range(moves):
        pick = jnp.where(slot == m, moving_ref[0, m], pick)
    leave_ref[total - 1] = pick[:moves].astype(jnp.float32)
    for a in range(3):
        copies[a].wait()
        for i in range(a * rows, (a + 1) * rows):
            leave_ref[i] = jnp.take_along_axis(state_ref[i], pick, axis=0)[:moves]


def split(value):
    high = value.astype(jnp.bfloat16).astype(jnp.float32)
    rest = value - high
    middle = rest.astype(jnp.bfloat16).astype(jnp.float32)
    return high, middle, rest - middle


def composite_kernel(meta_ref, *refs):
    peers = meta_ref.shape[0] // 2
    sources = refs[:peers]
    target_ref = refs[peers]
    image_ref = refs[peers + 1]
    slots_ref = refs[peers + 2]
    pbuf, qbuf, abuf, wbuf, ebuf, shbuf, errbuf, rbuf, gbuf, basis, lbuf = refs[peers + 3 :]
    listed, _, lanes = pbuf.shape
    width = listed * lanes
    groups = width // 8
    chunks = errbuf.shape[0] // 8
    spreads = qbuf.shape[0]
    assert chunks == 8
    for d in range(peers):
        pos = meta_ref[d]
        loc = meta_ref[peers + d]
        for r in range(NPROJ):
            pbuf[pos, pl.ds(r, 1), :] = sources[d][r, pl.ds(loc, 1), :]

    lane = lax.broadcasted_iota(jnp.int32, (8, lanes), 1)
    which = lax.broadcasted_iota(jnp.int32, (8, lanes), 0)
    px = (lane % TILE_SIDE).astype(jnp.float32) + (0.5 - HALF)
    py = (lane // TILE_SIDE).astype(jnp.float32) + (0.5 - HALF)
    step = float(lanes // TILE_SIDE)
    middle = py + step * ((chunks - 1) / 2.0)
    zero = jnp.zeros((8, lanes), jnp.float32)
    one = zero + 1.0

    def rows(*values):
        out = zero
        for r, value in enumerate(values):
            out = jnp.where(which == r, value, out)
        return out

    blank = jnp.zeros((24, lanes), jnp.bfloat16)
    for c in range(chunks):
        y = py + step * c
        high, low, _ = split(px * y)
        mono = rows(one, px, y, (px * px - 0.25) * 0.5, (y * y - 0.25) * 0.5, high, low)
        part = jnp.concatenate([mono, mono, mono], axis=0).astype(jnp.bfloat16)
        basis[0:24, c * lanes : (c + 1) * lanes] = part
        basis[24:48, c * lanes : (c + 1) * lanes] = blank
    for k in range(spreads):
        pick = jnp.where(which == k, one, zero)
        at = (chunks + k) * lanes
        basis[0:24, at : at + lanes] = blank
        basis[24:48, at : at + lanes] = jnp.concatenate([pick, pick, pick], axis=0).astype(jnp.bfloat16)

    def product(left, right):
        return jnp.dot(left, right, preferred_element_type=jnp.float32)

    def alphas(j, _):
        mx, my, ca, cb, cc, op = [pbuf[j, r : r + 1, :] for r in range(6)]
        a = -0.5 * LOG2E * ca
        b = -LOG2E * cb
        c = -0.5 * LOG2E * cc
        bx = b * mx
        by = b * my
        ax = a * mx
        cy = c * my
        flat = (ax + by) * mx + cy * my + 0.25 * (a + c) + jnp.log(op) * LOG2E
        power = rows(flat, -(2.0 * ax + by), -(2.0 * cy + bx), 2.0 * a, 2.0 * c, b, b)
        plain = rows(mx, my, *[pbuf[j, 6 + k : 7 + k, :] for k in range(3)])
        colours = rows(*[pbuf[j, 6 + k : 7 + k, :] for k in range(3)])
        high, mid, low = split(colours)
        left = jnp.concatenate([*split(power), *split(plain)], axis=0).T.astype(jnp.bfloat16)
        lbuf[pl.ds(pl.multiple_of(j * lanes, lanes), lanes), :] = jnp.concatenate(
            [high, high, mid, mid, high, low], axis=0
        ).T.astype(jnp.bfloat16)
        out = product(left, basis[...])
        for u in range(lanes // 8):
            row = pl.multiple_of(j * lanes + u * 8, 8)
            for n in range(chunks):
                part = out[u * 8 : (u + 1) * 8, n * lanes : (n + 1) * lanes]
                abuf[pl.ds(row * chunks + n * 8, 8), :] = jnp.exp2(part)
            for k in range(spreads):
                qbuf[k, pl.ds(row, 8), :] = out[u * 8 : (u + 1) * 8, (chunks + k) * lanes : (chunks + k + 1) * lanes]
        return 0

    lax.fori_loop(0, listed, alphas, 0, unroll=min(listed, 4))

    batch = 16

    def forward(n, running):
        trans, image = running
        base = pl.multiple_of(n * (batch * chunks), batch * chunks)
        for i in range(batch):
            alpha = abuf[pl.ds(base + (i // 8) * (8 * chunks) + i % 8, chunks, stride=8), :]
            weight = trans * alpha
            trans = trans * (1.0 - alpha)
            wbuf[pl.ds(base + i * chunks, chunks), :] = weight
            image = tuple(
                image[k] + weight * jnp.broadcast_to(qbuf[2 + k, pl.ds(n * batch + i, 1), :], (chunks, lanes))
                for k in range(3)
            )
        return (trans, image)

    _, image = lax.fori_loop(0, width // batch, forward, (one, (zero, zero, zero)))
    for k in range(8):
        if k < 3:
            image_ref[k] = image[k]
            errbuf[k * chunks : (k + 1) * chunks, :] = 2.0 * (image[k] - target_ref[k])
        else:
            errbuf[k * chunks : (k + 1) * chunks, :] = zero
    for c in range(chunks):
        high, mid, low = split(errbuf[pl.ds(c, 8, stride=chunks), :])
        basis[:, c * lanes : (c + 1) * lanes] = jnp.concatenate([high, mid, high, mid, low, high], axis=0).astype(
            jnp.bfloat16
        )

    def shading(j, _):
        out = product(lbuf[pl.ds(pl.multiple_of(j * lanes, lanes), lanes), :], basis[:, : chunks * lanes])
        for u in range(lanes // 8):
            row = pl.multiple_of(j * lanes + u * 8, 8)
            for n in range(chunks):
                shbuf[pl.ds(row * chunks + n * 8, 8), :] = out[u * 8 : (u + 1) * 8, n * lanes : (n + 1) * lanes]
        return 0

    lax.fori_loop(0, listed, shading, 0, unroll=min(listed, 4))
    for buf in (wbuf, ebuf):
        buf[pl.ds(width * chunks, 8 * chunks), :] = jnp.zeros((8 * chunks, lanes), jnp.float32)
    for k in range(2):
        qbuf[k, pl.ds(width, 8), :] = zero

    def reduce_pixels(u):
        row = pl.multiple_of(u * 8, 8)
        base = pl.multiple_of(u * (8 * chunks), 8 * chunks)
        part = [ebuf[pl.ds(base + c, 8, stride=chunks), :] for c in range(chunks)]
        light = [wbuf[pl.ds(base + c, 8, stride=chunks), :] for c in range(chunks)]
        dx = px - qbuf[0, pl.ds(row, 8), :]
        dy = middle - qbuf[1, pl.ds(row, 8), :]
        half = chunks // 2
        away = [((chunks - 1) / 2.0 - c) * step for c in range(half)]
        even = [part[c] + part[chunks - 1 - c] for c in range(half)]
        odd = [part[chunks - 1 - c] - part[c] for c in range(half)]
        plain = (even[0] + even[1]) + (even[2] + even[3])
        tilt = (away[0] * odd[0] + away[1] * odd[1]) + (away[2] * odd[2] + away[3] * odd[3])
        bend = (away[0] ** 2 * even[0] + away[1] ** 2 * even[1]) + (away[2] ** 2 * even[2] + away[3] ** 2 * even[3])
        sum_y = dy * plain + tilt
        sum_yy = dy * (sum_y + tilt) + bend
        sum_x = dx * plain
        sums = [plain, sum_x, sum_y, dx * sum_x, dx * sum_y, sum_yy]
        for k in range(3):
            lit = [light[c] * jnp.broadcast_to(errbuf[pl.ds(k * chunks + c, 1), :], (8, lanes)) for c in range(chunks)]
            sums.append(((lit[0] + lit[1]) + (lit[2] + lit[3])) + ((lit[4] + lit[5]) + (lit[6] + lit[7])))
        for r, value in enumerate(sums):
            rbuf[r, pl.ds(row, 8), :] = value

    def backward(n, behind):
        u = groups - 1 - n
        base = pl.multiple_of(u * (8 * chunks), 8 * chunks)
        reduce_pixels(u + 1)
        for i in reversed(range(8)):
            alpha = abuf[pl.ds(base + i, chunks, stride=8), :]
            ahead = shbuf[pl.ds(base + i, chunks, stride=8), :] - behind
            behind = behind + alpha * ahead
            ebuf[pl.ds(base + i * chunks, chunks), :] = wbuf[pl.ds(base + i * chunks, chunks), :] * ahead
        return behind

    lax.fori_loop(0, groups, backward, zero, unroll=2)
    reduce_pixels(0)

    def finish(j, _):
        at = pl.ds(pl.multiple_of(j * lanes, lanes), lanes)
        part = [jnp.sum(rbuf[r, at, :].T, axis=0, keepdims=True) for r in range(NPROJ)]
        s0, sx, sy, sxx, sxy, syy = part[:6]
        ca, cb, cc, op = [pbuf[j, r : r + 1, :] for r in range(2, 6)]
        gbuf[j, 0:1, :] = ca * sx + cb * sy
        gbuf[j, 1:2, :] = cb * sx + cc * sy
        gbuf[j, 2:3, :] = -0.5 * sxx
        gbuf[j, 3:4, :] = -sxy
        gbuf[j, 4:5, :] = -0.5 * syy
        gbuf[j, 5:6, :] = s0 / op
        for k in range(3):
            gbuf[j, 6 + k : 7 + k, :] = part[6 + k]
        gbuf[j, 9:16, :] = jnp.zeros((7, lanes), jnp.float32)
        return 0

    lax.fori_loop(0, listed, finish, 0, unroll=min(listed, 4))
    for d in range(peers):
        slots_ref[d] = gbuf[meta_ref[d]]
        slots_ref[d, NPROJ : NPROJ + 1, :] = jnp.full((1, lanes), 1, jnp.float32) * meta_ref[peers + d].astype(jnp.float32)


TERMS = 2 + 3 * 8 + 1 + 3


def prepare_kernel(moving_ref, basis_ref, state_ref, came_ref, mixed_ref, slope_ref, kbuf):
    total, blocks, lanes = state_ref.shape
    rows = total // 3
    moves = came_ref.shape[1]
    source, taken = picks(moving_ref, blocks, lanes)

    def arrived(i):
        kbuf[i % 8, 0:moves, :] = came_ref[i]
        return jnp.take_along_axis(kbuf[i % 8], source, axis=0)

    for a, factor in enumerate((None, beta_one, beta_two)):
        for i in range(a * rows, (a + 1) * rows):
            value = jnp.where(taken, arrived(i), state_ref[i])
            mixed_ref[i] = value if factor is None else factor * value
    slot = lax.broadcasted_iota(jnp.int32, (blocks, lanes), 0).astype(jnp.float32)
    slope_ref[TERMS] = jnp.where(taken, arrived(total), slot)
    slope_ref[TERMS + 1] = taken.astype(jnp.float32)

    part = 1.0 - beta_one
    p = lambda i: mixed_ref[i]
    v = geometry(p)
    slope_ref[0] = part * 0.375 * TILE_SIDE * (1.0 - v["tx"] * v["tx"])
    slope_ref[1] = part * 0.375 * TILE_SIDE * (1.0 - v["ty"] * v["ty"])
    slope_ref[TERMS - 4] = part * 0.99 * v["so"] * (1.0 - v["so"])
    for c in range(3):
        shade = colour(p, c, lambda k: basis_ref[k])
        slope_ref[TERMS - 3 + c] = part * shade * (1.0 - shade)
    U, L, e, f, idet = v["U"], v["L"], v["e"], v["f"], v["idet"]
    w, x, y, z = v["q"]
    share = jnp.where(v["norm"] > 1.0, 1.0, jnp.where(v["norm"] == 1.0, 0.5, 0.0))
    depth = (-2.0 / 3.0) * f * f * f * sigmoid(p(2)) * part
    for n, name in enumerate("ABC"):
        gdet = -v[name] * idet
        gxx = gdet * v["yy"]
        gyy = gdet * v["xx"]
        gxy = -2.0 * gdet * v["xy"]
        if name == "A":
            gyy = gyy + idet
        elif name == "B":
            gxy = gxy - idet
        else:
            gxx = gxx + idet
        slope_ref[2 + n] = (gxx * v["sxx"] + gyy * v["syy"] + gxy * v["sxy"]) * depth
        gU, gL = [], []
        for k in range(3):
            t = v["ts"][k]
            ze = v["z"] * e[k]
            ge = gxx * U[k] * U[k] + gyy * L[k] * L[k] + gxy * U[k] * L[k]
            slope_ref[5 + 3 * k + n] = (2.0 * part) * ge * ze * (1.0 - t * t)
            gU.append(ze * (2.0 * gxx * U[k] + gxy * L[k]))
            gL.append(ze * (2.0 * gyy * L[k] + gxy * U[k]))
        gq = [
            2.0 * (z * (gL[0] - gU[1]) + y * gU[2] - x * gL[2]),
            2.0 * (y * (gU[1] + gL[0]) + z * gU[2] - 2.0 * x * gL[1] - w * gL[2]),
            2.0 * (x * (gU[1] + gL[0]) - 2.0 * y * gU[0] + w * gU[2] + z * gL[2]),
            2.0 * (w * (gL[0] - gU[1]) - 2.0 * z * (gU[0] + gL[1]) + x * gU[2] + y * gL[2]),
        ]
        along = share * (w * gq[0] + x * gq[1] + y * gq[2] + z * gq[3])
        for k, unit in enumerate((w, x, y, z)):
            slope_ref[14 + 3 * k + n] = part * (gq[k] - unit * along) * v["inv"]


def update_kernel(basis_ref, mixed_ref, slope_ref, image_ref, *refs):
    sources = refs[:-9]
    outs = refs[-9:-6]
    picture_hbm = refs[-6]
    stages = refs[-5:-2]
    sems, picture_sem = refs[-2:]
    total, blocks, lanes = mixed_ref.shape
    rows = total // 3
    picture = pltpu.make_async_copy(image_ref, picture_hbm, picture_sem.at[0])
    picture.start()
    want = slope_ref[TERMS]
    taken = slope_ref[TERMS + 1] > 0.5
    wide = lambda row: jnp.broadcast_to(row, (blocks, lanes))
    grads = [jnp.zeros((blocks, lanes), jnp.float32) for _ in range(NPROJ)]
    for ref in sources:
        for side in range(2):
            mask = jnp.logical_and(want == wide(ref[side, NPROJ : NPROJ + 1, :]), taken if side else ~taken)
            for r in range(NPROJ):
                grads[r] = grads[r] + jnp.where(mask, wide(ref[side, r : r + 1, :]), 0.0)

    def store(i, grad):
        one = mixed_ref[rows + i] + grad
        two = mixed_ref[2 * rows + i] + ((1.0 - beta_two) / (1.0 - beta_one) ** 2) * (grad * grad)
        scaled = (rate_of(i) / (1.0 - beta_one**adam_step)) * one
        stages[0][i] = mixed_ref[i] - scaled / (jnp.sqrt(two * (1.0 / (1.0 - beta_two**adam_step))) + adam_eps)
        stages[1][i] = one
        stages[2][i] = two

    copies = []

    def ship(low, high):
        for a in range(3):
            copy = pltpu.make_async_copy(
                stages[a].at[low:high], outs[a].at[low:high], sems.at[len(copies)]
            )
            copy.start()
            copies.append(copy)

    for c in range(3):
        logit = grads[6 + c] * slope_ref[TERMS - 3 + c]
        for k in range(SH):
            store(11 + SH * c + k, logit * basis_ref[k])
        ship(11 + SH * c, 11 + SH * (c + 1))
    store(0, grads[0] * slope_ref[0])
    store(1, grads[1] * slope_ref[1])
    for i in range(8):
        at = 2 + 3 * i
        store(2 + i, grads[2] * slope_ref[at] + grads[3] * slope_ref[at + 1] + grads[4] * slope_ref[at + 2])
    store(10, grads[5] * slope_ref[TERMS - 4])
    ship(0, 11)
    for copy in copies:
        copy.wait()
    picture.wait()


def on_device(params, first_moment, second_moment, view_basis, target, tile_blocks, moving):
    blocks, rows, lanes = params.shape
    peers = lax.axis_size("tile")
    listed = tile_blocks.shape[1]
    moves = moving.shape[1]
    pixels = target.shape[2]
    chunks = pixels // lanes
    width = listed * lanes
    f32 = jnp.float32
    smem = pl.BlockSpec(memory_space=pltpu.SMEM)
    vmem = pl.BlockSpec(memory_space=pltpu.VMEM)
    sds = jax.ShapeDtypeStruct

    me = lax.axis_index("tile")
    partner = jnp.bitwise_xor(me, jnp.arange(peers, dtype=jnp.int32))
    matches = (tile_blocks[0][None, :] // blocks) == partner[:, None]
    pos = jnp.sum(jnp.where(matches, jnp.arange(listed, dtype=jnp.int32)[None, :], 0), axis=1)
    loc = jnp.sum(jnp.where(matches, (tile_blocks[0] % blocks)[None, :], 0), axis=1)
    meta = jnp.concatenate([pos, loc]).astype(jnp.int32)

    hbm = pl.BlockSpec(memory_space=pltpu.HBM)
    stay = lambda value: pltpu.with_memory_space_constraint(value, pltpu.HBM)
    dma = pltpu.SemaphoreType.DMA
    turned = [jnp.transpose(a, (1, 0, 2)) for a in (params, first_moment, second_moment)]
    projected = pl.pallas_call(
        project_kernel,
        out_shape=sds((NPROJ, blocks, lanes), f32),
        in_specs=[hbm, hbm],
        out_specs=vmem,
        scratch_shapes=[pltpu.VMEM((rows, blocks, lanes), f32), pltpu.SMEM(view_basis.shape, f32), dma((3,))],
        compiler_params=pltpu.CompilerParams(vmem_limit_bytes=2 << 20),
        name="project",
    )(stay(view_basis), stay(turned[0]))
    leaving, state = pl.pallas_call(
        pack_kernel,
        out_shape=(sds((3 * rows + 1, moves, lanes), f32), sds((3 * rows, blocks, lanes), f32)),
        in_specs=[smem, hbm, hbm, hbm],
        out_specs=(vmem, vmem),
        scratch_shapes=[dma((3,))],
        compiler_params=pltpu.CompilerParams(vmem_limit_bytes=4 << 20),
        name="pack",
    )(moving, *[stay(a) for a in turned])

    def swapped(value, d):
        return lax.ppermute(value, "tile", [(i, i ^ d) for i in range(peers)])

    regions = lax.axis_size("region")
    onward = lambda value: lax.ppermute(value, "region", [(i, (i + 1) % regions) for i in range(regions)])

    away = {d: swapped(projected, d) for d in reversed(range(1, peers))}
    came = onward(leaving)
    image, slots = pl.pallas_call(
        composite_kernel,
        out_shape=(sds((3, chunks, lanes), f32), sds((peers, GRADS, lanes), f32)),
        in_specs=[smem] + [vmem] * (peers + 1),
        out_specs=(vmem, vmem),
        scratch_shapes=[
            pltpu.VMEM((listed, GRADS, lanes), f32),
            pltpu.VMEM((5, width + 8, lanes), f32),
            pltpu.VMEM((chunks * width, lanes), f32),
            pltpu.VMEM((chunks * (width + 8), lanes), f32),
            pltpu.VMEM((chunks * (width + 8), lanes), f32),
            pltpu.VMEM((chunks * width, lanes), f32),
            pltpu.VMEM((8 * chunks, lanes), f32),
            pltpu.VMEM((NPROJ, width + 8, lanes), f32),
            pltpu.VMEM((listed, GRADS, lanes), f32),
            pltpu.VMEM((48, (chunks + 5) * lanes), jnp.bfloat16),
            pltpu.VMEM((width, 48), jnp.bfloat16),
        ],
        compiler_params=pltpu.CompilerParams(vmem_limit_bytes=(4 * chunks + 20) * (width + 8) * lanes * 4 + (3 << 20)),
        name="composite",
    )(meta, projected, *[away[d] for d in range(1, peers)], target.reshape(3, chunks, lanes))
    mixed, slope = pl.pallas_call(
        prepare_kernel,
        out_shape=(sds((3 * rows, blocks, lanes), f32), sds((TERMS + 2, blocks, lanes), f32)),
        in_specs=[smem, smem, vmem, vmem],
        out_specs=(vmem, vmem),
        scratch_shapes=[pltpu.VMEM((8, blocks, lanes), f32)],
        compiler_params=pltpu.CompilerParams(vmem_limit_bytes=5 << 20),
        name="prepare",
    )(moving, view_basis, state, came)
    pairs = jnp.stack([slots, onward(slots)], axis=1)
    gathered = {0: pairs[0]}
    for d in reversed(range(1, peers)):
        gathered[d] = swapped(pairs[d], d)
    updated = pl.pallas_call(
        update_kernel,
        out_shape=(sds((rows, blocks, lanes), f32),) * 3 + (sds(image.shape, f32),),
        in_specs=[smem] + [vmem] * (3 + peers),
        out_specs=(hbm,) * 4,
        scratch_shapes=[pltpu.VMEM((rows, blocks, lanes), f32)] * 3 + [dma((12,)), dma((1,))],
        compiler_params=pltpu.CompilerParams(vmem_limit_bytes=5 << 20),
        name="update",
    )(view_basis, mixed, slope, image, *[gathered[d] for d in range(peers)])
    turned_back = [jnp.transpose(a, (1, 0, 2)) for a in updated[:3]]
    return (*turned_back, updated[3].reshape(1, 3, pixels))


def solution(mesh):
    three = P(("region", "tile"), None, None)
    two = P(("region", "tile"), None)
    return jax.shard_map(
        on_device,
        mesh=mesh,
        in_specs=(three, three, three, P(), three, two, two),
        out_specs=(three, three, three, three),
        check_vma=False,
    )
```

time: 45.3 us -> 32.5 us (0.72)
  Pallas kernels: 19.8 us -> 10.9 us
  waiting for transfers between devices: 11.6 us -> 8.94 us
  local copies, waits for them, and re-layouts: 2.71 us -> 1.23 us
    pallas_call x1, Pallas kernels: 13.9 us -> 5.76 us  [on_device(): pl.pallas_call(composite_kernel, out_shape=(sds((3, chunks, lanes), f32),...]
    ppermute x6, waiting for transfers between devices: 7.26 us -> 4.71 us  [swapped(): return lax.ppermute(value, 'tile', [(i, i ^ d) for i in range(peers)])]
    unnamed x18 -> x8, local copies, waits for them, and re-layouts: 2.71 us -> 1.23 us
    pallas_call x1, Pallas kernels: 2.4 us -> 1.56 us  [on_device(): pl.pallas_call(update_kernel, out_shape=(sds((rows, blocks, lanes), f32),...]
    pallas_call x2 -> x3, Pallas kernels: 3.45 us -> 3.61 us  [the longest x1 1.76 us: on_device(): pl.pallas_call(pack_kernel, out_shape=(sds((3 * rows + 1, moves, lanes),...]
  transfers between devices with their start and end apart: 8 -> 8, of which waited for: 5 -> 3; matrix products, arithmetic and copies ran while one was open for 1% -> 1% of each run, Pallas kernels for 34% -> 26%
where the time goes in v3:
time: 32.5 us; the launch traced here: 32.3 us
  Pallas kernels  10.9 us (34%)
  starting transfers between devices  10.2 us (31%)
  waiting for transfers between devices  8.94 us (28%)
  local copies, waits for them, and re-layouts  1.23 us (4%)
  between operations  0.73 us (2%)
    ppermute x6, starting transfers between devices, swapped(): return lax.ppermute(value, 'tile', [(i, i ^ d) for i in range(peers)])  10.1 us
    pallas_call x1, Pallas kernels, on_device(): pl.pallas_call(composite_kernel, out_shape=(sds((3, chunks, lanes), f32),...  5.76 us
    ppermute x6, waiting for transfers between devices, swapped(): return lax.ppermute(value, 'tile', [(i, i ^ d) for i in range(peers)])  4.71 us
    ppermute x2, waiting for transfers between devices, on_device(): lax.ppermute(value, 'region', [(i, (i + 1) % regions) for i in range(regi...  4.23 us
    pallas_call x1, Pallas kernels, on_device(): pl.pallas_call(pack_kernel, out_shape=(sds((3 * rows + 1, moves, lanes),...  1.76 us
    pallas_call x1, Pallas kernels, on_device(): pl.pallas_call(update_kernel, out_shape=(sds((rows, blocks, lanes), f32),...  1.56 us
    unnamed x8, local copies, waits for them, and re-layouts  1.23 us
    pallas_call x1, Pallas kernels, on_device(): pl.pallas_call(project_kernel, out_shape=sds((NPROJ, blocks, lanes), f32)...  1.03 us
  transfers between devices with their start and end apart: 8, of which 3 were waited for; matrix products, arithmetic and copies ran while one was open for 1% of the time, Pallas kernels for 26%

profile of v3, /device:TPU:0, one launch (start us, length us, event | category | flops | bytes accessed | tf_op | source)
XLA Modules:
  0.0 32.3 jit_solution(871089293233472238)
XLA Ops:
  0.6 1.0 %project.1.refs_0_ = f32[9,8,128]{2,1,0:T(8,128)S(1)} custom-call(f32[16]{0:T(128)} %basis_ref.3, f32[59,8,128]{2,1,0:T(8,128)} %bitcast.24), custom_call_target="tpu_custom_call" | custom-call | tf_op jit(solution)/shard_map/project/pallas_call | solution.py:472
  1.7 3.1 %collective-permute-start.1 = (f32[9,8,128]{2,1,0:T(8,128)S(1)}, f32[9,8,128]{2,1,0:T(8,128)S(1)}, u32[]{:S(2)}, u32[]{:S(2)}) collective-permute-start(f32[9,8,128]{2,1,0:T(8,128)S(1)} %project.1.refs_0_), channel_id=1, source_target_pairs={{0,1},{1,0},{2,3},{3,2},{4,5},{5,4},{6,7},{7,6},{8,9},{9,8},{10,11... | collective-permute-start | bytes 110600 | tf_op jit(solution)/shard_map/ppermute | solution.py:492
  4.8 2.6 %collective-permute-start.2 = (f32[9,8,128]{2,1,0:T(8,128)S(1)}, f32[9,8,128]{2,1,0:T(8,128)S(1)}, u32[]{:S(2)}, u32[]{:S(2)}) collective-permute-start(f32[9,8,128]{2,1,0:T(8,128)S(1)} %project.1.refs_0_), channel_id=1, source_target_pairs={{0,2},{1,3},{2,0},{3,1},{4,6},{5,7},{6,4},{7,5},{8,10},{9,11},{10,... | collective-permute-start | bytes 110600 | tf_op jit(solution)/shard_map/ppermute | solution.py:492
  7.4 0.0 collective-permute-start.3
  7.4 0.7 %copy-done.2 = s32[1,4]{1,0:T(1,128)S(1)} copy-done((s32[1,4]{1,0:T(1,128)S(1)}, s32[1,4]{1,0:T(1,128)}, u32[]{:S(2)}) %copy-start.2) | copy-done | bytes 40
  8.0 1.8 %pack.1 = (f32[178,4,128]{2,1,0:T(4,128)S(1)}, f32[177,8,128]{2,1,0:T(8,128)S(1)}) custom-call(s32[1,4]{1,0:T(1,128)S(1)} %copy-done.2, f32[59,8,128]{2,1,0:T(8,128)} %bitcast.25, f32[59,8,128]{2,1,0:T(8,128)} %bitcast.26, f32[59,8,128]{2,1,0:T(8,128)} %bitcast.27), custom_call_target="tpu_custom_call" | custom-call | tf_op jit(solution)/shard_map/pack/pallas_call | solution.py:481
  9.8 0.0 copy-start.3
  9.8 0.0 copy-start
  9.8 0.1 collective-permute-start
  9.9 0.6 %copy-done.3 = s32[1,4]{1,0:T(1,128)S(1)} copy-done((s32[1,4]{1,0:T(1,128)S(1)}, s32[1,4]{1,0:T(1,128)}, u32[]{:S(2)}) %copy-start.3) | copy-done | bytes 40
  10.5 0.2 fusion.7
  10.6 0.1 pad_add_fusion.meta_ref
  10.7 0.0 collective-permute-done.1.refs_1_
  10.7 2.4 %collective-permute-done.3.refs_3_ = f32[9,8,128]{2,1,0:T(8,128)S(1)} collective-permute-done((f32[9,8,128]{2,1,0:T(8,128)S(1)}, f32[9,8,128]{2,1,0:T(8,128)S(1)}, u32[]{:S(2)}, u32[]{:S(2)}) %collective-permute-start.3) | collective-permute-done | bytes 36896 | tf_op jit(solution)/shard_map/ppermute | solution.py:492
  13.1 5.8 %composite.1 = (f32[3,8,128]{2,1,0:T(8,128)S(1)}, f32[4,16,128]{2,1,0:T(8,128)S(1)}) custom-call(s32[8]{0:T(128)S(1)} %pad_add_fusion.meta_ref, f32[9,8,128]{2,1,0:T(8,128)S(1)} %project.1.refs_0_, f32[9,8,128]{2,1,0:T(8,128)S(1)} %collective-permute-done.1.refs_1_, f32[9,8,128]{2,1,0:T(8,128)S(1)} %collective-permute-done.2.refs_2_, ...), custom_call_target="tpu_custom_call" | custom-call | tf_op jit(solution)/shard_map/composite/pallas_call | solution.py:499
  18.9 0.1 collective-permute-start.4
  18.9 4.2 %collective-permute-done.4 = f32[4,16,128]{2,1,0:T(8,128)S(1)} collective-permute-done((f32[4,16,128]{2,1,0:T(8,128)S(1)}, f32[4,16,128]{2,1,0:T(8,128)S(1)}, u32[]{:S(2)}, u32[]{:S(2)}) %collective-permute-start.4) | collective-permute-done | bytes 32800 | tf_op jit(solution)/shard_map/ppermute | solution.py:495
  23.2 2.0 %collective-permute-start.6 = (f32[2,16,128]{2,1,0:T(8,128)S(1)}, f32[2,16,128]{2,1,0:T(8,128)S(1)}, u32[]{:S(2)}, u32[]{:S(2)}) collective-permute-start(f32[2,16,128]{2,1,0:T(8,128)S(1)} %get-tuple-element.41), channel_id=1, source_target_pairs={{0,2},{1,3},{2,0},{3,1},{4,6},{5,7},{6,4},{7,5},{8,10},{9,11},{10,... | collective-permute-start | bytes 49160 | tf_op jit(solution)/shard_map/ppermute | solution.py:492
  25.2 2.4 %collective-permute-start.7 = (f32[2,16,128]{2,1,0:T(8,128)S(1)}, f32[2,16,128]{2,1,0:T(8,128)S(1)}, u32[]{:S(2)}, u32[]{:S(2)}) collective-permute-start(f32[2,16,128]{2,1,0:T(8,128)S(1)} %get-tuple-element.38), channel_id=1, source_target_pairs={{0,3},{1,2},{2,1},{3,0},{4,7},{5,6},{6,5},{7,4},{8,11},{9,10},{10,... | collective-permute-start | bytes 49160 | tf_op jit(solution)/shard_map/ppermute | solution.py:492
  27.6 0.0 collective-permute-done.came_ref
  27.6 0.8 %prepare.1 = (f32[177,8,128]{2,1,0:T(8,128)S(1)}, f32[32,8,128]{2,1,0:T(8,128)S(1)}) custom-call(s32[1,4]{1,0:T(1,128)S(1)} %copy-done.2, f32[16]{0:T(128)S(1)} %copy-done.1, f32[177,8,128]{2,1,0:T(8,128)S(1)} %get-tuple-element.14.state_ref, f32[178,4,128]{2,1,0:T(4,128)S(1)} %collective-permute-done.came_ref), custom_call_target="tpu_custom_call" | custom-call | tf_op jit(solution)/shard_map/prepare/pallas_call | solution.py:520
  28.4 0.0 collective-permute-done.6.refs_2_
  28.4 2.3 %collective-permute-done.7.refs_3_ = f32[2,16,128]{2,1,0:T(8,128)S(1)} collective-permute-done((f32[2,16,128]{2,1,0:T(8,128)S(1)}, f32[2,16,128]{2,1,0:T(8,128)S(1)}, u32[]{:S(2)}, u32[]{:S(2)}) %collective-permute-start.7) | collective-permute-done | bytes 16416 | tf_op jit(solution)/shard_map/ppermute | solution.py:492
  30.7 1.6 %update.1 = (f32[59,8,128]{2,1,0:T(8,128)}, f32[59,8,128]{2,1,0:T(8,128)}, f32[59,8,128]{2,1,0:T(8,128)}, f32[3,8,128]{2,1,0:T(8,128)}) custom-call(f32[16]{0:T(128)S(1)} %copy-done.1, f32[177,8,128]{2,1,0:T(8,128)S(1)} %get-tuple-element.16.mixed_ref, f32[32,8,128]{2,1,0:T(8,128)S(1)} %get-tuple-element.17.slope_ref, ...), custom_call_target="tpu_custom_call" | custom-call | tf_op jit(solution)/shard_map/update/pallas_call | solution.py:533
  (10 shorter events, 0.0 us)
Async XLA Ops:
  1.7 9.1 %collective-permute-start.1 = (f32[9,8,128]{2,1,0:T(8,128)S(1)}, f32[9,8,128]{2,1,0:T(8,128)S(1)}, u32[]{:S(2)}, u32[]{:S(2)}) collective-permute-start(f32[9,8,128]{2,1,0:T(8,128)S(1)} %project.1.refs_0_), channel_id=1, source_target_pairs={{0,1},{1,0},{2,3},{3,2},{4,5},{5,4},{6,7},{7,6},{8,9},{9,8},{10,11... | collective-permute-start | bytes 110600 | tf_op jit(solution)/shard_map/ppermute | solution.py:492
  4.8 6.0 %collective-permute-start.2 = (f32[9,8,128]{2,1,0:T(8,128)S(1)}, f32[9,8,128]{2,1,0:T(8,128)S(1)}, u32[]{:S(2)}, u32[]{:S(2)}) collective-permute-start(f32[9,8,128]{2,1,0:T(8,128)S(1)} %project.1.refs_0_), channel_id=1, source_target_pairs={{0,2},{1,3},{2,0},{3,1},{4,6},{5,7},{6,4},{7,5},{8,10},{9,11},{10,... | collective-permute-start | bytes 110600 | tf_op jit(solution)/shard_map/ppermute | solution.py:492
  7.4 5.8 %collective-permute-start.3 = (f32[9,8,128]{2,1,0:T(8,128)S(1)}, f32[9,8,128]{2,1,0:T(8,128)S(1)}, u32[]{:S(2)}, u32[]{:S(2)}) collective-permute-start(f32[9,8,128]{2,1,0:T(8,128)S(1)} %project.1.refs_0_), channel_id=1, source_target_pairs={{0,3},{1,2},{2,1},{3,0},{4,7},{5,6},{6,5},{7,4},{8,11},{9,10},{10,... | collective-permute-start | bytes 110600 | tf_op jit(solution)/shard_map/ppermute | solution.py:492
  7.4 0.7 %copy-start.2 = (s32[1,4]{1,0:T(1,128)S(1)}, s32[1,4]{1,0:T(1,128)}, u32[]{:S(2)}) copy-start(s32[1,4]{1,0:T(1,128)} %moving_ref.3) | copy-start | bytes 52
  9.8 0.7 %copy-start.3 = (s32[1,4]{1,0:T(1,128)S(1)}, s32[1,4]{1,0:T(1,128)}, u32[]{:S(2)}) copy-start(s32[1,4]{1,0:T(1,128)} %param.12) | copy-start | bytes 52
  9.8 3.3 %copy-start = (f32[1,3,1024]{2,0,1:T(1,128)S(1)}, f32[1,3,1024]{2,0,1:T(1,128)}, u32[]{:S(2)}) copy-start(f32[1,3,1024]{2,0,1:T(1,128)} %param.11) | copy-start | bytes 36868
  9.8 17.8 %collective-permute-start = (f32[178,4,128]{2,1,0:T(4,128)S(1)}, f32[178,4,128]{2,1,0:T(4,128)S(1)}, u32[]{:S(2)}, u32[]{:S(2)}) collective-permute-start(f32[178,4,128]{2,1,0:T(4,128)S(1)} %get-tuple-element.15), channel_id=1, source_target_pairs={{0,4},{4,8},{8,12},{12,16},{16,20},{20,24},{24,28},{28,0},{1,5},{5... | collective-permute-start | bytes 1093640 | tf_op jit(solution)/shard_map/ppermute | solution.py:495
  18.9 4.3 %collective-permute-start.4 = (f32[4,16,128]{2,1,0:T(8,128)S(1)}, f32[4,16,128]{2,1,0:T(8,128)S(1)}, u32[]{:S(2)}, u32[]{:S(2)}) collective-permute-start(f32[4,16,128]{2,1,0:T(8,128)S(1)} %get-tuple-element.19), channel_id=1, source_target_pairs={{0,4},{4,8},{8,12},{12,16},{16,20},{20,24},{24,28},{28,0},{1,5},{5... | collective-permute-start | bytes 98312 | tf_op jit(solution)/shard_map/ppermute | solution.py:495
  23.2 5.2 %collective-permute-start.5 = (f32[2,16,128]{2,1,0:T(8,128)S(1)}, f32[2,16,128]{2,1,0:T(8,128)S(1)}, u32[]{:S(2)}, u32[]{:S(2)}) collective-permute-start(f32[2,16,128]{2,1,0:T(8,128)S(1)} %get-tuple-element.40), channel_id=1, source_target_pairs={{0,1},{1,0},{2,3},{3,2},{4,5},{5,4},{6,7},{7,6},{8,9},{9,8},{10,11... | collective-permute-start | bytes 49160 | tf_op jit(solution)/shard_map/ppermute | solution.py:492
  23.2 5.2 %collective-permute-start.6 = (f32[2,16,128]{2,1,0:T(8,128)S(1)}, f32[2,16,128]{2,1,0:T(8,128)S(1)}, u32[]{:S(2)}, u32[]{:S(2)}) collective-permute-start(f32[2,16,128]{2,1,0:T(8,128)S(1)} %get-tuple-element.41), channel_id=1, source_target_pairs={{0,2},{1,3},{2,0},{3,1},{4,6},{5,7},{6,4},{7,5},{8,10},{9,11},{10,... | collective-permute-start | bytes 49160 | tf_op jit(solution)/shard_map/ppermute | solution.py:492
  25.2 2.4 %copy-start.1 = (f32[16]{0:T(128)S(1)}, f32[16]{0:T(128)}, u32[]{:S(2)}) copy-start(f32[16]{0:T(128)} %basis_ref.3) | copy-start | bytes 196
  25.2 5.5 %collective-permute-start.7 = (f32[2,16,128]{2,1,0:T(8,128)S(1)}, f32[2,16,128]{2,1,0:T(8,128)S(1)}, u32[]{:S(2)}, u32[]{:S(2)}) collective-permute-start(f32[2,16,128]{2,1,0:T(8,128)S(1)} %get-tuple-element.38), channel_id=1, source_target_pairs={{0,3},{1,2},{2,1},{3,0},{4,7},{5,6},{6,5},{7,4},{8,11},{9,10},{10,... | collective-permute-start | bytes 49160 | tf_op jit(solution)/shard_map/ppermute | solution.py:492

commit v4 on v3

--- a/solution.py
+++ b/solution.py
@@ -79,13 +79,17 @@
     return sigmoid(total)
 
 
-def project_kernel(basis_hbm, p_hbm, proj_ref, p_ref, basis_ref, sems):
+def project_kernel(peers, basis_hbm, listed_hbm, p_hbm, proj_ref, meta_ref, p_ref, basis_ref, listed_ref, sems):
     head = 11
+    blocks = p_ref.shape[1]
     copies = [
         pltpu.make_async_copy(p_hbm.at[:head], p_ref.at[:head], sems.at[0]),
-        pltpu.make_async_copy(p_hbm.at[head:], p_ref.at[head:], sems.at[1]),
-        pltpu.make_async_copy(basis_hbm, basis_ref, sems.at[2]),
+        pltpu.make_async_copy(basis_hbm, basis_ref, sems.at[1]),
+        pltpu.make_async_copy(listed_hbm, listed_ref, sems.at[2]),
     ]
+    for c in range(3):
+        span = pl.ds(head + SH * c, SH)
+        copies.append(pltpu.make_async_copy(p_hbm.at[span], p_ref.at[span], sems.at[3 + c]))
     for copy in copies:
         copy.start()
     p = lambda i: p_ref[i]
@@ -97,9 +101,16 @@
     proj_ref[3] = v["B"]
     proj_ref[4] = v["C"]
     proj_ref[5] = 0.99 * v["so"]
+    copies[2].wait()
+    me = lax.axis_index("tile")
+    for n in range(listed_ref.shape[1]):
+        listed = listed_ref[0, n]
+        distance = jnp.bitwise_xor(listed // blocks, me)
+        meta_ref[distance] = n
+        meta_ref[peers + distance] = listed % blocks
     copies[1].wait()
-    copies[2].wait()
     for c in range(3):
+        copies[3 + c].wait()
         proj_ref[6 + c] = colour(p, c, lambda k: basis_ref[k])
 
 
@@ -114,23 +125,37 @@
     return source, taken
 
 
-def pack_kernel(moving_ref, p_hbm, f_hbm, s_hbm, leave_ref, state_ref, sems):
+PIECES = 4
+
+
+def pieces(rows):
+    cuts = [rows * n // PIECES for n in range(PIECES + 1)]
+    return list(zip(cuts[:-1], cuts[1:]))
+
+
+def pack_kernel(moving_hbm, p_hbm, f_hbm, s_hbm, leave_ref, state_ref, moving_ref, sems):
     total, moves, lanes = leave_ref.shape
     rows, blocks, _ = p_hbm.shape
-    copies = [
-        pltpu.make_async_copy(ref, state_ref.at[a * rows : (a + 1) * rows], sems.at[a])
-        for a, ref in enumerate((p_hbm, f_hbm, s_hbm))
-    ]
-    for copy in copies:
-        copy.start()
+    ids = pltpu.make_async_copy(moving_hbm, moving_ref, sems.at[3 * PIECES])
+    ids.start()
+    spans = []
+    copies = []
+    for a, ref in enumerate((p_hbm, f_hbm, s_hbm)):
+        for low, high in pieces(rows):
+            span = (a * rows + low, a * rows + high)
+            copy = pltpu.make_async_copy(ref.at[low:high], state_ref.at[span[0] : span[1]], sems.at[len(copies)])
+            copy.start()
+            spans.append(span)
+            copies.append(copy)
+    ids.wait()
     slot = lax.broadcasted_iota(jnp.int32, (blocks, lanes), 0)
     pick = jnp.zeros((blocks, lanes), jnp.int32)
     for m in range(moves):
         pick = jnp.where(slot == m, moving_ref[0, m], pick)
     leave_ref[total - 1] = pick[:moves].astype(jnp.float32)
-    for a in range(3):
-        copies[a].wait()
-        for i in range(a * rows, (a + 1) * rows):
+    for copy, span in zip(copies, spans):
+        copy.wait()
+        for i in range(*span):
             leave_ref[i] = jnp.take_along_axis(state_ref[i], pick, axis=0)[:moves]
 
 
@@ -143,7 +168,7 @@
 
 def composite_kernel(meta_ref, *refs):
     peers = meta_ref.shape[0] // 2
-    sources = refs[:peers]
+    sources = refs[:peers][::-1]
     target_ref = refs[peers]
     image_ref = refs[peers + 1]
     slots_ref = refs[peers + 2]
@@ -458,43 +483,44 @@
     vmem = pl.BlockSpec(memory_space=pltpu.VMEM)
     sds = jax.ShapeDtypeStruct
 
-    me = lax.axis_index("tile")
-    partner = jnp.bitwise_xor(me, jnp.arange(peers, dtype=jnp.int32))
-    matches = (tile_blocks[0][None, :] // blocks) == partner[:, None]
-    pos = jnp.sum(jnp.where(matches, jnp.arange(listed, dtype=jnp.int32)[None, :], 0), axis=1)
-    loc = jnp.sum(jnp.where(matches, (tile_blocks[0] % blocks)[None, :], 0), axis=1)
-    meta = jnp.concatenate([pos, loc]).astype(jnp.int32)
-
     hbm = pl.BlockSpec(memory_space=pltpu.HBM)
     stay = lambda value: pltpu.with_memory_space_constraint(value, pltpu.HBM)
     dma = pltpu.SemaphoreType.DMA
     turned = [jnp.transpose(a, (1, 0, 2)) for a in (params, first_moment, second_moment)]
-    projected = pl.pallas_call(
-        project_kernel,
-        out_shape=sds((NPROJ, blocks, lanes), f32),
-        in_specs=[hbm, hbm],
-        out_specs=vmem,
-        scratch_shapes=[pltpu.VMEM((rows, blocks, lanes), f32), pltpu.SMEM(view_basis.shape, f32), dma((3,))],
+    projected, meta = pl.pallas_call(
+        functools.partial(project_kernel, peers),
+        out_shape=(sds((NPROJ, blocks, lanes), f32), sds((2 * peers,), jnp.int32)),
+        in_specs=[hbm, hbm, hbm],
+        out_specs=(vmem, smem),
+        scratch_shapes=[
+            pltpu.VMEM((rows, blocks, lanes), f32),
+            pltpu.SMEM(view_basis.shape, f32),
+            pltpu.SMEM(tile_blocks.shape, jnp.int32),
+            dma((6,)),
+        ],
         compiler_params=pltpu.CompilerParams(vmem_limit_bytes=2 << 20),
         name="project",
-    )(stay(view_basis), stay(turned[0]))
+    )(stay(view_basis), stay(tile_blocks), stay(turned[0]))
+    def swapped(value, d):
+        return lax.ppermute(value, "tile", [(i, i ^ d) for i in range(peers)])
+
+    regions = lax.axis_size("region")
+    onward = lambda value: lax.ppermute(value, "region", [(i, (i + 1) % regions) for i in range(regions)])
+
+    away = {0: projected}
+    for d in range(1, peers):
+        away[d] = swapped(projected, d)
+    held, away[peers - 1] = lax.optimization_barrier((moving, away[peers - 1]))
     leaving, state = pl.pallas_call(
         pack_kernel,
         out_shape=(sds((3 * rows + 1, moves, lanes), f32), sds((3 * rows, blocks, lanes), f32)),
-        in_specs=[smem, hbm, hbm, hbm],
+        in_specs=[hbm] * 4,
         out_specs=(vmem, vmem),
-        scratch_shapes=[dma((3,))],
+        scratch_shapes=[pltpu.SMEM(moving.shape, jnp.int32), dma((3 * PIECES + 1,))],
         compiler_params=pltpu.CompilerParams(vmem_limit_bytes=4 << 20),
+        cost_estimate=pl.CostEstimate(flops=0, transcendentals=0, bytes_accessed=4 * 3 * rows * lanes * (2 * blocks + moves)),
         name="pack",
-    )(moving, *[stay(a) for a in turned])
-
-    def swapped(value, d):
-        return lax.ppermute(value, "tile", [(i, i ^ d) for i in range(peers)])
-
-    regions = lax.axis_size("region")
-    onward = lambda value: lax.ppermute(value, "region", [(i, (i + 1) % regions) for i in range(regions)])
-
-    away = {d: swapped(projected, d) for d in reversed(range(1, peers))}
+    )(stay(held), *[stay(a) for a in turned])
     came = onward(leaving)
     image, slots = pl.pallas_call(
         composite_kernel,
@@ -516,7 +542,8 @@
         ],
         compiler_params=pltpu.CompilerParams(vmem_limit_bytes=(4 * chunks + 20) * (width + 8) * lanes * 4 + (3 << 20)),
         name="composite",
-    )(meta, projected, *[away[d] for d in range(1, peers)], target.reshape(3, chunks, lanes))
+    )(meta, *[away[d] for d in reversed(range(peers))], target.reshape(3, chunks, lanes))
+    passed = onward(slots)
     mixed, slope = pl.pallas_call(
         prepare_kernel,
         out_shape=(sds((3 * rows, blocks, lanes), f32), sds((TERMS + 2, blocks, lanes), f32)),
@@ -526,9 +553,9 @@
         compiler_params=pltpu.CompilerParams(vmem_limit_bytes=5 << 20),
         name="prepare",
     )(moving, view_basis, state, came)
-    pairs = jnp.stack([slots, onward(slots)], axis=1)
+    pairs = jnp.stack([slots, passed], axis=1)
     gathered = {0: pairs[0]}
-    for d in reversed(range(1, peers)):
+    for d in range(1, peers):
         gathered[d] = swapped(pairs[d], d)
     updated = pl.pallas_call(
         update_kernel,
@@ -538,7 +565,7 @@
         scratch_shapes=[pltpu.VMEM((rows, blocks, lanes), f32)] * 3 + [dma((12,)), dma((1,))],
         compiler_params=pltpu.CompilerParams(vmem_limit_bytes=5 << 20),
         name="update",
-    )(view_basis, mixed, slope, image, *[gathered[d] for d in range(peers)])
+    )(view_basis, mixed, slope, image, *[gathered[d] for d in reversed(range(peers))])
     turned_back = [jnp.transpose(a, (1, 0, 2)) for a in updated[:3]]
     return (*turned_back, updated[3].reshape(1, 3, pixels))
 

time: 32.5 us -> 36.2 us (1.11)
  starting transfers between devices: 10.2 us -> 14.6 us
  local copies, waits for them, and re-layouts: 1.23 us -> 0.01 us
  waiting for transfers between devices: 8.94 us -> 9.65 us
    ppermute x6, starting transfers between devices: 10.1 us -> 13.9 us  [swapped(): return lax.ppermute(value, 'tile', [(i, i ^ d) for i in range(peers)])]
    ppermute x6, waiting for transfers between devices: 4.71 us -> 5.98 us  [swapped(): return lax.ppermute(value, 'tile', [(i, i ^ d) for i in range(peers)])]
    unnamed x8 -> x6, local copies, waits for them, and re-layouts: 1.23 us -> 0.01 us
    pallas_call x1, Pallas kernels: 1.03 us -> 1.61 us  [on_device(): pl.pallas_call(functools.partial(project_kernel, peers), out_shape=(sds((...]
    ppermute x2, starting transfers between devices: 0.12 us -> 0.68 us  [on_device(): lax.ppermute(value, 'region', [(i, (i + 1) % regions) for i in range(regi...]
    ppermute x2, waiting for transfers between devices: 4.23 us -> 3.67 us  [on_device(): lax.ppermute(value, 'region', [(i, (i + 1) % regions) for i in range(regi...]
    pallas_call x1, Pallas kernels: 1.76 us -> 1.26 us  [on_device(): pl.pallas_call(pack_kernel, out_shape=(sds((3 * rows + 1, moves, lanes),...]
  transfers between devices with their start and end apart: 8 -> 8, of which waited for: 3 -> 7; matrix products, arithmetic and copies ran while one was open for 1% -> 0% of each run, Pallas kernels for 26% -> 18%
where the time goes in v4:
time: 36.2 us; the launch traced here: 36 us
  starting transfers between devices  14.6 us (40%)
  Pallas kernels  11 us (30%)
  waiting for transfers between devices  9.65 us (27%)
  between operations  0.67 us (2%)
    ppermute x6, starting transfers between devices, swapped(): return lax.ppermute(value, 'tile', [(i, i ^ d) for i in range(peers)])  13.9 us
    ppermute x6, waiting for transfers between devices, swapped(): return lax.ppermute(value, 'tile', [(i, i ^ d) for i in range(peers)])  5.98 us
    pallas_call x1, Pallas kernels, on_device(): pl.pallas_call(composite_kernel, out_shape=(sds((3, chunks, lanes), f32),...  5.76 us
    ppermute x2, waiting for transfers between devices, on_device(): lax.ppermute(value, 'region', [(i, (i + 1) % regions) for i in range(regi...  3.67 us
    pallas_call x1, Pallas kernels, on_device(): pl.pallas_call(functools.partial(project_kernel, peers), out_shape=(sds((...  1.61 us
    pallas_call x1, Pallas kernels, on_device(): pl.pallas_call(update_kernel, out_shape=(sds((rows, blocks, lanes), f32),...  1.56 us
    pallas_call x1, Pallas kernels, on_device(): pl.pallas_call(pack_kernel, out_shape=(sds((3 * rows + 1, moves, lanes),...  1.26 us
    pallas_call x1, Pallas kernels, on_device(): pl.pallas_call(prepare_kernel, out_shape=(sds((3 * rows, blocks, lanes),...  0.83 us
  transfers between devices with their start and end apart: 8, of which 7 were waited for; matrix products, arithmetic and copies ran while one was open for 0% of the time, Pallas kernels for 18%

profile of v4, /device:TPU:0, one launch (start us, length us, event | category | flops | bytes accessed | tf_op | source)
XLA Modules:
  0.0 36.0 jit_solution(5535521783531311609)
XLA Ops:
  0.6 1.6 %project.1 = (f32[9,8,128]{2,1,0:T(8,128)S(1)}, s32[8]{0:T(128)S(1)}) custom-call(f32[16]{0:T(128)} %basis_ref.3, s32[1,4]{1,0:T(1,128)} %listed_hbm.1, f32[59,8,128]{2,1,0:T(8,128)} %bitcast.20), custom_call_target="tpu_custom_call" | custom-call | tf_op jit(solution)/shard_map/project/pallas_call | solution.py:490
  2.2 5.1 %collective-permute-start = (f32[9,8,128]{2,1,0:T(8,128)S(1)}, f32[9,8,128]{2,1,0:T(8,128)S(1)}, u32[]{:S(2)}, u32[]{:S(2)}) collective-permute-start(f32[9,8,128]{2,1,0:T(8,128)S(1)} %get-tuple-element.18.refs_3_), channel_id=1, source_target_pairs={{0,3},{1,2},{2,1},{3,0},{4,7},{5,6},{6,5},{7,4},{8,11},{9,10},{10,... | collective-permute-start | bytes 110600 | tf_op jit(solution)/shard_map/ppermute | solution.py:505
  7.4 1.9 %collective-permute-done.refs_0_ = f32[9,8,128]{2,1,0:T(8,128)S(1)} collective-permute-done((f32[9,8,128]{2,1,0:T(8,128)S(1)}, f32[9,8,128]{2,1,0:T(8,128)S(1)}, u32[]{:S(2)}, u32[]{:S(2)}) %collective-permute-start) | collective-permute-done | bytes 36896 | tf_op jit(solution)/shard_map/ppermute | solution.py:505
  9.3 1.3 %pack.1 = (f32[178,4,128]{2,1,0:T(4,128)S(1)}, f32[177,8,128]{2,1,0:T(8,128)S(1)}) custom-call(s32[1,4]{1,0:T(1,128)} %moving_ref.1, f32[59,8,128]{2,1,0:T(8,128)} %bitcast.21, f32[59,8,128]{2,1,0:T(8,128)} %bitcast.22, f32[59,8,128]{2,1,0:T(8,128)} %bitcast.23), custom_call_target="tpu_custom_call" | custom-call | bytes 1812480 | tf_op jit(solution)/shard_map/pack/pallas_call | solution.py:514
  10.6 0.1 collective-permute-start.1
  10.6 1.1 %collective-permute-start.2 = (f32[9,8,128]{2,1,0:T(8,128)S(1)}, f32[9,8,128]{2,1,0:T(8,128)S(1)}, u32[]{:S(2)}, u32[]{:S(2)}) collective-permute-start(f32[9,8,128]{2,1,0:T(8,128)S(1)} %get-tuple-element.18.refs_3_), channel_id=1, source_target_pairs={{0,2},{1,3},{2,0},{3,1},{4,6},{5,7},{6,4},{7,5},{8,10},{9,11},{10,... | collective-permute-start | bytes 110600 | tf_op jit(solution)/shard_map/ppermute | solution.py:505
  11.7 3.4 %collective-permute-start.3 = (f32[9,8,128]{2,1,0:T(8,128)S(1)}, f32[9,8,128]{2,1,0:T(8,128)S(1)}, u32[]{:S(2)}, u32[]{:S(2)}) collective-permute-start(f32[9,8,128]{2,1,0:T(8,128)S(1)} %get-tuple-element.18.refs_3_), channel_id=1, source_target_pairs={{0,1},{1,0},{2,3},{3,2},{4,5},{5,4},{6,7},{7,6},{8,9},{9,8},{10,11... | collective-permute-start | bytes 110600 | tf_op jit(solution)/shard_map/ppermute | solution.py:505
  15.1 0.5 %collective-permute-done.2.refs_1_ = f32[9,8,128]{2,1,0:T(8,128)S(1)} collective-permute-done((f32[9,8,128]{2,1,0:T(8,128)S(1)}, f32[9,8,128]{2,1,0:T(8,128)S(1)}, u32[]{:S(2)}, u32[]{:S(2)}) %collective-permute-start.2) | collective-permute-done | bytes 36896 | tf_op jit(solution)/shard_map/ppermute | solution.py:505
  15.6 1.6 %collective-permute-done.3.refs_2_ = f32[9,8,128]{2,1,0:T(8,128)S(1)} collective-permute-done((f32[9,8,128]{2,1,0:T(8,128)S(1)}, f32[9,8,128]{2,1,0:T(8,128)S(1)}, u32[]{:S(2)}, u32[]{:S(2)}) %collective-permute-start.3) | collective-permute-done | bytes 36896 | tf_op jit(solution)/shard_map/ppermute | solution.py:505
  17.1 0.0 copy-done
  17.1 5.8 %composite.1 = (f32[3,8,128]{2,1,0:T(8,128)S(1)}, f32[4,16,128]{2,1,0:T(8,128)S(1)}) custom-call(s32[8]{0:T(128)S(1)} %get-tuple-element.24.meta_ref, f32[9,8,128]{2,1,0:T(8,128)S(1)} %collective-permute-done.refs_0_, f32[9,8,128]{2,1,0:T(8,128)S(1)} %collective-permute-done.2.refs_1_, f32[9,8,128]{2,1,0:T(8,128)S(1)} %collective-permute-done.3.refs_2_, ...), custom_call_target="tpu_custom_call" | custom-call | tf_op jit(solution)/shard_map/composite/pallas_call | solution.py:525
  22.9 0.6 %collective-permute-start.4 = (f32[4,16,128]{2,1,0:T(8,128)S(1)}, f32[4,16,128]{2,1,0:T(8,128)S(1)}, u32[]{:S(2)}, u32[]{:S(2)}) collective-permute-start(f32[4,16,128]{2,1,0:T(8,128)S(1)} %get-tuple-element.27), channel_id=1, source_target_pairs={{0,4},{4,8},{8,12},{12,16},{16,20},{20,24},{24,28},{28,0},{1,5},{5... | collective-permute-start | bytes 98312 | tf_op jit(solution)/shard_map/ppermute | solution.py:508
  23.5 3.7 %collective-permute-done.4 = f32[4,16,128]{2,1,0:T(8,128)S(1)} collective-permute-done((f32[4,16,128]{2,1,0:T(8,128)S(1)}, f32[4,16,128]{2,1,0:T(8,128)S(1)}, u32[]{:S(2)}, u32[]{:S(2)}) %collective-permute-start.4) | collective-permute-done | bytes 32800 | tf_op jit(solution)/shard_map/ppermute | solution.py:508
  27.2 2.3 %collective-permute-start.5 = (f32[2,16,128]{2,1,0:T(8,128)S(1)}, f32[2,16,128]{2,1,0:T(8,128)S(1)}, u32[]{:S(2)}, u32[]{:S(2)}) collective-permute-start(f32[2,16,128]{2,1,0:T(8,128)S(1)} %get-tuple-element.41), channel_id=1, source_target_pairs={{0,3},{1,2},{2,1},{3,0},{4,7},{5,6},{6,5},{7,4},{8,11},{9,10},{10,... | collective-permute-start | bytes 49160 | tf_op jit(solution)/shard_map/ppermute | solution.py:505
  29.5 1.2 %collective-permute-start.6 = (f32[2,16,128]{2,1,0:T(8,128)S(1)}, f32[2,16,128]{2,1,0:T(8,128)S(1)}, u32[]{:S(2)}, u32[]{:S(2)}) collective-permute-start(f32[2,16,128]{2,1,0:T(8,128)S(1)} %get-tuple-element.42), channel_id=1, source_target_pairs={{0,2},{1,3},{2,0},{3,1},{4,6},{5,7},{6,4},{7,5},{8,10},{9,11},{10,... | collective-permute-start | bytes 49160 | tf_op jit(solution)/shard_map/ppermute | solution.py:505
  30.7 0.9 %collective-permute-start.7 = (f32[2,16,128]{2,1,0:T(8,128)S(1)}, f32[2,16,128]{2,1,0:T(8,128)S(1)}, u32[]{:S(2)}, u32[]{:S(2)}) collective-permute-start(f32[2,16,128]{2,1,0:T(8,128)S(1)} %get-tuple-element.43), channel_id=1, source_target_pairs={{0,1},{1,0},{2,3},{3,2},{4,5},{5,4},{6,7},{7,6},{8,9},{9,8},{10,11... | collective-permute-start | bytes 49160 | tf_op jit(solution)/shard_map/ppermute | solution.py:505
  31.6 0.0 collective-permute-done.1.came_ref
  31.6 0.0 copy-done.1
  31.6 0.0 copy-done.2
  31.6 0.8 %prepare.1 = (f32[177,8,128]{2,1,0:T(8,128)S(1)}, f32[32,8,128]{2,1,0:T(8,128)S(1)}) custom-call(s32[1,4]{1,0:T(1,128)S(1)} %copy-done.2, f32[16]{0:T(128)S(1)} %copy-done.1, f32[177,8,128]{2,1,0:T(8,128)S(1)} %get-tuple-element.20.state_ref, f32[178,4,128]{2,1,0:T(4,128)S(1)} %collective-permute-done.1.came_ref), custom_call_target="tpu_custom_call" | custom-call | tf_op jit(solution)/shard_map/prepare/pallas_call | solution.py:547
  32.4 0.3 collective-permute-done.5.refs_0_
  32.7 1.4 %collective-permute-done.6.refs_1_ = f32[2,16,128]{2,1,0:T(8,128)S(1)} collective-permute-done((f32[2,16,128]{2,1,0:T(8,128)S(1)}, f32[2,16,128]{2,1,0:T(8,128)S(1)}, u32[]{:S(2)}, u32[]{:S(2)}) %collective-permute-start.6) | collective-permute-done | bytes 16416 | tf_op jit(solution)/shard_map/ppermute | solution.py:505
  34.1 0.3 collective-permute-done.7.refs_2_
  34.4 1.6 %update.1 = (f32[59,8,128]{2,1,0:T(8,128)}, f32[59,8,128]{2,1,0:T(8,128)}, f32[59,8,128]{2,1,0:T(8,128)}, f32[3,8,128]{2,1,0:T(8,128)}) custom-call(f32[16]{0:T(128)S(1)} %copy-done.1, f32[177,8,128]{2,1,0:T(8,128)S(1)} %get-tuple-element.22.mixed_ref, f32[32,8,128]{2,1,0:T(8,128)S(1)} %get-tuple-element.23.slope_ref, ...), custom_call_target="tpu_custom_call" | custom-call | tf_op jit(solution)/shard_map/update/pallas_call | solution.py:560
  (4 shorter events, 0.0 us)
Async XLA Ops:
  2.2 7.1 %collective-permute-start = (f32[9,8,128]{2,1,0:T(8,128)S(1)}, f32[9,8,128]{2,1,0:T(8,128)S(1)}, u32[]{:S(2)}, u32[]{:S(2)}) collective-permute-start(f32[9,8,128]{2,1,0:T(8,128)S(1)} %get-tuple-element.18.refs_3_), channel_id=1, source_target_pairs={{0,3},{1,2},{2,1},{3,0},{4,7},{5,6},{6,5},{7,4},{8,11},{9,10},{10,... | collective-permute-start | bytes 110600 | tf_op jit(solution)/shard_map/ppermute | solution.py:505
  9.3 7.8 %copy-start = (f32[1,3,1024]{2,0,1:T(1,128)S(1)}, f32[1,3,1024]{2,0,1:T(1,128)}, u32[]{:S(2)}) copy-start(f32[1,3,1024]{2,0,1:T(1,128)} %param.11) | copy-start | bytes 36868
  10.6 21.0 %collective-permute-start.1 = (f32[178,4,128]{2,1,0:T(4,128)S(1)}, f32[178,4,128]{2,1,0:T(4,128)S(1)}, u32[]{:S(2)}, u32[]{:S(2)}) collective-permute-start(f32[178,4,128]{2,1,0:T(4,128)S(1)} %get-tuple-element.21), channel_id=1, source_target_pairs={{0,4},{4,8},{8,12},{12,16},{16,20},{20,24},{24,28},{28,0},{1,5},{5... | collective-permute-start | bytes 1093640 | tf_op jit(solution)/shard_map/ppermute | solution.py:508
  10.6 4.9 %collective-permute-start.2 = (f32[9,8,128]{2,1,0:T(8,128)S(1)}, f32[9,8,128]{2,1,0:T(8,128)S(1)}, u32[]{:S(2)}, u32[]{:S(2)}) collective-permute-start(f32[9,8,128]{2,1,0:T(8,128)S(1)} %get-tuple-element.18.refs_3_), channel_id=1, source_target_pairs={{0,2},{1,3},{2,0},{3,1},{4,6},{5,7},{6,4},{7,5},{8,10},{9,11},{10,... | collective-permute-start | bytes 110600 | tf_op jit(solution)/shard_map/ppermute | solution.py:505
  11.7 5.4 %collective-permute-start.3 = (f32[9,8,128]{2,1,0:T(8,128)S(1)}, f32[9,8,128]{2,1,0:T(8,128)S(1)}, u32[]{:S(2)}, u32[]{:S(2)}) collective-permute-start(f32[9,8,128]{2,1,0:T(8,128)S(1)} %get-tuple-element.18.refs_3_), channel_id=1, source_target_pairs={{0,1},{1,0},{2,3},{3,2},{4,5},{5,4},{6,7},{7,6},{8,9},{9,8},{10,11... | collective-permute-start | bytes 110600 | tf_op jit(solution)/shard_map/ppermute | solution.py:505
  22.9 4.3 %collective-permute-start.4 = (f32[4,16,128]{2,1,0:T(8,128)S(1)}, f32[4,16,128]{2,1,0:T(8,128)S(1)}, u32[]{:S(2)}, u32[]{:S(2)}) collective-permute-start(f32[4,16,128]{2,1,0:T(8,128)S(1)} %get-tuple-element.27), channel_id=1, source_target_pairs={{0,4},{4,8},{8,12},{12,16},{16,20},{20,24},{24,28},{28,0},{1,5},{5... | collective-permute-start | bytes 98312 | tf_op jit(solution)/shard_map/ppermute | solution.py:508
  27.2 5.5 %collective-permute-start.5 = (f32[2,16,128]{2,1,0:T(8,128)S(1)}, f32[2,16,128]{2,1,0:T(8,128)S(1)}, u32[]{:S(2)}, u32[]{:S(2)}) collective-permute-start(f32[2,16,128]{2,1,0:T(8,128)S(1)} %get-tuple-element.41), channel_id=1, source_target_pairs={{0,3},{1,2},{2,1},{3,0},{4,7},{5,6},{6,5},{7,4},{8,11},{9,10},{10,... | collective-permute-start | bytes 49160 | tf_op jit(solution)/shard_map/ppermute | solution.py:505
  29.5 4.6 %collective-permute-start.6 = (f32[2,16,128]{2,1,0:T(8,128)S(1)}, f32[2,16,128]{2,1,0:T(8,128)S(1)}, u32[]{:S(2)}, u32[]{:S(2)}) collective-permute-start(f32[2,16,128]{2,1,0:T(8,128)S(1)} %get-tuple-element.42), channel_id=1, source_target_pairs={{0,2},{1,3},{2,0},{3,1},{4,6},{5,7},{6,4},{7,5},{8,10},{9,11},{10,... | collective-permute-start | bytes 49160 | tf_op jit(solution)/shard_map/ppermute | solution.py:505
  30.7 0.9 %copy-start.1 = (f32[16]{0:T(128)S(1)}, f32[16]{0:T(128)}, u32[]{:S(2)}) copy-start(f32[16]{0:T(128)} %basis_ref.3) | copy-start | bytes 196
  30.7 0.9 %copy-start.2 = (s32[1,4]{1,0:T(1,128)S(1)}, s32[1,4]{1,0:T(1,128)}, u32[]{:S(2)}) copy-start(s32[1,4]{1,0:T(1,128)} %moving_ref.1) | copy-start | bytes 52
  30.7 3.7 %collective-permute-start.7 = (f32[2,16,128]{2,1,0:T(8,128)S(1)}, f32[2,16,128]{2,1,0:T(8,128)S(1)}, u32[]{:S(2)}, u32[]{:S(2)}) collective-permute-start(f32[2,16,128]{2,1,0:T(8,128)S(1)} %get-tuple-element.43), channel_id=1, source_target_pairs={{0,1},{1,0},{2,3},{3,2},{4,5},{5,4},{6,7},{7,6},{8,9},{9,8},{10,11... | collective-permute-start | bytes 49160 | tf_op jit(solution)/shard_map/ppermute | solution.py:505

commit v5 on v4

--- a/solution.py
+++ b/solution.py
@@ -79,17 +79,15 @@
     return sigmoid(total)
 
 
-def project_kernel(peers, basis_hbm, listed_hbm, p_hbm, proj_ref, meta_ref, p_ref, basis_ref, listed_ref, sems):
+def project_kernel(basis_hbm, p_hbm, proj_ref, p_ref, basis_ref, sems):
     head = 11
-    blocks = p_ref.shape[1]
     copies = [
         pltpu.make_async_copy(p_hbm.at[:head], p_ref.at[:head], sems.at[0]),
         pltpu.make_async_copy(basis_hbm, basis_ref, sems.at[1]),
-        pltpu.make_async_copy(listed_hbm, listed_ref, sems.at[2]),
     ]
     for c in range(3):
         span = pl.ds(head + SH * c, SH)
-        copies.append(pltpu.make_async_copy(p_hbm.at[span], p_ref.at[span], sems.at[3 + c]))
+        copies.append(pltpu.make_async_copy(p_hbm.at[span], p_ref.at[span], sems.at[2 + c]))
     for copy in copies:
         copy.start()
     p = lambda i: p_ref[i]
@@ -101,16 +99,9 @@
     proj_ref[3] = v["B"]
     proj_ref[4] = v["C"]
     proj_ref[5] = 0.99 * v["so"]
-    copies[2].wait()
-    me = lax.axis_index("tile")
-    for n in range(listed_ref.shape[1]):
-        listed = listed_ref[0, n]
-        distance = jnp.bitwise_xor(listed // blocks, me)
-        meta_ref[distance] = n
-        meta_ref[peers + distance] = listed % blocks
     copies[1].wait()
     for c in range(3):
-        copies[3 + c].wait()
+        copies[2 + c].wait()
         proj_ref[6 + c] = colour(p, c, lambda k: basis_ref[k])
 
 
@@ -133,11 +124,13 @@
     return list(zip(cuts[:-1], cuts[1:]))
 
 
-def pack_kernel(moving_hbm, p_hbm, f_hbm, s_hbm, leave_ref, state_ref, moving_ref, sems):
+def pack_kernel(moving_hbm, listed_hbm, p_hbm, f_hbm, s_hbm, leave_ref, state_ref, moving_ref, listed_ref, sems):
     total, moves, lanes = leave_ref.shape
     rows, blocks, _ = p_hbm.shape
     ids = pltpu.make_async_copy(moving_hbm, moving_ref, sems.at[3 * PIECES])
     ids.start()
+    lists = pltpu.make_async_copy(listed_hbm, listed_ref, sems.at[3 * PIECES + 1])
+    lists.start()
     spans = []
     copies = []
     for a, ref in enumerate((p_hbm, f_hbm, s_hbm)):
@@ -148,6 +141,7 @@
             spans.append(span)
             copies.append(copy)
     ids.wait()
+    lists.wait()
     slot = lax.broadcasted_iota(jnp.int32, (blocks, lanes), 0)
     pick = jnp.zeros((blocks, lanes), jnp.int32)
     for m in range(moves):
@@ -166,8 +160,7 @@
     return high, middle, rest - middle
 
 
-def composite_kernel(meta_ref, *refs):
-    peers = meta_ref.shape[0] // 2
+def composite_kernel(peers, listed_ref, *refs):
     sources = refs[:peers][::-1]
     target_ref = refs[peers]
     image_ref = refs[peers + 1]
@@ -179,9 +172,18 @@
     chunks = errbuf.shape[0] // 8
     spreads = qbuf.shape[0]
     assert chunks == 8
+    blocks = sources[0].shape[1]
+    me = lax.axis_index("tile")
+    places, ids = [], []
     for d in range(peers):
-        pos = meta_ref[d]
-        loc = meta_ref[peers + d]
+        pos, loc = jnp.int32(0), jnp.int32(0)
+        for n in range(listed):
+            named = listed_ref[0, n]
+            here = lax.div(named, jnp.int32(blocks)) == jnp.bitwise_xor(me, d)
+            pos = jnp.where(here, n, pos)
+            loc = jnp.where(here, lax.rem(named, jnp.int32(blocks)), loc)
+        places.append(pos)
+        ids.append(loc)
         for r in range(NPROJ):
             pbuf[pos, pl.ds(r, 1), :] = sources[d][r, pl.ds(loc, 1), :]
 
@@ -346,8 +348,8 @@
 
     lax.fori_loop(0, listed, finish, 0, unroll=min(listed, 4))
     for d in range(peers):
-        slots_ref[d] = gbuf[meta_ref[d]]
-        slots_ref[d, NPROJ : NPROJ + 1, :] = jnp.full((1, lanes), 1, jnp.float32) * meta_ref[peers + d].astype(jnp.float32)
+        slots_ref[d] = gbuf[places[d]]
+        slots_ref[d, NPROJ : NPROJ + 1, :] = jnp.full((1, lanes), 1, jnp.float32) * ids[d].astype(jnp.float32)
 
 
 TERMS = 2 + 3 * 8 + 1 + 3
@@ -487,43 +489,45 @@
     stay = lambda value: pltpu.with_memory_space_constraint(value, pltpu.HBM)
     dma = pltpu.SemaphoreType.DMA
     turned = [jnp.transpose(a, (1, 0, 2)) for a in (params, first_moment, second_moment)]
-    projected, meta = pl.pallas_call(
-        functools.partial(project_kernel, peers),
-        out_shape=(sds((NPROJ, blocks, lanes), f32), sds((2 * peers,), jnp.int32)),
-        in_specs=[hbm, hbm, hbm],
-        out_specs=(vmem, smem),
-        scratch_shapes=[
-            pltpu.VMEM((rows, blocks, lanes), f32),
-            pltpu.SMEM(view_basis.shape, f32),
-            pltpu.SMEM(tile_blocks.shape, jnp.int32),
-            dma((6,)),
-        ],
+    projected = pl.pallas_call(
+        project_kernel,
+        out_shape=sds((NPROJ, blocks, lanes), f32),
+        in_specs=[hbm, hbm],
+        out_specs=vmem,
+        scratch_shapes=[pltpu.VMEM((rows, blocks, lanes), f32), pltpu.SMEM(view_basis.shape, f32), dma((5,))],
         compiler_params=pltpu.CompilerParams(vmem_limit_bytes=2 << 20),
         name="project",
-    )(stay(view_basis), stay(tile_blocks), stay(turned[0]))
+    )(stay(view_basis), stay(turned[0]))
+
     def swapped(value, d):
         return lax.ppermute(value, "tile", [(i, i ^ d) for i in range(peers)])
 
     regions = lax.axis_size("region")
     onward = lambda value: lax.ppermute(value, "region", [(i, (i + 1) % regions) for i in range(regions)])
 
+    leaving, state, moved, named = pl.pallas_call(
+        pack_kernel,
+        out_shape=(
+            sds((3 * rows + 1, moves, lanes), f32),
+            sds((3 * rows, blocks, lanes), f32),
+            sds(moving.shape, jnp.int32),
+            sds(tile_blocks.shape, jnp.int32),
+        ),
+        in_specs=[hbm] * 5,
+        out_specs=(vmem, vmem, smem, smem),
+        scratch_shapes=[dma((3 * PIECES + 2,))],
+        compiler_params=pltpu.CompilerParams(vmem_limit_bytes=4 << 20),
+        name="pack",
+    )(stay(moving), stay(tile_blocks), *[stay(a) for a in turned])
     away = {0: projected}
     for d in range(1, peers):
         away[d] = swapped(projected, d)
-    held, away[peers - 1] = lax.optimization_barrier((moving, away[peers - 1]))
-    leaving, state = pl.pallas_call(
-        pack_kernel,
-        out_shape=(sds((3 * rows + 1, moves, lanes), f32), sds((3 * rows, blocks, lanes), f32)),
-        in_specs=[hbm] * 4,
-        out_specs=(vmem, vmem),
-        scratch_shapes=[pltpu.SMEM(moving.shape, jnp.int32), dma((3 * PIECES + 1,))],
-        compiler_params=pltpu.CompilerParams(vmem_limit_bytes=4 << 20),
-        cost_estimate=pl.CostEstimate(flops=0, transcendentals=0, bytes_accessed=4 * 3 * rows * lanes * (2 * blocks + moves)),
-        name="pack",
-    )(stay(held), *[stay(a) for a in turned])
+    leaving, *rest = lax.optimization_barrier((leaving, *[away[d] for d in range(1, peers)]))
+    for d in range(1, peers):
+        away[d] = rest[d - 1]
     came = onward(leaving)
     image, slots = pl.pallas_call(
-        composite_kernel,
+        functools.partial(composite_kernel, peers),
         out_shape=(sds((3, chunks, lanes), f32), sds((peers, GRADS, lanes), f32)),
         in_specs=[smem] + [vmem] * (peers + 1),
         out_specs=(vmem, vmem),
@@ -541,8 +545,11 @@
             pltpu.VMEM((width, 48), jnp.bfloat16),
         ],
         compiler_params=pltpu.CompilerParams(vmem_limit_bytes=(4 * chunks + 20) * (width + 8) * lanes * 4 + (3 << 20)),
+        cost_estimate=pl.CostEstimate(
+            flops=64 * width * pixels, transcendentals=width * pixels, bytes_accessed=48 * width * pixels
+        ),
         name="composite",
-    )(meta, *[away[d] for d in reversed(range(peers))], target.reshape(3, chunks, lanes))
+    )(named, *[away[d] for d in reversed(range(peers))], target.reshape(3, chunks, lanes))
     passed = onward(slots)
     mixed, slope = pl.pallas_call(
         prepare_kernel,
@@ -552,7 +559,7 @@
         scratch_shapes=[pltpu.VMEM((8, blocks, lanes), f32)],
         compiler_params=pltpu.CompilerParams(vmem_limit_bytes=5 << 20),
         name="prepare",
-    )(moving, view_basis, state, came)
+    )(moved, view_basis, state, came)
     pairs = jnp.stack([slots, passed], axis=1)
     gathered = {0: pairs[0]}
     for d in range(1, peers):

time: 36.2 us -> 29.8 us (0.82)
  waiting for transfers between devices: 9.65 us -> 5.39 us
  starting transfers between devices: 14.6 us -> 11.8 us
  local copies, waits for them, and re-layouts: 0.01 us -> 0.66 us
    ppermute x6, starting transfers between devices: 13.9 us -> 10.1 us  [swapped(): return lax.ppermute(value, 'tile', [(i, i ^ d) for i in range(peers)])]
    ppermute x6, waiting for transfers between devices: 5.98 us -> 2.74 us  [swapped(): return lax.ppermute(value, 'tile', [(i, i ^ d) for i in range(peers)])]
    ppermute x2, waiting for transfers between devices: 3.67 us -> 2.65 us  [on_device(): lax.ppermute(value, 'region', [(i, (i + 1) % regions) for i in range(regi...]
    ppermute x2, starting transfers between devices: 0.68 us -> 1.64 us  [on_device(): lax.ppermute(value, 'region', [(i, (i + 1) % regions) for i in range(regi...]
    unnamed x6 -> x4, local copies, waits for them, and re-layouts: 0.01 us -> 0.66 us
    pallas_call x1, Pallas kernels: 1.26 us -> 1.86 us  [on_device(): pl.pallas_call(pack_kernel, out_shape=(sds((3 * rows + 1, moves, lanes),...]
    pallas_call x2, Pallas kernels: 7.37 us -> 6.81 us  [the longest x1 5.78 us: on_device(): pl.pallas_call(functools.partial(composite_kernel, peers), out_shape=(sds...]
  transfers between devices with their start and end apart: 8 -> 8, of which waited for: 7 -> 3; matrix products, arithmetic and copies ran while one was open for 0% -> 0% of each run, Pallas kernels for 18% -> 29%
where the time goes in v5:
time: 29.8 us; the launch traced here: 29.6 us
  starting transfers between devices  11.8 us (40%)
  Pallas kernels  11.1 us (37%)
  waiting for transfers between devices  5.39 us (18%)
  between operations  0.68 us (2%)
  local copies, waits for them, and re-layouts  0.66 us (2%)
    ppermute x6, starting transfers between devices, swapped(): return lax.ppermute(value, 'tile', [(i, i ^ d) for i in range(peers)])  10.1 us
    pallas_call x1, Pallas kernels, on_device(): pl.pallas_call(functools.partial(composite_kernel, peers), out_shape=(sds...  5.78 us
    ppermute x6, waiting for transfers between devices, swapped(): return lax.ppermute(value, 'tile', [(i, i ^ d) for i in range(peers)])  2.74 us
    ppermute x2, waiting for transfers between devices, on_device(): lax.ppermute(value, 'region', [(i, (i + 1) % regions) for i in range(regi...  2.65 us
    pallas_call x1, Pallas kernels, on_device(): pl.pallas_call(pack_kernel, out_shape=(sds((3 * rows + 1, moves, lanes),...  1.86 us
    ppermute x2, starting transfers between devices, on_device(): lax.ppermute(value, 'region', [(i, (i + 1) % regions) for i in range(regi...  1.64 us
    pallas_call x1, Pallas kernels, on_device(): pl.pallas_call(update_kernel, out_shape=(sds((rows, blocks, lanes), f32),...  1.56 us
    pallas_call x1, Pallas kernels, on_device(): pl.pallas_call(project_kernel, out_shape=sds((NPROJ, blocks, lanes), f32)...  1.02 us
  transfers between devices with their start and end apart: 8, of which 3 were waited for; matrix products, arithmetic and copies ran while one was open for 0% of the time, Pallas kernels for 29%

profile of v5, /device:TPU:0, one launch (start us, length us, event | category | flops | bytes accessed | tf_op | source)
XLA Modules:
  0.0 29.6 jit_solution(13705676730328401299)
XLA Ops:
  0.6 1.0 %project.1.refs_3_ = f32[9,8,128]{2,1,0:T(8,128)S(1)} custom-call(f32[16]{0:T(128)} %basis_ref.3, f32[59,8,128]{2,1,0:T(8,128)} %bitcast.20), custom_call_target="tpu_custom_call" | custom-call | tf_op jit(solution)/shard_map/project/pallas_call | solution.py:492
  1.7 5.1 %collective-permute-start.2 = (f32[9,8,128]{2,1,0:T(8,128)S(1)}, f32[9,8,128]{2,1,0:T(8,128)S(1)}, u32[]{:S(2)}, u32[]{:S(2)}) collective-permute-start(f32[9,8,128]{2,1,0:T(8,128)S(1)} %project.1.refs_3_), channel_id=1, source_target_pairs={{0,3},{1,2},{2,1},{3,0},{4,7},{5,6},{6,5},{7,4},{8,11},{9,10},{10,... | collective-permute-start | bytes 110600 | tf_op jit(solution)/shard_map/ppermute | solution.py:503
  6.8 0.0 collective-permute-start.1
  6.8 0.6 %collective-permute-start = (f32[9,8,128]{2,1,0:T(8,128)S(1)}, f32[9,8,128]{2,1,0:T(8,128)S(1)}, u32[]{:S(2)}, u32[]{:S(2)}) collective-permute-start(f32[9,8,128]{2,1,0:T(8,128)S(1)} %project.1.refs_3_), channel_id=1, source_target_pairs={{0,1},{1,0},{2,3},{3,2},{4,5},{5,4},{6,7},{7,6},{8,9},{9,8},{10,11... | collective-permute-start | bytes 110600 | tf_op jit(solution)/shard_map/ppermute | solution.py:503
  7.4 0.0 copy-start.1
  7.4 1.9 %pack.1 = (f32[178,4,128]{2,1,0:T(4,128)S(1)}, f32[177,8,128]{2,1,0:T(8,128)S(1)}, s32[1,4]{1,0:T(1,128)S(1)}, s32[1,4]{1,0:T(1,128)S(1)}) custom-call(s32[1,4]{1,0:T(1,128)} %moving_hbm.1, s32[1,4]{1,0:T(1,128)} %listed_hbm.1, f32[59,8,128]{2,1,0:T(8,128)} %bitcast.21, f32[59,8,128]{2,1,0:T(8,128)} %bitcast.22, f32[59,8,128]{2,1,0:T(8,128)} %bitcast.23), custom_call_target="tpu_custom_call" | custom-call | tf_op jit(solution)/shard_map/pack/pallas_call | solution.py:508
  9.3 0.0 collective-permute-done.2.refs_0_
  9.3 2.3 %collective-permute-done.1.refs_1_ = f32[9,8,128]{2,1,0:T(8,128)S(1)} collective-permute-done((f32[9,8,128]{2,1,0:T(8,128)S(1)}, f32[9,8,128]{2,1,0:T(8,128)S(1)}, u32[]{:S(2)}, u32[]{:S(2)}) %collective-permute-start.1) | collective-permute-done | bytes 36896 | tf_op jit(solution)/shard_map/ppermute | solution.py:503
  11.6 0.0 collective-permute-done.refs_2_
  11.6 0.0 collective-permute-start.3
  11.6 0.0 copy-done.1
  11.6 5.8 %composite.1 = (f32[3,8,128]{2,1,0:T(8,128)S(1)}, f32[4,16,128]{2,1,0:T(8,128)S(1)}) custom-call(s32[1,4]{1,0:T(1,128)S(1)} %get-tuple-element.26.listed_ref, f32[9,8,128]{2,1,0:T(8,128)S(1)} %collective-permute-done.2.refs_0_, f32[9,8,128]{2,1,0:T(8,128)S(1)} %collective-permute-done.1.refs_1_, f32[9,8,128]{2,1,0:T(8,128)S(1)} %collective-permute-done.refs_2_, ...), custom_call_target="tpu_custom_call" | custom-call | flops 33554432 | bytes 25165824 | tf_op jit(solution)/shard_map/composite/pallas_call | solution.py:529
  17.4 1.6 %collective-permute-start.4 = (f32[4,16,128]{2,1,0:T(8,128)S(1)}, f32[4,16,128]{2,1,0:T(8,128)S(1)}, u32[]{:S(2)}, u32[]{:S(2)}) collective-permute-start(f32[4,16,128]{2,1,0:T(8,128)S(1)} %get-tuple-element.31), channel_id=1, source_target_pairs={{0,4},{4,8},{8,12},{12,16},{16,20},{20,24},{24,28},{28,0},{1,5},{5... | collective-permute-start | bytes 98312 | tf_op jit(solution)/shard_map/ppermute | solution.py:506
  19.1 2.7 %collective-permute-done.4 = f32[4,16,128]{2,1,0:T(8,128)S(1)} collective-permute-done((f32[4,16,128]{2,1,0:T(8,128)S(1)}, f32[4,16,128]{2,1,0:T(8,128)S(1)}, u32[]{:S(2)}, u32[]{:S(2)}) %collective-permute-start.4) | collective-permute-done | bytes 32800 | tf_op jit(solution)/shard_map/ppermute | solution.py:506
  21.7 1.5 %collective-permute-start.5 = (f32[2,16,128]{2,1,0:T(8,128)S(1)}, f32[2,16,128]{2,1,0:T(8,128)S(1)}, u32[]{:S(2)}, u32[]{:S(2)}) collective-permute-start(f32[2,16,128]{2,1,0:T(8,128)S(1)} %get-tuple-element.45), channel_id=1, source_target_pairs={{0,3},{1,2},{2,1},{3,0},{4,7},{5,6},{6,5},{7,4},{8,11},{9,10},{10,... | collective-permute-start | bytes 49160 | tf_op jit(solution)/shard_map/ppermute | solution.py:503
  23.2 0.6 %collective-permute-start.6 = (f32[2,16,128]{2,1,0:T(8,128)S(1)}, f32[2,16,128]{2,1,0:T(8,128)S(1)}, u32[]{:S(2)}, u32[]{:S(2)}) collective-permute-start(f32[2,16,128]{2,1,0:T(8,128)S(1)} %get-tuple-element.46), channel_id=1, source_target_pairs={{0,2},{1,3},{2,0},{3,1},{4,6},{5,7},{6,4},{7,5},{8,10},{9,11},{10,... | collective-permute-start | bytes 49160 | tf_op jit(solution)/shard_map/ppermute | solution.py:503
  23.8 2.3 %collective-permute-start.7 = (f32[2,16,128]{2,1,0:T(8,128)S(1)}, f32[2,16,128]{2,1,0:T(8,128)S(1)}, u32[]{:S(2)}, u32[]{:S(2)}) collective-permute-start(f32[2,16,128]{2,1,0:T(8,128)S(1)} %get-tuple-element.47), channel_id=1, source_target_pairs={{0,1},{1,0},{2,3},{3,2},{4,5},{5,4},{6,7},{7,6},{8,9},{9,8},{10,11... | collective-permute-start | bytes 49160 | tf_op jit(solution)/shard_map/ppermute | solution.py:503
  26.1 0.0 collective-permute-done.3.came_ref
  26.1 0.7 %copy-done = f32[16]{0:T(128)S(1)} copy-done((f32[16]{0:T(128)S(1)}, f32[16]{0:T(128)}, u32[]{:S(2)}) %copy-start) | copy-done | bytes 88
  26.8 0.8 %prepare.1 = (f32[177,8,128]{2,1,0:T(8,128)S(1)}, f32[32,8,128]{2,1,0:T(8,128)S(1)}) custom-call(s32[1,4]{1,0:T(1,128)S(1)} %get-tuple-element.20.moving_ref, f32[16]{0:T(128)S(1)} %copy-done, f32[177,8,128]{2,1,0:T(8,128)S(1)} %get-tuple-element.21.state_ref, f32[178,4,128]{2,1,0:T(4,128)S(1)} %collective-permute-done.3.came_ref), custom_call_target="tpu_custom_call" | custom-call | tf_op jit(solution)/shard_map/prepare/pallas_call | solution.py:554
  27.6 0.0 collective-permute-done.5.refs_0_
  27.6 0.4 %collective-permute-done.6.refs_1_ = f32[2,16,128]{2,1,0:T(8,128)S(1)} collective-permute-done((f32[2,16,128]{2,1,0:T(8,128)S(1)}, f32[2,16,128]{2,1,0:T(8,128)S(1)}, u32[]{:S(2)}, u32[]{:S(2)}) %collective-permute-start.6) | collective-permute-done | bytes 16416 | tf_op jit(solution)/shard_map/ppermute | solution.py:503
  28.0 0.0 collective-permute-done.7.refs_2_
  28.0 1.6 %update.1 = (f32[59,8,128]{2,1,0:T(8,128)}, f32[59,8,128]{2,1,0:T(8,128)}, f32[59,8,128]{2,1,0:T(8,128)}, f32[3,8,128]{2,1,0:T(8,128)}) custom-call(f32[16]{0:T(128)S(1)} %copy-done, f32[177,8,128]{2,1,0:T(8,128)S(1)} %get-tuple-element.24.mixed_ref, f32[32,8,128]{2,1,0:T(8,128)S(1)} %get-tuple-element.25.slope_ref, ...), custom_call_target="tpu_custom_call" | custom-call | tf_op jit(solution)/shard_map/update/pallas_call | solution.py:567
  (2 shorter events, 0.0 us)
Async XLA Ops:
  1.7 7.6 %collective-permute-start.2 = (f32[9,8,128]{2,1,0:T(8,128)S(1)}, f32[9,8,128]{2,1,0:T(8,128)S(1)}, u32[]{:S(2)}, u32[]{:S(2)}) collective-permute-start(f32[9,8,128]{2,1,0:T(8,128)S(1)} %project.1.refs_3_), channel_id=1, source_target_pairs={{0,3},{1,2},{2,1},{3,0},{4,7},{5,6},{6,5},{7,4},{8,11},{9,10},{10,... | collective-permute-start | bytes 110600 | tf_op jit(solution)/shard_map/ppermute | solution.py:503
  6.8 4.9 %collective-permute-start.1 = (f32[9,8,128]{2,1,0:T(8,128)S(1)}, f32[9,8,128]{2,1,0:T(8,128)S(1)}, u32[]{:S(2)}, u32[]{:S(2)}) collective-permute-start(f32[9,8,128]{2,1,0:T(8,128)S(1)} %project.1.refs_3_), channel_id=1, source_target_pairs={{0,2},{1,3},{2,0},{3,1},{4,6},{5,7},{6,4},{7,5},{8,10},{9,11},{10,... | collective-permute-start | bytes 110600 | tf_op jit(solution)/shard_map/ppermute | solution.py:503
  6.8 4.9 %collective-permute-start = (f32[9,8,128]{2,1,0:T(8,128)S(1)}, f32[9,8,128]{2,1,0:T(8,128)S(1)}, u32[]{:S(2)}, u32[]{:S(2)}) collective-permute-start(f32[9,8,128]{2,1,0:T(8,128)S(1)} %project.1.refs_3_), channel_id=1, source_target_pairs={{0,1},{1,0},{2,3},{3,2},{4,5},{5,4},{6,7},{7,6},{8,9},{9,8},{10,11... | collective-permute-start | bytes 110600 | tf_op jit(solution)/shard_map/ppermute | solution.py:503
  7.4 4.2 %copy-start.1 = (f32[1,3,1024]{2,0,1:T(1,128)S(1)}, f32[1,3,1024]{2,0,1:T(1,128)}, u32[]{:S(2)}) copy-start(f32[1,3,1024]{2,0,1:T(1,128)} %param.11) | copy-start | bytes 36868
  11.6 14.5 %collective-permute-start.3 = (f32[178,4,128]{2,1,0:T(4,128)S(1)}, f32[178,4,128]{2,1,0:T(4,128)S(1)}, u32[]{:S(2)}, u32[]{:S(2)}) collective-permute-start(f32[178,4,128]{2,1,0:T(4,128)S(1)} %get-tuple-element.23), channel_id=1, source_target_pairs={{0,4},{4,8},{8,12},{12,16},{16,20},{20,24},{24,28},{28,0},{1,5},{5... | collective-permute-start | bytes 1093640 | tf_op jit(solution)/shard_map/ppermute | solution.py:506
  17.4 4.3 %collective-permute-start.4 = (f32[4,16,128]{2,1,0:T(8,128)S(1)}, f32[4,16,128]{2,1,0:T(8,128)S(1)}, u32[]{:S(2)}, u32[]{:S(2)}) collective-permute-start(f32[4,16,128]{2,1,0:T(8,128)S(1)} %get-tuple-element.31), channel_id=1, source_target_pairs={{0,4},{4,8},{8,12},{12,16},{16,20},{20,24},{24,28},{28,0},{1,5},{5... | collective-permute-start | bytes 98312 | tf_op jit(solution)/shard_map/ppermute | solution.py:506
  21.7 5.9 %collective-permute-start.5 = (f32[2,16,128]{2,1,0:T(8,128)S(1)}, f32[2,16,128]{2,1,0:T(8,128)S(1)}, u32[]{:S(2)}, u32[]{:S(2)}) collective-permute-start(f32[2,16,128]{2,1,0:T(8,128)S(1)} %get-tuple-element.45), channel_id=1, source_target_pairs={{0,3},{1,2},{2,1},{3,0},{4,7},{5,6},{6,5},{7,4},{8,11},{9,10},{10,... | collective-permute-start | bytes 49160 | tf_op jit(solution)/shard_map/ppermute | solution.py:503
  23.2 4.7 %collective-permute-start.6 = (f32[2,16,128]{2,1,0:T(8,128)S(1)}, f32[2,16,128]{2,1,0:T(8,128)S(1)}, u32[]{:S(2)}, u32[]{:S(2)}) collective-permute-start(f32[2,16,128]{2,1,0:T(8,128)S(1)} %get-tuple-element.46), channel_id=1, source_target_pairs={{0,2},{1,3},{2,0},{3,1},{4,6},{5,7},{6,4},{7,5},{8,10},{9,11},{10,... | collective-permute-start | bytes 49160 | tf_op jit(solution)/shard_map/ppermute | solution.py:503
  23.8 4.2 %collective-permute-start.7 = (f32[2,16,128]{2,1,0:T(8,128)S(1)}, f32[2,16,128]{2,1,0:T(8,128)S(1)}, u32[]{:S(2)}, u32[]{:S(2)}) collective-permute-start(f32[2,16,128]{2,1,0:T(8,128)S(1)} %get-tuple-element.47), channel_id=1, source_target_pairs={{0,1},{1,0},{2,3},{3,2},{4,5},{5,4},{6,7},{7,6},{8,9},{9,8},{10,11... | collective-permute-start | bytes 49160 | tf_op jit(solution)/shard_map/ppermute | solution.py:503
  26.1 0.7 %copy-start = (f32[16]{0:T(128)S(1)}, f32[16]{0:T(128)}, u32[]{:S(2)}) copy-start(f32[16]{0:T(128)} %basis_ref.3) | copy-start | bytes 196

commit v6 on v5

--- a/solution.py
+++ b/solution.py
@@ -249,7 +249,7 @@
 
     lax.fori_loop(0, listed, alphas, 0, unroll=min(listed, 4))
 
-    batch = 16
+    batch = 32
 
     def forward(n, running):
         trans, image = running
@@ -296,7 +296,6 @@
         row = pl.multiple_of(u * 8, 8)
         base = pl.multiple_of(u * (8 * chunks), 8 * chunks)
         part = [ebuf[pl.ds(base + c, 8, stride=chunks), :] for c in range(chunks)]
-        light = [wbuf[pl.ds(base + c, 8, stride=chunks), :] for c in range(chunks)]
         dx = px - qbuf[0, pl.ds(row, 8), :]
         dy = middle - qbuf[1, pl.ds(row, 8), :]
         half = chunks // 2
@@ -310,9 +309,6 @@
         sum_yy = dy * (sum_y + tilt) + bend
         sum_x = dx * plain
         sums = [plain, sum_x, sum_y, dx * sum_x, dx * sum_y, sum_yy]
-        for k in range(3):
-            lit = [light[c] * jnp.broadcast_to(errbuf[pl.ds(k * chunks + c, 1), :], (8, lanes)) for c in range(chunks)]
-            sums.append(((lit[0] + lit[1]) + (lit[2] + lit[3])) + ((lit[4] + lit[5]) + (lit[6] + lit[7])))
         for r, value in enumerate(sums):
             rbuf[r, pl.ds(row, 8), :] = value
 
@@ -322,17 +318,32 @@
         reduce_pixels(u + 1)
         for i in reversed(range(8)):
             alpha = abuf[pl.ds(base + i, chunks, stride=8), :]
-            ahead = shbuf[pl.ds(base + i, chunks, stride=8), :] - behind
-            behind = behind + alpha * ahead
-            ebuf[pl.ds(base + i * chunks, chunks), :] = wbuf[pl.ds(base + i * chunks, chunks), :] * ahead
+            shade = shbuf[pl.ds(base + i, chunks, stride=8), :]
+            weight = wbuf[pl.ds(base + i * chunks, chunks), :]
+            ebuf[pl.ds(base + i * chunks, chunks), :] = weight * (shade - behind)
+            behind = (1.0 - alpha) * behind + alpha * shade
         return behind
 
-    lax.fori_loop(0, groups, backward, zero, unroll=2)
+    lax.fori_loop(0, groups, backward, zero, unroll=16)
     reduce_pixels(0)
 
     def finish(j, _):
         at = pl.ds(pl.multiple_of(j * lanes, lanes), lanes)
-        part = [jnp.sum(rbuf[r, at, :].T, axis=0, keepdims=True) for r in range(NPROJ)]
+        part = [jnp.sum(rbuf[r, at, :].T, axis=0, keepdims=True) for r in range(6)]
+        first = pl.multiple_of(j * lanes * chunks, lanes * chunks)
+        lights = [wbuf[pl.ds(first + c, lanes, stride=chunks), :] for c in range(chunks)]
+        lit = jnp.zeros((lanes, 48), jnp.float32)
+        for n in range(2):
+            terms = [light.astype(jnp.bfloat16) for light in lights]
+            lights = [light - term.astype(jnp.float32) for light, term in zip(lights, terms)]
+            lit = lit + lax.dot_general(
+                jnp.concatenate(terms, axis=1),
+                basis[:, : chunks * lanes],
+                (((1,), (1,)), ((), ())),
+                preferred_element_type=jnp.float32,
+            )
+        lit = lit.T
+        part += [lit[k : k + 1] + lit[8 + k : 9 + k] + lit[32 + k : 33 + k] for k in range(3)]
         s0, sx, sy, sxx, sxy, syy = part[:6]
         ca, cb, cc, op = [pbuf[j, r : r + 1, :] for r in range(2, 6)]
         gbuf[j, 0:1, :] = ca * sx + cb * sy
@@ -352,10 +363,12 @@
         slots_ref[d, NPROJ : NPROJ + 1, :] = jnp.full((1, lanes), 1, jnp.float32) * ids[d].astype(jnp.float32)
 
 
-TERMS = 2 + 3 * 8 + 1 + 3
-
-
-def prepare_kernel(moving_ref, basis_ref, state_ref, came_ref, mixed_ref, slope_ref, kbuf):
+TERMS = 2 + 3 * 8 + 1 + 3 * SH
+
+
+def prepare_kernel(moving_ref, basis_hbm, state_ref, came_ref, mixed_ref, slope_ref, kbuf, basis_ref, sem):
+    fetch = pltpu.make_async_copy(basis_hbm, basis_ref, sem.at[0])
+    fetch.start()
     total, blocks, lanes = state_ref.shape
     rows = total // 3
     moves = came_ref.shape[1]
@@ -378,10 +391,13 @@
     v = geometry(p)
     slope_ref[0] = part * 0.375 * TILE_SIDE * (1.0 - v["tx"] * v["tx"])
     slope_ref[1] = part * 0.375 * TILE_SIDE * (1.0 - v["ty"] * v["ty"])
-    slope_ref[TERMS - 4] = part * 0.99 * v["so"] * (1.0 - v["so"])
+    slope_ref[26] = part * 0.99 * v["so"] * (1.0 - v["so"])
+    fetch.wait()
     for c in range(3):
         shade = colour(p, c, lambda k: basis_ref[k])
-        slope_ref[TERMS - 3 + c] = part * shade * (1.0 - shade)
+        rise = part * shade * (1.0 - shade)
+        for k in range(SH):
+            slope_ref[27 + SH * c + k] = rise * basis_ref[k]
     U, L, e, f, idet = v["U"], v["L"], v["e"], v["f"], v["idet"]
     w, x, y, z = v["q"]
     share = jnp.where(v["norm"] > 1.0, 1.0, jnp.where(v["norm"] == 1.0, 0.5, 0.0))
@@ -417,7 +433,7 @@
             slope_ref[14 + 3 * k + n] = part * (gq[k] - unit * along) * v["inv"]
 
 
-def update_kernel(basis_ref, mixed_ref, slope_ref, image_ref, *refs):
+def update_kernel(mixed_ref, slope_ref, image_ref, *refs):
     sources = refs[:-9]
     outs = refs[-9:-6]
     picture_hbm = refs[-6]
@@ -456,16 +472,15 @@
             copies.append(copy)
 
     for c in range(3):
-        logit = grads[6 + c] * slope_ref[TERMS - 3 + c]
         for k in range(SH):
-            store(11 + SH * c + k, logit * basis_ref[k])
+            store(11 + SH * c + k, grads[6 + c] * slope_ref[27 + SH * c + k])
         ship(11 + SH * c, 11 + SH * (c + 1))
     store(0, grads[0] * slope_ref[0])
     store(1, grads[1] * slope_ref[1])
     for i in range(8):
         at = 2 + 3 * i
         store(2 + i, grads[2] * slope_ref[at] + grads[3] * slope_ref[at + 1] + grads[4] * slope_ref[at + 2])
-    store(10, grads[5] * slope_ref[TERMS - 4])
+    store(10, grads[5] * slope_ref[26])
     ship(0, 11)
     for copy in copies:
         copy.wait()
@@ -539,7 +554,7 @@
             pltpu.VMEM((chunks * (width + 8), lanes), f32),
             pltpu.VMEM((chunks * width, lanes), f32),
             pltpu.VMEM((8 * chunks, lanes), f32),
-            pltpu.VMEM((NPROJ, width + 8, lanes), f32),
+            pltpu.VMEM((6, width + 8, lanes), f32),
             pltpu.VMEM((listed, GRADS, lanes), f32),
             pltpu.VMEM((48, (chunks + 5) * lanes), jnp.bfloat16),
             pltpu.VMEM((width, 48), jnp.bfloat16),
@@ -554,12 +569,12 @@
     mixed, slope = pl.pallas_call(
         prepare_kernel,
         out_shape=(sds((3 * rows, blocks, lanes), f32), sds((TERMS + 2, blocks, lanes), f32)),
-        in_specs=[smem, smem, vmem, vmem],
+        in_specs=[smem, hbm, vmem, vmem],
         out_specs=(vmem, vmem),
-        scratch_shapes=[pltpu.VMEM((8, blocks, lanes), f32)],
+        scratch_shapes=[pltpu.VMEM((8, blocks, lanes), f32), pltpu.SMEM(view_basis.shape, f32), dma((1,))],
         compiler_params=pltpu.CompilerParams(vmem_limit_bytes=5 << 20),
         name="prepare",
-    )(moved, view_basis, state, came)
+    )(moved, stay(view_basis), state, came)
     pairs = jnp.stack([slots, passed], axis=1)
     gathered = {0: pairs[0]}
     for d in range(1, peers):
@@ -567,12 +582,12 @@
     updated = pl.pallas_call(
         update_kernel,
         out_shape=(sds((rows, blocks, lanes), f32),) * 3 + (sds(image.shape, f32),),
-        in_specs=[smem] + [vmem] * (3 + peers),
+        in_specs=[vmem] * (3 + peers),
         out_specs=(hbm,) * 4,
         scratch_shapes=[pltpu.VMEM((rows, blocks, lanes), f32)] * 3 + [dma((12,)), dma((1,))],
         compiler_params=pltpu.CompilerParams(vmem_limit_bytes=5 << 20),
         name="update",
-    )(view_basis, mixed, slope, image, *[gathered[d] for d in reversed(range(peers))])
+    )(mixed, slope, image, *[gathered[d] for d in reversed(range(peers))])
     turned_back = [jnp.transpose(a, (1, 0, 2)) for a in updated[:3]]
     return (*turned_back, updated[3].reshape(1, 3, pixels))
 

time: 29.8 us -> 28.3 us (0.950)
  Pallas kernels: 11.1 us -> 10 us
  local copies, waits for them, and re-layouts: 0.66 us -> 0.01 us
    pallas_call x1, Pallas kernels: 5.78 us -> 4.81 us  [on_device(): pl.pallas_call(functools.partial(composite_kernel, peers), out_shape=(sds...]
    unnamed x4 -> x2, local copies, waits for them, and re-layouts: 0.66 us -> 0.01 us
    pallas_call x1, Pallas kernels: 1.56 us -> 1.02 us  [on_device(): pl.pallas_call(update_kernel, out_shape=(sds((rows, blocks, lanes), f32),...]
    pallas_call x1, Pallas kernels: 0.82 us -> 1.31 us  [on_device(): pl.pallas_call(prepare_kernel, out_shape=(sds((3 * rows, blocks, lanes),...]
  transfers between devices with their start and end apart: 8 -> 8, of which waited for: 3 -> 3; matrix products, arithmetic and copies ran while one was open for 0% -> 0% of each run, Pallas kernels for 29% -> 28%
where the time goes in v6:
time: 28.3 us; the launch traced here: 28.1 us
  starting transfers between devices  11.8 us (42%)
  Pallas kernels  10 us (35%)
  waiting for transfers between devices  5.55 us (20%)
  between operations  0.69 us (2%)
    ppermute x6, starting transfers between devices, swapped(): return lax.ppermute(value, 'tile', [(i, i ^ d) for i in range(peers)])  10.1 us
    pallas_call x1, Pallas kernels, on_device(): pl.pallas_call(functools.partial(composite_kernel, peers), out_shape=(sds...  4.81 us
    ppermute x6, waiting for transfers between devices, swapped(): return lax.ppermute(value, 'tile', [(i, i ^ d) for i in range(peers)])  2.9 us
    ppermute x2, waiting for transfers between devices, on_device(): lax.ppermute(value, 'region', [(i, (i + 1) % regions) for i in range(regi...  2.65 us
    pallas_call x1, Pallas kernels, on_device(): pl.pallas_call(pack_kernel, out_shape=(sds((3 * rows + 1, moves, lanes),...  1.86 us
    ppermute x2, starting transfers between devices, on_device(): lax.ppermute(value, 'region', [(i, (i + 1) % regions) for i in range(regi...  1.64 us
    pallas_call x1, Pallas kernels, on_device(): pl.pallas_call(prepare_kernel, out_shape=(sds((3 * rows, blocks, lanes),...  1.31 us
    pallas_call x1, Pallas kernels, on_device(): pl.pallas_call(project_kernel, out_shape=sds((NPROJ, blocks, lanes), f32)...  1.02 us
  transfers between devices with their start and end apart: 8, of which 3 were waited for; matrix products, arithmetic and copies ran while one was open for 0% of the time, Pallas kernels for 28%

profile of v6, /device:TPU:0, one launch (start us, length us, event | category | flops | bytes accessed | tf_op | source)
XLA Modules:
  0.0 28.1 jit_solution(16167134083469537457)
XLA Ops:
  0.6 1.0 %project.1.refs_3_ = f32[9,8,128]{2,1,0:T(8,128)S(1)} custom-call(f32[16]{0:T(128)} %basis_hbm.3, f32[59,8,128]{2,1,0:T(8,128)} %bitcast.20), custom_call_target="tpu_custom_call" | custom-call | tf_op jit(solution)/shard_map/project/pallas_call | solution.py:507
  1.7 5.1 %collective-permute-start.2 = (f32[9,8,128]{2,1,0:T(8,128)S(1)}, f32[9,8,128]{2,1,0:T(8,128)S(1)}, u32[]{:S(2)}, u32[]{:S(2)}) collective-permute-start(f32[9,8,128]{2,1,0:T(8,128)S(1)} %project.1.refs_3_), channel_id=1, source_target_pairs={{0,3},{1,2},{2,1},{3,0},{4,7},{5,6},{6,5},{7,4},{8,11},{9,10},{10,... | collective-permute-start | bytes 110600 | tf_op jit(solution)/shard_map/ppermute | solution.py:518
  6.8 0.0 collective-permute-start.1
  6.8 0.6 %collective-permute-start = (f32[9,8,128]{2,1,0:T(8,128)S(1)}, f32[9,8,128]{2,1,0:T(8,128)S(1)}, u32[]{:S(2)}, u32[]{:S(2)}) collective-permute-start(f32[9,8,128]{2,1,0:T(8,128)S(1)} %project.1.refs_3_), channel_id=1, source_target_pairs={{0,1},{1,0},{2,3},{3,2},{4,5},{5,4},{6,7},{7,6},{8,9},{9,8},{10,11... | collective-permute-start | bytes 110600 | tf_op jit(solution)/shard_map/ppermute | solution.py:518
  7.4 0.0 copy-start
  7.4 1.9 %pack.1 = (f32[178,4,128]{2,1,0:T(4,128)S(1)}, f32[177,8,128]{2,1,0:T(8,128)S(1)}, s32[1,4]{1,0:T(1,128)S(1)}, s32[1,4]{1,0:T(1,128)S(1)}) custom-call(s32[1,4]{1,0:T(1,128)} %moving_hbm.1, s32[1,4]{1,0:T(1,128)} %listed_hbm.1, f32[59,8,128]{2,1,0:T(8,128)} %bitcast.21, f32[59,8,128]{2,1,0:T(8,128)} %bitcast.22, f32[59,8,128]{2,1,0:T(8,128)} %bitcast.23), custom_call_target="tpu_custom_call" | custom-call | tf_op jit(solution)/shard_map/pack/pallas_call | solution.py:523
  9.3 0.0 collective-permute-done.2.refs_0_
  9.3 2.3 %collective-permute-done.1.refs_1_ = f32[9,8,128]{2,1,0:T(8,128)S(1)} collective-permute-done((f32[9,8,128]{2,1,0:T(8,128)S(1)}, f32[9,8,128]{2,1,0:T(8,128)S(1)}, u32[]{:S(2)}, u32[]{:S(2)}) %collective-permute-start.1) | collective-permute-done | bytes 36896 | tf_op jit(solution)/shard_map/ppermute | solution.py:518
  11.6 0.0 collective-permute-done.refs_2_
  11.6 0.0 collective-permute-start.3
  11.6 0.0 copy-done
  11.6 4.8 %composite.1 = (f32[3,8,128]{2,1,0:T(8,128)S(1)}, f32[4,16,128]{2,1,0:T(8,128)S(1)}) custom-call(s32[1,4]{1,0:T(1,128)S(1)} %get-tuple-element.26.listed_ref, f32[9,8,128]{2,1,0:T(8,128)S(1)} %collective-permute-done.2.refs_0_, f32[9,8,128]{2,1,0:T(8,128)S(1)} %collective-permute-done.1.refs_1_, f32[9,8,128]{2,1,0:T(8,128)S(1)} %collective-permute-done.refs_2_, ...), custom_call_target="tpu_custom_call" | custom-call | flops 33554432 | bytes 25165824 | tf_op jit(solution)/shard_map/composite/pallas_call | solution.py:544
  16.5 1.6 %collective-permute-start.4 = (f32[4,16,128]{2,1,0:T(8,128)S(1)}, f32[4,16,128]{2,1,0:T(8,128)S(1)}, u32[]{:S(2)}, u32[]{:S(2)}) collective-permute-start(f32[4,16,128]{2,1,0:T(8,128)S(1)} %get-tuple-element.31), channel_id=1, source_target_pairs={{0,4},{4,8},{8,12},{12,16},{16,20},{20,24},{24,28},{28,0},{1,5},{5... | collective-permute-start | bytes 98312 | tf_op jit(solution)/shard_map/ppermute | solution.py:521
  18.1 2.7 %collective-permute-done.4 = f32[4,16,128]{2,1,0:T(8,128)S(1)} collective-permute-done((f32[4,16,128]{2,1,0:T(8,128)S(1)}, f32[4,16,128]{2,1,0:T(8,128)S(1)}, u32[]{:S(2)}, u32[]{:S(2)}) %collective-permute-start.4) | collective-permute-done | bytes 32800 | tf_op jit(solution)/shard_map/ppermute | solution.py:521
  20.8 1.5 %collective-permute-start.5 = (f32[2,16,128]{2,1,0:T(8,128)S(1)}, f32[2,16,128]{2,1,0:T(8,128)S(1)}, u32[]{:S(2)}, u32[]{:S(2)}) collective-permute-start(f32[2,16,128]{2,1,0:T(8,128)S(1)} %get-tuple-element.45), channel_id=1, source_target_pairs={{0,3},{1,2},{2,1},{3,0},{4,7},{5,6},{6,5},{7,4},{8,11},{9,10},{10,... | collective-permute-start | bytes 49160 | tf_op jit(solution)/shard_map/ppermute | solution.py:518
  22.3 0.6 %collective-permute-start.6 = (f32[2,16,128]{2,1,0:T(8,128)S(1)}, f32[2,16,128]{2,1,0:T(8,128)S(1)}, u32[]{:S(2)}, u32[]{:S(2)}) collective-permute-start(f32[2,16,128]{2,1,0:T(8,128)S(1)} %get-tuple-element.46), channel_id=1, source_target_pairs={{0,2},{1,3},{2,0},{3,1},{4,6},{5,7},{6,4},{7,5},{8,10},{9,11},{10,... | collective-permute-start | bytes 49160 | tf_op jit(solution)/shard_map/ppermute | solution.py:518
  22.9 2.3 %collective-permute-start.7 = (f32[2,16,128]{2,1,0:T(8,128)S(1)}, f32[2,16,128]{2,1,0:T(8,128)S(1)}, u32[]{:S(2)}, u32[]{:S(2)}) collective-permute-start(f32[2,16,128]{2,1,0:T(8,128)S(1)} %get-tuple-element.47), channel_id=1, source_target_pairs={{0,1},{1,0},{2,3},{3,2},{4,5},{5,4},{6,7},{7,6},{8,9},{9,8},{10,11... | collective-permute-start | bytes 49160 | tf_op jit(solution)/shard_map/ppermute | solution.py:518
  25.2 0.0 collective-permute-done.3.came_ref
  25.2 1.3 %prepare.1 = (f32[177,8,128]{2,1,0:T(8,128)S(1)}, f32[77,8,128]{2,1,0:T(8,128)S(1)}) custom-call(s32[1,4]{1,0:T(1,128)S(1)} %get-tuple-element.20.moving_ref, f32[16]{0:T(128)} %basis_hbm.3, f32[177,8,128]{2,1,0:T(8,128)S(1)} %get-tuple-element.21.state_ref, f32[178,4,128]{2,1,0:T(4,128)S(1)} %collective-permute-done.3.came_ref), custom_call_target="tpu_custom_call" | custom-call | tf_op jit(solution)/shard_map/prepare/pallas_call | solution.py:569
  26.5 0.0 collective-permute-done.5.refs_0_
  26.5 0.5 %collective-permute-done.6.refs_1_ = f32[2,16,128]{2,1,0:T(8,128)S(1)} collective-permute-done((f32[2,16,128]{2,1,0:T(8,128)S(1)}, f32[2,16,128]{2,1,0:T(8,128)S(1)}, u32[]{:S(2)}, u32[]{:S(2)}) %collective-permute-start.6) | collective-permute-done | bytes 16416 | tf_op jit(solution)/shard_map/ppermute | solution.py:518
  27.0 0.0 collective-permute-done.7.refs_2_
  27.0 1.0 %update.1 = (f32[59,8,128]{2,1,0:T(8,128)}, f32[59,8,128]{2,1,0:T(8,128)}, f32[59,8,128]{2,1,0:T(8,128)}, f32[3,8,128]{2,1,0:T(8,128)}) custom-call(f32[177,8,128]{2,1,0:T(8,128)S(1)} %get-tuple-element.24.mixed_ref, f32[77,8,128]{2,1,0:T(8,128)S(1)} %get-tuple-element.25.slope_ref, f32[3,8,128]{2,1,0:T(8,128)S(1)} %get-tuple-element.30.image_ref, ...), custom_call_target="tpu_custom_call" | custom-call | tf_op jit(solution)/shard_map/update/pallas_call | solution.py:582
  (1 shorter events, 0.0 us)
Async XLA Ops:
  1.7 7.6 %collective-permute-start.2 = (f32[9,8,128]{2,1,0:T(8,128)S(1)}, f32[9,8,128]{2,1,0:T(8,128)S(1)}, u32[]{:S(2)}, u32[]{:S(2)}) collective-permute-start(f32[9,8,128]{2,1,0:T(8,128)S(1)} %project.1.refs_3_), channel_id=1, source_target_pairs={{0,3},{1,2},{2,1},{3,0},{4,7},{5,6},{6,5},{7,4},{8,11},{9,10},{10,... | collective-permute-start | bytes 110600 | tf_op jit(solution)/shard_map/ppermute | solution.py:518
  6.8 4.9 %collective-permute-start.1 = (f32[9,8,128]{2,1,0:T(8,128)S(1)}, f32[9,8,128]{2,1,0:T(8,128)S(1)}, u32[]{:S(2)}, u32[]{:S(2)}) collective-permute-start(f32[9,8,128]{2,1,0:T(8,128)S(1)} %project.1.refs_3_), channel_id=1, source_target_pairs={{0,2},{1,3},{2,0},{3,1},{4,6},{5,7},{6,4},{7,5},{8,10},{9,11},{10,... | collective-permute-start | bytes 110600 | tf_op jit(solution)/shard_map/ppermute | solution.py:518
  6.8 4.9 %collective-permute-start = (f32[9,8,128]{2,1,0:T(8,128)S(1)}, f32[9,8,128]{2,1,0:T(8,128)S(1)}, u32[]{:S(2)}, u32[]{:S(2)}) collective-permute-start(f32[9,8,128]{2,1,0:T(8,128)S(1)} %project.1.refs_3_), channel_id=1, source_target_pairs={{0,1},{1,0},{2,3},{3,2},{4,5},{5,4},{6,7},{7,6},{8,9},{9,8},{10,11... | collective-permute-start | bytes 110600 | tf_op jit(solution)/shard_map/ppermute | solution.py:518
  7.4 4.2 %copy-start = (f32[1,3,1024]{2,0,1:T(1,128)S(1)}, f32[1,3,1024]{2,0,1:T(1,128)}, u32[]{:S(2)}) copy-start(f32[1,3,1024]{2,0,1:T(1,128)} %param.11) | copy-start | bytes 36868
  11.6 13.5 %collective-permute-start.3 = (f32[178,4,128]{2,1,0:T(4,128)S(1)}, f32[178,4,128]{2,1,0:T(4,128)S(1)}, u32[]{:S(2)}, u32[]{:S(2)}) collective-permute-start(f32[178,4,128]{2,1,0:T(4,128)S(1)} %get-tuple-element.23), channel_id=1, source_target_pairs={{0,4},{4,8},{8,12},{12,16},{16,20},{20,24},{24,28},{28,0},{1,5},{5... | collective-permute-start | bytes 1093640 | tf_op jit(solution)/shard_map/ppermute | solution.py:521
  16.5 4.3 %collective-permute-start.4 = (f32[4,16,128]{2,1,0:T(8,128)S(1)}, f32[4,16,128]{2,1,0:T(8,128)S(1)}, u32[]{:S(2)}, u32[]{:S(2)}) collective-permute-start(f32[4,16,128]{2,1,0:T(8,128)S(1)} %get-tuple-element.31), channel_id=1, source_target_pairs={{0,4},{4,8},{8,12},{12,16},{16,20},{20,24},{24,28},{28,0},{1,5},{5... | collective-permute-start | bytes 98312 | tf_op jit(solution)/shard_map/ppermute | solution.py:521
  20.8 5.7 %collective-permute-start.5 = (f32[2,16,128]{2,1,0:T(8,128)S(1)}, f32[2,16,128]{2,1,0:T(8,128)S(1)}, u32[]{:S(2)}, u32[]{:S(2)}) collective-permute-start(f32[2,16,128]{2,1,0:T(8,128)S(1)} %get-tuple-element.45), channel_id=1, source_target_pairs={{0,3},{1,2},{2,1},{3,0},{4,7},{5,6},{6,5},{7,4},{8,11},{9,10},{10,... | collective-permute-start | bytes 49160 | tf_op jit(solution)/shard_map/ppermute | solution.py:518
  22.3 4.7 %collective-permute-start.6 = (f32[2,16,128]{2,1,0:T(8,128)S(1)}, f32[2,16,128]{2,1,0:T(8,128)S(1)}, u32[]{:S(2)}, u32[]{:S(2)}) collective-permute-start(f32[2,16,128]{2,1,0:T(8,128)S(1)} %get-tuple-element.46), channel_id=1, source_target_pairs={{0,2},{1,3},{2,0},{3,1},{4,6},{5,7},{6,4},{7,5},{8,10},{9,11},{10,... | collective-permute-start | bytes 49160 | tf_op jit(solution)/shard_map/ppermute | solution.py:518
  22.9 4.2 %collective-permute-start.7 = (f32[2,16,128]{2,1,0:T(8,128)S(1)}, f32[2,16,128]{2,1,0:T(8,128)S(1)}, u32[]{:S(2)}, u32[]{:S(2)}) collective-permute-start(f32[2,16,128]{2,1,0:T(8,128)S(1)} %get-tuple-element.47), channel_id=1, source_target_pairs={{0,1},{1,0},{2,3},{3,2},{4,5},{5,4},{6,7},{7,6},{8,9},{9,8},{10,11... | collective-permute-start | bytes 49160 | tf_op jit(solution)/shard_map/ppermute | solution.py:518

commit v7 on v6

--- a/solution.py
+++ b/solution.py
@@ -1,4 +1,3 @@
-import functools
 import math
 import jax
 import jax.numpy as jnp
@@ -124,7 +123,7 @@
     return list(zip(cuts[:-1], cuts[1:]))
 
 
-def pack_kernel(moving_hbm, listed_hbm, p_hbm, f_hbm, s_hbm, leave_ref, state_ref, moving_ref, listed_ref, sems):
+def pack_kernel(moving_hbm, listed_hbm, p_hbm, f_hbm, s_hbm, leave_ref, state_ref, mine_ref, place_ref, moving_ref, listed_ref, sems):
     total, moves, lanes = leave_ref.shape
     rows, blocks, _ = p_hbm.shape
     ids = pltpu.make_async_copy(moving_hbm, moving_ref, sems.at[3 * PIECES])
@@ -142,6 +141,19 @@
             copies.append(copy)
     ids.wait()
     lists.wait()
+    source, taken = picks(moving_ref, blocks, lanes)
+    mine_ref[0] = source
+    mine_ref[1] = taken.astype(jnp.int32)
+    me = lax.axis_index("tile")
+    for d in range(place_ref.shape[1]):
+        place, named = jnp.int32(0), jnp.int32(0)
+        for n in range(listed_ref.shape[1]):
+            entry = listed_ref[0, n]
+            here = lax.div(entry, jnp.int32(blocks)) == jnp.bitwise_xor(me, d)
+            place = jnp.where(here, n, place)
+            named = jnp.where(here, lax.rem(entry, jnp.int32(blocks)), named)
+        place_ref[0, d] = jnp.zeros((blocks, lanes), jnp.int32) + place
+        place_ref[1, d] = jnp.zeros((blocks, lanes), jnp.int32) + named
     slot = lax.broadcasted_iota(jnp.int32, (blocks, lanes), 0)
     pick = jnp.zeros((blocks, lanes), jnp.int32)
     for m in range(moves):
@@ -160,7 +172,8 @@
     return high, middle, rest - middle
 
 
-def composite_kernel(peers, listed_ref, *refs):
+def composite_kernel(place_ref, *refs):
+    peers = place_ref.shape[1]
     sources = refs[:peers][::-1]
     target_ref = refs[peers]
     image_ref = refs[peers + 1]
@@ -172,20 +185,14 @@
     chunks = errbuf.shape[0] // 8
     spreads = qbuf.shape[0]
     assert chunks == 8
-    blocks = sources[0].shape[1]
-    me = lax.axis_index("tile")
-    places, ids = [], []
-    for d in range(peers):
-        pos, loc = jnp.int32(0), jnp.int32(0)
-        for n in range(listed):
-            named = listed_ref[0, n]
-            here = lax.div(named, jnp.int32(blocks)) == jnp.bitwise_xor(me, d)
-            pos = jnp.where(here, n, pos)
-            loc = jnp.where(here, lax.rem(named, jnp.int32(blocks)), loc)
-        places.append(pos)
-        ids.append(loc)
-        for r in range(NPROJ):
-            pbuf[pos, pl.ds(r, 1), :] = sources[d][r, pl.ds(loc, 1), :]
+    at_place = [[place_ref[0, d] == j for d in range(peers)] for j in range(listed)]
+    for r in range(NPROJ):
+        found = [jnp.take_along_axis(sources[d][r], place_ref[1, d], axis=0) for d in range(peers)]
+        for j in range(listed):
+            row = found[0]
+            for d in range(1, peers):
+                row = jnp.where(at_place[j][d], found[d], row)
+            pbuf[j, r : r + 1, :] = row[0:1]
 
     lane = lax.broadcasted_iota(jnp.int32, (8, lanes), 1)
     which = lax.broadcasted_iota(jnp.int32, (8, lanes), 0)
@@ -359,20 +366,25 @@
 
     lax.fori_loop(0, listed, finish, 0, unroll=min(listed, 4))
     for d in range(peers):
-        slots_ref[d] = gbuf[places[d]]
-        slots_ref[d, NPROJ : NPROJ + 1, :] = jnp.full((1, lanes), 1, jnp.float32) * ids[d].astype(jnp.float32)
+        for low in range(0, GRADS, 8):
+            out = gbuf[0, low : low + 8, :]
+            for j in range(1, listed):
+                out = jnp.where(at_place[j][d], gbuf[j, low : low + 8, :], out)
+            slots_ref[d, low : low + 8, :] = out
+        slots_ref[d, NPROJ : NPROJ + 1, :] = place_ref[1, d][0:1].astype(jnp.float32)
 
 
 TERMS = 2 + 3 * 8 + 1 + 3 * SH
 
 
-def prepare_kernel(moving_ref, basis_hbm, state_ref, came_ref, mixed_ref, slope_ref, kbuf, basis_ref, sem):
+def prepare_kernel(mine_ref, basis_hbm, state_ref, came_ref, mixed_ref, slope_ref, kbuf, basis_ref, sem):
     fetch = pltpu.make_async_copy(basis_hbm, basis_ref, sem.at[0])
     fetch.start()
     total, blocks, lanes = state_ref.shape
     rows = total // 3
     moves = came_ref.shape[1]
-    source, taken = picks(moving_ref, blocks, lanes)
+    source = mine_ref[0]
+    taken = mine_ref[1] > 0
 
     def arrived(i):
         kbuf[i % 8, 0:moves, :] = came_ref[i]
@@ -496,7 +508,6 @@
     chunks = pixels // lanes
     width = listed * lanes
     f32 = jnp.float32
-    smem = pl.BlockSpec(memory_space=pltpu.SMEM)
     vmem = pl.BlockSpec(memory_space=pltpu.VMEM)
     sds = jax.ShapeDtypeStruct
 
@@ -520,17 +531,21 @@
     regions = lax.axis_size("region")
     onward = lambda value: lax.ppermute(value, "region", [(i, (i + 1) % regions) for i in range(regions)])
 
-    leaving, state, moved, named = pl.pallas_call(
+    leaving, state, mine, place = pl.pallas_call(
         pack_kernel,
         out_shape=(
             sds((3 * rows + 1, moves, lanes), f32),
             sds((3 * rows, blocks, lanes), f32),
-            sds(moving.shape, jnp.int32),
-            sds(tile_blocks.shape, jnp.int32),
+            sds((2, blocks, lanes), jnp.int32),
+            sds((2, peers, blocks, lanes), jnp.int32),
         ),
         in_specs=[hbm] * 5,
-        out_specs=(vmem, vmem, smem, smem),
-        scratch_shapes=[dma((3 * PIECES + 2,))],
+        out_specs=(vmem,) * 4,
+        scratch_shapes=[
+            pltpu.SMEM(moving.shape, jnp.int32),
+            pltpu.SMEM(tile_blocks.shape, jnp.int32),
+            dma((3 * PIECES + 2,)),
+        ],
         compiler_params=pltpu.CompilerParams(vmem_limit_bytes=4 << 20),
         name="pack",
     )(stay(moving), stay(tile_blocks), *[stay(a) for a in turned])
@@ -542,9 +557,9 @@
         away[d] = rest[d - 1]
     came = onward(leaving)
     image, slots = pl.pallas_call(
-        functools.partial(composite_kernel, peers),
+        composite_kernel,
         out_shape=(sds((3, chunks, lanes), f32), sds((peers, GRADS, lanes), f32)),
-        in_specs=[smem] + [vmem] * (peers + 1),
+        in_specs=[vmem] * (peers + 2),
         out_specs=(vmem, vmem),
         scratch_shapes=[
             pltpu.VMEM((listed, GRADS, lanes), f32),
@@ -564,17 +579,17 @@
             flops=64 * width * pixels, transcendentals=width * pixels, bytes_accessed=48 * width * pixels
         ),
         name="composite",
-    )(named, *[away[d] for d in reversed(range(peers))], target.reshape(3, chunks, lanes))
+    )(place, *[away[d] for d in reversed(range(peers))], target.reshape(3, chunks, lanes))
     passed = onward(slots)
     mixed, slope = pl.pallas_call(
         prepare_kernel,
         out_shape=(sds((3 * rows, blocks, lanes), f32), sds((TERMS + 2, blocks, lanes), f32)),
-        in_specs=[smem, hbm, vmem, vmem],
+        in_specs=[vmem, hbm, vmem, vmem],
         out_specs=(vmem, vmem),
         scratch_shapes=[pltpu.VMEM((8, blocks, lanes), f32), pltpu.SMEM(view_basis.shape, f32), dma((1,))],
         compiler_params=pltpu.CompilerParams(vmem_limit_bytes=5 << 20),
         name="prepare",
-    )(moved, stay(view_basis), state, came)
+    )(mine, stay(view_basis), state, came)
     pairs = jnp.stack([slots, passed], axis=1)
     gathered = {0: pairs[0]}
     for d in range(1, peers):

time: 28.3 us -> 27.8 us (0.982)
  Pallas kernels: 10 us -> 8.34 us
  waiting for transfers between devices: 5.55 us -> 6.69 us
    ppermute x6, waiting for transfers between devices: 2.9 us -> 4.04 us  [swapped(): return lax.ppermute(value, 'tile', [(i, i ^ d) for i in range(peers)])]
    pallas_call x1, Pallas kernels: 1.86 us -> 1.27 us  [on_device(): pl.pallas_call(pack_kernel, out_shape=(sds((3 * rows + 1, moves, lanes),...]
    pallas_call x1, Pallas kernels: 4.81 us -> 4.27 us  [on_device(): pl.pallas_call(composite_kernel, out_shape=(sds((3, chunks, lanes), f32),...]
    pallas_call x1, Pallas kernels: 1.31 us -> 0.77 us  [on_device(): pl.pallas_call(prepare_kernel, out_shape=(sds((3 * rows, blocks, lanes),...]
  transfers between devices with their start and end apart: 8 -> 8, of which waited for: 3 -> 5; matrix products, arithmetic and copies ran while one was open for 0% -> 0% of each run, Pallas kernels for 28% -> 23%
where the time goes in v7:
time: 27.8 us; the launch traced here: 27.5 us
  starting transfers between devices  11.8 us (42%)
  Pallas kernels  8.34 us (30%)
  waiting for transfers between devices  6.69 us (24%)
  between operations  0.67 us (2%)
    ppermute x6, starting transfers between devices, swapped(): return lax.ppermute(value, 'tile', [(i, i ^ d) for i in range(peers)])  10.1 us
    pallas_call x1, Pallas kernels, on_device(): pl.pallas_call(composite_kernel, out_shape=(sds((3, chunks, lanes), f32),...  4.27 us
    ppermute x6, waiting for transfers between devices, swapped(): return lax.ppermute(value, 'tile', [(i, i ^ d) for i in range(peers)])  4.04 us
    ppermute x2, waiting for transfers between devices, on_device(): lax.ppermute(value, 'region', [(i, (i + 1) % regions) for i in range(regi...  2.64 us
    ppermute x2, starting transfers between devices, on_device(): lax.ppermute(value, 'region', [(i, (i + 1) % regions) for i in range(regi...  1.65 us
    pallas_call x1, Pallas kernels, on_device(): pl.pallas_call(pack_kernel, out_shape=(sds((3 * rows + 1, moves, lanes),...  1.27 us
    pallas_call x1, Pallas kernels, on_device(): pl.pallas_call(project_kernel, out_shape=sds((NPROJ, blocks, lanes), f32)...  1.02 us
    pallas_call x1, Pallas kernels, on_device(): pl.pallas_call(update_kernel, out_shape=(sds((rows, blocks, lanes), f32),...  1.02 us
  transfers between devices with their start and end apart: 8, of which 5 were waited for; matrix products, arithmetic and copies ran while one was open for 0% of the time, Pallas kernels for 23%

profile of v7, /device:TPU:0, one launch (start us, length us, event | category | flops | bytes accessed | tf_op | source)
XLA Modules:
  0.0 27.5 jit_solution(2847099023293391357)
XLA Ops:
  0.6 1.0 %project.1.refs_3_ = f32[9,8,128]{2,1,0:T(8,128)S(1)} custom-call(f32[16]{0:T(128)} %basis_hbm.3, f32[59,8,128]{2,1,0:T(8,128)} %bitcast.20), custom_call_target="tpu_custom_call" | custom-call | tf_op jit(solution)/shard_map/project/pallas_call | solution.py:518
  1.7 5.1 %collective-permute-start.2 = (f32[9,8,128]{2,1,0:T(8,128)S(1)}, f32[9,8,128]{2,1,0:T(8,128)S(1)}, u32[]{:S(2)}, u32[]{:S(2)}) collective-permute-start(f32[9,8,128]{2,1,0:T(8,128)S(1)} %project.1.refs_3_), channel_id=1, source_target_pairs={{0,3},{1,2},{2,1},{3,0},{4,7},{5,6},{6,5},{7,4},{8,11},{9,10},{10,... | collective-permute-start | bytes 110600 | tf_op jit(solution)/shard_map/ppermute | solution.py:529
  6.8 0.0 collective-permute-start.1
  6.8 0.6 %collective-permute-start = (f32[9,8,128]{2,1,0:T(8,128)S(1)}, f32[9,8,128]{2,1,0:T(8,128)S(1)}, u32[]{:S(2)}, u32[]{:S(2)}) collective-permute-start(f32[9,8,128]{2,1,0:T(8,128)S(1)} %project.1.refs_3_), channel_id=1, source_target_pairs={{0,1},{1,0},{2,3},{3,2},{4,5},{5,4},{6,7},{7,6},{8,9},{9,8},{10,11... | collective-permute-start | bytes 110600 | tf_op jit(solution)/shard_map/ppermute | solution.py:529
  7.4 0.0 copy-start
  7.4 1.3 %pack.1 = (f32[178,4,128]{2,1,0:T(4,128)S(1)}, f32[177,8,128]{2,1,0:T(8,128)S(1)}, s32[2,8,128]{2,1,0:T(8,128)S(1)}, s32[2,4,8,128]{3,2,1,0:T(8,128)S(1)}) custom-call(s32[1,4]{1,0:T(1,128)} %moving_hbm.1, s32[1,4]{1,0:T(1,128)} %listed_hbm.1, f32[59,8,128]{2,1,0:T(8,128)} %bitcast.21, f32[59,8,128]{2,1,0:T(8,128)} %bitcast.22, f32[59,8,128]{2,1,0:T(8,128)} %bitcast.23), custom_call_target="tpu_custom_call" | custom-call | tf_op jit(solution)/shard_map/pack/pallas_call | solution.py:534
  8.7 0.0 collective-permute-done.2.refs_0_
  8.7 2.9 %collective-permute-done.1.refs_1_ = f32[9,8,128]{2,1,0:T(8,128)S(1)} collective-permute-done((f32[9,8,128]{2,1,0:T(8,128)S(1)}, f32[9,8,128]{2,1,0:T(8,128)S(1)}, u32[]{:S(2)}, u32[]{:S(2)}) %collective-permute-start.1) | collective-permute-done | bytes 36896 | tf_op jit(solution)/shard_map/ppermute | solution.py:529
  11.6 0.0 collective-permute-done.refs_2_
  11.6 0.0 collective-permute-start.3
  11.6 0.0 copy-done
  11.6 4.3 %composite.1 = (f32[3,8,128]{2,1,0:T(8,128)S(1)}, f32[4,16,128]{2,1,0:T(8,128)S(1)}) custom-call(s32[2,4,8,128]{3,2,1,0:T(8,128)S(1)} %get-tuple-element.26.place_ref, f32[9,8,128]{2,1,0:T(8,128)S(1)} %collective-permute-done.2.refs_0_, f32[9,8,128]{2,1,0:T(8,128)S(1)} %collective-permute-done.1.refs_1_, f32[9,8,128]{2,1,0:T(8,128)S(1)} %collective-permute-done.refs_2_, ...), custom_call_target="tpu_custom_call" | custom-call | flops 33554432 | bytes 25165824 | tf_op jit(solution)/shard_map/composite/pallas_call | solution.py:559
  15.9 1.6 %collective-permute-start.4 = (f32[4,16,128]{2,1,0:T(8,128)S(1)}, f32[4,16,128]{2,1,0:T(8,128)S(1)}, u32[]{:S(2)}, u32[]{:S(2)}) collective-permute-start(f32[4,16,128]{2,1,0:T(8,128)S(1)} %get-tuple-element.31), channel_id=1, source_target_pairs={{0,4},{4,8},{8,12},{12,16},{16,20},{20,24},{24,28},{28,0},{1,5},{5... | collective-permute-start | bytes 98312 | tf_op jit(solution)/shard_map/ppermute | solution.py:532
  17.6 2.6 %collective-permute-done.4 = f32[4,16,128]{2,1,0:T(8,128)S(1)} collective-permute-done((f32[4,16,128]{2,1,0:T(8,128)S(1)}, f32[4,16,128]{2,1,0:T(8,128)S(1)}, u32[]{:S(2)}, u32[]{:S(2)}) %collective-permute-start.4) | collective-permute-done | bytes 32800 | tf_op jit(solution)/shard_map/ppermute | solution.py:532
  20.2 1.5 %collective-permute-start.5 = (f32[2,16,128]{2,1,0:T(8,128)S(1)}, f32[2,16,128]{2,1,0:T(8,128)S(1)}, u32[]{:S(2)}, u32[]{:S(2)}) collective-permute-start(f32[2,16,128]{2,1,0:T(8,128)S(1)} %get-tuple-element.45), channel_id=1, source_target_pairs={{0,3},{1,2},{2,1},{3,0},{4,7},{5,6},{6,5},{7,4},{8,11},{9,10},{10,... | collective-permute-start | bytes 49160 | tf_op jit(solution)/shard_map/ppermute | solution.py:529
  21.7 0.6 %collective-permute-start.6 = (f32[2,16,128]{2,1,0:T(8,128)S(1)}, f32[2,16,128]{2,1,0:T(8,128)S(1)}, u32[]{:S(2)}, u32[]{:S(2)}) collective-permute-start(f32[2,16,128]{2,1,0:T(8,128)S(1)} %get-tuple-element.46), channel_id=1, source_target_pairs={{0,2},{1,3},{2,0},{3,1},{4,6},{5,7},{6,4},{7,5},{8,10},{9,11},{10,... | collective-permute-start | bytes 49160 | tf_op jit(solution)/shard_map/ppermute | solution.py:529
  22.3 2.3 %collective-permute-start.7 = (f32[2,16,128]{2,1,0:T(8,128)S(1)}, f32[2,16,128]{2,1,0:T(8,128)S(1)}, u32[]{:S(2)}, u32[]{:S(2)}) collective-permute-start(f32[2,16,128]{2,1,0:T(8,128)S(1)} %get-tuple-element.47), channel_id=1, source_target_pairs={{0,1},{1,0},{2,3},{3,2},{4,5},{5,4},{6,7},{7,6},{8,9},{9,8},{10,11... | collective-permute-start | bytes 49160 | tf_op jit(solution)/shard_map/ppermute | solution.py:529
  24.6 0.0 collective-permute-done.3.came_ref
  24.6 0.8 %prepare.1 = (f32[177,8,128]{2,1,0:T(8,128)S(1)}, f32[77,8,128]{2,1,0:T(8,128)S(1)}) custom-call(s32[2,8,128]{2,1,0:T(8,128)S(1)} %get-tuple-element.20.mine_ref, f32[16]{0:T(128)} %basis_hbm.3, f32[177,8,128]{2,1,0:T(8,128)S(1)} %get-tuple-element.21.state_ref, f32[178,4,128]{2,1,0:T(4,128)S(1)} %collective-permute-done.3.came_ref), custom_call_target="tpu_custom_call" | custom-call | tf_op jit(solution)/shard_map/prepare/pallas_call | solution.py:584
  25.4 0.4 %collective-permute-done.5.refs_0_ = f32[2,16,128]{2,1,0:T(8,128)S(1)} collective-permute-done((f32[2,16,128]{2,1,0:T(8,128)S(1)}, f32[2,16,128]{2,1,0:T(8,128)S(1)}, u32[]{:S(2)}, u32[]{:S(2)}) %collective-permute-start.5) | collective-permute-done | bytes 16416 | tf_op jit(solution)/shard_map/ppermute | solution.py:529
  25.8 0.6 %collective-permute-done.6.refs_1_ = f32[2,16,128]{2,1,0:T(8,128)S(1)} collective-permute-done((f32[2,16,128]{2,1,0:T(8,128)S(1)}, f32[2,16,128]{2,1,0:T(8,128)S(1)}, u32[]{:S(2)}, u32[]{:S(2)}) %collective-permute-start.6) | collective-permute-done | bytes 16416 | tf_op jit(solution)/shard_map/ppermute | solution.py:529
  26.3 0.2 collective-permute-done.7.refs_2_
  26.5 1.0 %update.1 = (f32[59,8,128]{2,1,0:T(8,128)}, f32[59,8,128]{2,1,0:T(8,128)}, f32[59,8,128]{2,1,0:T(8,128)}, f32[3,8,128]{2,1,0:T(8,128)}) custom-call(f32[177,8,128]{2,1,0:T(8,128)S(1)} %get-tuple-element.24.mixed_ref, f32[77,8,128]{2,1,0:T(8,128)S(1)} %get-tuple-element.25.slope_ref, f32[3,8,128]{2,1,0:T(8,128)S(1)} %get-tuple-element.30.image_ref, ...), custom_call_target="tpu_custom_call" | custom-call | tf_op jit(solution)/shard_map/update/pallas_call | solution.py:597
  (1 shorter events, 0.0 us)
Async XLA Ops:
  1.7 7.1 %collective-permute-start.2 = (f32[9,8,128]{2,1,0:T(8,128)S(1)}, f32[9,8,128]{2,1,0:T(8,128)S(1)}, u32[]{:S(2)}, u32[]{:S(2)}) collective-permute-start(f32[9,8,128]{2,1,0:T(8,128)S(1)} %project.1.refs_3_), channel_id=1, source_target_pairs={{0,3},{1,2},{2,1},{3,0},{4,7},{5,6},{6,5},{7,4},{8,11},{9,10},{10,... | collective-permute-start | bytes 110600 | tf_op jit(solution)/shard_map/ppermute | solution.py:529
  6.8 4.9 %collective-permute-start.1 = (f32[9,8,128]{2,1,0:T(8,128)S(1)}, f32[9,8,128]{2,1,0:T(8,128)S(1)}, u32[]{:S(2)}, u32[]{:S(2)}) collective-permute-start(f32[9,8,128]{2,1,0:T(8,128)S(1)} %project.1.refs_3_), channel_id=1, source_target_pairs={{0,2},{1,3},{2,0},{3,1},{4,6},{5,7},{6,4},{7,5},{8,10},{9,11},{10,... | collective-permute-start | bytes 110600 | tf_op jit(solution)/shard_map/ppermute | solution.py:529
  6.8 4.9 %collective-permute-start = (f32[9,8,128]{2,1,0:T(8,128)S(1)}, f32[9,8,128]{2,1,0:T(8,128)S(1)}, u32[]{:S(2)}, u32[]{:S(2)}) collective-permute-start(f32[9,8,128]{2,1,0:T(8,128)S(1)} %project.1.refs_3_), channel_id=1, source_target_pairs={{0,1},{1,0},{2,3},{3,2},{4,5},{5,4},{6,7},{7,6},{8,9},{9,8},{10,11... | collective-permute-start | bytes 110600 | tf_op jit(solution)/shard_map/ppermute | solution.py:529
  7.4 4.2 %copy-start = (f32[1,3,1024]{2,0,1:T(1,128)S(1)}, f32[1,3,1024]{2,0,1:T(1,128)}, u32[]{:S(2)}) copy-start(f32[1,3,1024]{2,0,1:T(1,128)} %param.11) | copy-start | bytes 36868
  11.6 13.0 %collective-permute-start.3 = (f32[178,4,128]{2,1,0:T(4,128)S(1)}, f32[178,4,128]{2,1,0:T(4,128)S(1)}, u32[]{:S(2)}, u32[]{:S(2)}) collective-permute-start(f32[178,4,128]{2,1,0:T(4,128)S(1)} %get-tuple-element.23), channel_id=1, source_target_pairs={{0,4},{4,8},{8,12},{12,16},{16,20},{20,24},{24,28},{28,0},{1,5},{5... | collective-permute-start | bytes 1093640 | tf_op jit(solution)/shard_map/ppermute | solution.py:532
  15.9 4.3 %collective-permute-start.4 = (f32[4,16,128]{2,1,0:T(8,128)S(1)}, f32[4,16,128]{2,1,0:T(8,128)S(1)}, u32[]{:S(2)}, u32[]{:S(2)}) collective-permute-start(f32[4,16,128]{2,1,0:T(8,128)S(1)} %get-tuple-element.31), channel_id=1, source_target_pairs={{0,4},{4,8},{8,12},{12,16},{16,20},{20,24},{24,28},{28,0},{1,5},{5... | collective-permute-start | bytes 98312 | tf_op jit(solution)/shard_map/ppermute | solution.py:532
  20.2 5.5 %collective-permute-start.5 = (f32[2,16,128]{2,1,0:T(8,128)S(1)}, f32[2,16,128]{2,1,0:T(8,128)S(1)}, u32[]{:S(2)}, u32[]{:S(2)}) collective-permute-start(f32[2,16,128]{2,1,0:T(8,128)S(1)} %get-tuple-element.45), channel_id=1, source_target_pairs={{0,3},{1,2},{2,1},{3,0},{4,7},{5,6},{6,5},{7,4},{8,11},{9,10},{10,... | collective-permute-start | bytes 49160 | tf_op jit(solution)/shard_map/ppermute | solution.py:529
  21.7 4.7 %collective-permute-start.6 = (f32[2,16,128]{2,1,0:T(8,128)S(1)}, f32[2,16,128]{2,1,0:T(8,128)S(1)}, u32[]{:S(2)}, u32[]{:S(2)}) collective-permute-start(f32[2,16,128]{2,1,0:T(8,128)S(1)} %get-tuple-element.46), channel_id=1, source_target_pairs={{0,2},{1,3},{2,0},{3,1},{4,6},{5,7},{6,4},{7,5},{8,10},{9,11},{10,... | collective-permute-start | bytes 49160 | tf_op jit(solution)/shard_map/ppermute | solution.py:529
  22.3 4.2 %collective-permute-start.7 = (f32[2,16,128]{2,1,0:T(8,128)S(1)}, f32[2,16,128]{2,1,0:T(8,128)S(1)}, u32[]{:S(2)}, u32[]{:S(2)}) collective-permute-start(f32[2,16,128]{2,1,0:T(8,128)S(1)} %get-tuple-element.47), channel_id=1, source_target_pairs={{0,1},{1,0},{2,3},{3,2},{4,5},{5,4},{6,7},{7,6},{8,9},{9,8},{10,11... | collective-permute-start | bytes 49160 | tf_op jit(solution)/shard_map/ppermute | solution.py:529

commit v8 on v7

--- a/solution.py
+++ b/solution.py
@@ -377,7 +377,15 @@
 TERMS = 2 + 3 * 8 + 1 + 3 * SH
 
 
-def prepare_kernel(mine_ref, basis_hbm, state_ref, came_ref, mixed_ref, slope_ref, kbuf, basis_ref, sem):
+def gather_grads(grads, ref, want, taken):
+    wide = lambda row: jnp.broadcast_to(row, want.shape)
+    for side in range(2):
+        mask = jnp.logical_and(want == wide(ref[side, NPROJ : NPROJ + 1, :]), taken if side else ~taken)
+        grads = [grads[r] + jnp.where(mask, wide(ref[side, r : r + 1, :]), 0.0) for r in range(NPROJ)]
+    return grads
+
+
+def prepare_kernel(mine_ref, basis_hbm, state_ref, came_ref, near_ref, mixed_ref, slope_ref, early_ref, kbuf, basis_ref, sem):
     fetch = pltpu.make_async_copy(basis_hbm, basis_ref, sem.at[0])
     fetch.start()
     total, blocks, lanes = state_ref.shape
@@ -397,6 +405,9 @@
     slot = lax.broadcasted_iota(jnp.int32, (blocks, lanes), 0).astype(jnp.float32)
     slope_ref[TERMS] = jnp.where(taken, arrived(total), slot)
     slope_ref[TERMS + 1] = taken.astype(jnp.float32)
+    start = [jnp.zeros((blocks, lanes), jnp.float32) for _ in range(NPROJ)]
+    for r, value in enumerate(gather_grads(start, near_ref, slope_ref[TERMS], taken)):
+        early_ref[r] = value
 
     part = 1.0 - beta_one
     p = lambda i: mixed_ref[i]
@@ -445,7 +456,7 @@
             slope_ref[14 + 3 * k + n] = part * (gq[k] - unit * along) * v["inv"]
 
 
-def update_kernel(mixed_ref, slope_ref, image_ref, *refs):
+def update_kernel(mixed_ref, slope_ref, early_ref, image_ref, *refs):
     sources = refs[:-9]
     outs = refs[-9:-6]
     picture_hbm = refs[-6]
@@ -457,13 +468,9 @@
     picture.start()
     want = slope_ref[TERMS]
     taken = slope_ref[TERMS + 1] > 0.5
-    wide = lambda row: jnp.broadcast_to(row, (blocks, lanes))
-    grads = [jnp.zeros((blocks, lanes), jnp.float32) for _ in range(NPROJ)]
+    grads = [early_ref[r] for r in range(NPROJ)]
     for ref in sources:
-        for side in range(2):
-            mask = jnp.logical_and(want == wide(ref[side, NPROJ : NPROJ + 1, :]), taken if side else ~taken)
-            for r in range(NPROJ):
-                grads[r] = grads[r] + jnp.where(mask, wide(ref[side, r : r + 1, :]), 0.0)
+        grads = gather_grads(grads, ref, want, taken)
 
     def store(i, grad):
         one = mixed_ref[rows + i] + grad
@@ -581,17 +588,17 @@
         name="composite",
     )(place, *[away[d] for d in reversed(range(peers))], target.reshape(3, chunks, lanes))
     passed = onward(slots)
-    mixed, slope = pl.pallas_call(
+    pairs = jnp.stack([slots, passed], axis=1)
+    mixed, slope, early = pl.pallas_call(
         prepare_kernel,
-        out_shape=(sds((3 * rows, blocks, lanes), f32), sds((TERMS + 2, blocks, lanes), f32)),
-        in_specs=[vmem, hbm, vmem, vmem],
-        out_specs=(vmem, vmem),
+        out_shape=(sds((3 * rows, blocks, lanes), f32), sds((TERMS + 2, blocks, lanes), f32), sds((NPROJ, blocks, lanes), f32)),
+        in_specs=[vmem, hbm, vmem, vmem, vmem],
+        out_specs=(vmem,) * 3,
         scratch_shapes=[pltpu.VMEM((8, blocks, lanes), f32), pltpu.SMEM(view_basis.shape, f32), dma((1,))],
         compiler_params=pltpu.CompilerParams(vmem_limit_bytes=5 << 20),
         name="prepare",
-    )(mine, stay(view_basis), state, came)
-    pairs = jnp.stack([slots, passed], axis=1)
-    gathered = {0: pairs[0]}
+    )(mine, stay(view_basis), state, came, pairs[0])
+    gathered = {}
     for d in range(1, peers):
         gathered[d] = swapped(pairs[d], d)
     updated = pl.pallas_call(
@@ -602,7 +609,7 @@
         scratch_shapes=[pltpu.VMEM((rows, blocks, lanes), f32)] * 3 + [dma((12,)), dma((1,))],
         compiler_params=pltpu.CompilerParams(vmem_limit_bytes=5 << 20),
         name="update",
-    )(mixed, slope, image, *[gathered[d] for d in reversed(range(peers))])
+    )(mixed, slope, early, image, *[gathered[d] for d in reversed(range(1, peers))])
     turned_back = [jnp.transpose(a, (1, 0, 2)) for a in updated[:3]]
     return (*turned_back, updated[3].reshape(1, 3, pixels))
 

time: 27.8 us -> 29.6 us (1.065)
  waiting for transfers between devices: 6.69 us -> 9.43 us
  starting transfers between devices: 11.8 us -> 10.9 us
    ppermute x6, waiting for transfers between devices: 4.04 us -> 6.78 us  [swapped(): return lax.ppermute(value, 'tile', [(i, i ^ d) for i in range(peers)])]
    ppermute x6, starting transfers between devices: 10.1 us -> 9.24 us  [swapped(): return lax.ppermute(value, 'tile', [(i, i ^ d) for i in range(peers)])]
  transfers between devices with their start and end apart: 8 -> 8, of which waited for: 5 -> 4; matrix products, arithmetic and copies ran while one was open for 0% -> 0% of each run, Pallas kernels for 23% -> 21%
where the time goes in v8:
time: 29.6 us; the launch traced here: 29.4 us
  starting transfers between devices  10.9 us (37%)
  waiting for transfers between devices  9.43 us (32%)
  Pallas kernels  8.34 us (28%)
  between operations  0.68 us (2%)
    ppermute x6, starting transfers between devices, swapped(): return lax.ppermute(value, 'tile', [(i, i ^ d) for i in range(peers)])  9.24 us
    ppermute x6, waiting for transfers between devices, swapped(): return lax.ppermute(value, 'tile', [(i, i ^ d) for i in range(peers)])  6.78 us
    pallas_call x1, Pallas kernels, on_device(): pl.pallas_call(composite_kernel, out_shape=(sds((3, chunks, lanes), f32),...  4.27 us
    ppermute x2, waiting for transfers between devices, on_device(): lax.ppermute(value, 'region', [(i, (i + 1) % regions) for i in range(regi...  2.64 us
    ppermute x2, starting transfers between devices, on_device(): lax.ppermute(value, 'region', [(i, (i + 1) % regions) for i in range(regi...  1.65 us
    pallas_call x1, Pallas kernels, on_device(): pl.pallas_call(pack_kernel, out_shape=(sds((3 * rows + 1, moves, lanes),...  1.27 us
    pallas_call x1, Pallas kernels, on_device(): pl.pallas_call(project_kernel, out_shape=sds((NPROJ, blocks, lanes), f32)...  1.02 us
    pallas_call x1, Pallas kernels, on_device(): pl.pallas_call(update_kernel, out_shape=(sds((rows, blocks, lanes), f32),...  1.02 us
  transfers between devices with their start and end apart: 8, of which 4 were waited for; matrix products, arithmetic and copies ran while one was open for 0% of the time, Pallas kernels for 21%

profile of v8, /device:TPU:0, one launch (start us, length us, event | category | flops | bytes accessed | tf_op | source)
XLA Modules:
  0.0 29.4 jit_solution(13124516880578241934)
XLA Ops:
  0.6 1.0 %project.1.refs_3_ = f32[9,8,128]{2,1,0:T(8,128)S(1)} custom-call(f32[16]{0:T(128)} %basis_hbm.3, f32[59,8,128]{2,1,0:T(8,128)} %bitcast.20), custom_call_target="tpu_custom_call" | custom-call | tf_op jit(solution)/shard_map/project/pallas_call | solution.py:525
  1.7 5.1 %collective-permute-start.2 = (f32[9,8,128]{2,1,0:T(8,128)S(1)}, f32[9,8,128]{2,1,0:T(8,128)S(1)}, u32[]{:S(2)}, u32[]{:S(2)}) collective-permute-start(f32[9,8,128]{2,1,0:T(8,128)S(1)} %project.1.refs_3_), channel_id=1, source_target_pairs={{0,3},{1,2},{2,1},{3,0},{4,7},{5,6},{6,5},{7,4},{8,11},{9,10},{10,... | collective-permute-start | bytes 110600 | tf_op jit(solution)/shard_map/ppermute | solution.py:536
  6.8 0.0 collective-permute-start.1
  6.8 0.6 %collective-permute-start = (f32[9,8,128]{2,1,0:T(8,128)S(1)}, f32[9,8,128]{2,1,0:T(8,128)S(1)}, u32[]{:S(2)}, u32[]{:S(2)}) collective-permute-start(f32[9,8,128]{2,1,0:T(8,128)S(1)} %project.1.refs_3_), channel_id=1, source_target_pairs={{0,1},{1,0},{2,3},{3,2},{4,5},{5,4},{6,7},{7,6},{8,9},{9,8},{10,11... | collective-permute-start | bytes 110600 | tf_op jit(solution)/shard_map/ppermute | solution.py:536
  7.4 0.0 copy-start
  7.4 1.3 %pack.1 = (f32[178,4,128]{2,1,0:T(4,128)S(1)}, f32[177,8,128]{2,1,0:T(8,128)S(1)}, s32[2,8,128]{2,1,0:T(8,128)S(1)}, s32[2,4,8,128]{3,2,1,0:T(8,128)S(1)}) custom-call(s32[1,4]{1,0:T(1,128)} %moving_hbm.1, s32[1,4]{1,0:T(1,128)} %listed_hbm.1, f32[59,8,128]{2,1,0:T(8,128)} %bitcast.21, f32[59,8,128]{2,1,0:T(8,128)} %bitcast.22, f32[59,8,128]{2,1,0:T(8,128)} %bitcast.23), custom_call_target="tpu_custom_call" | custom-call | tf_op jit(solution)/shard_map/pack/pallas_call | solution.py:541
  8.7 0.0 collective-permute-done.2.refs_0_
  8.7 2.9 %collective-permute-done.1.refs_1_ = f32[9,8,128]{2,1,0:T(8,128)S(1)} collective-permute-done((f32[9,8,128]{2,1,0:T(8,128)S(1)}, f32[9,8,128]{2,1,0:T(8,128)S(1)}, u32[]{:S(2)}, u32[]{:S(2)}) %collective-permute-start.1) | collective-permute-done | bytes 36896 | tf_op jit(solution)/shard_map/ppermute | solution.py:536
  11.6 0.0 collective-permute-done.refs_2_
  11.6 0.0 collective-permute-start.3
  11.6 0.0 copy-done
  11.6 4.3 %composite.1 = (f32[3,8,128]{2,1,0:T(8,128)S(1)}, f32[4,16,128]{2,1,0:T(8,128)S(1)}) custom-call(s32[2,4,8,128]{3,2,1,0:T(8,128)S(1)} %get-tuple-element.25.place_ref, f32[9,8,128]{2,1,0:T(8,128)S(1)} %collective-permute-done.2.refs_0_, f32[9,8,128]{2,1,0:T(8,128)S(1)} %collective-permute-done.1.refs_1_, f32[9,8,128]{2,1,0:T(8,128)S(1)} %collective-permute-done.refs_2_, ...), custom_call_target="tpu_custom_call" | custom-call | flops 33554432 | bytes 25165824 | tf_op jit(solution)/shard_map/composite/pallas_call | solution.py:566
  15.9 1.6 %collective-permute-start.4 = (f32[4,16,128]{2,1,0:T(8,128)S(1)}, f32[4,16,128]{2,1,0:T(8,128)S(1)}, u32[]{:S(2)}, u32[]{:S(2)}) collective-permute-start(f32[4,16,128]{2,1,0:T(8,128)S(1)} %get-tuple-element.29), channel_id=1, source_target_pairs={{0,4},{4,8},{8,12},{12,16},{16,20},{20,24},{24,28},{28,0},{1,5},{5... | collective-permute-start | bytes 98312 | tf_op jit(solution)/shard_map/ppermute | solution.py:539
  17.6 2.6 %collective-permute-done.4 = f32[4,16,128]{2,1,0:T(8,128)S(1)} collective-permute-done((f32[4,16,128]{2,1,0:T(8,128)S(1)}, f32[4,16,128]{2,1,0:T(8,128)S(1)}, u32[]{:S(2)}, u32[]{:S(2)}) %collective-permute-start.4) | collective-permute-done | bytes 32800 | tf_op jit(solution)/shard_map/ppermute | solution.py:539
  20.2 0.0 collective-permute-start.7
  20.2 3.5 %collective-permute-start.5 = (f32[2,16,128]{2,1,0:T(8,128)S(1)}, f32[2,16,128]{2,1,0:T(8,128)S(1)}, u32[]{:S(2)}, u32[]{:S(2)}) collective-permute-start(f32[2,16,128]{2,1,0:T(8,128)S(1)} %get-tuple-element.48), channel_id=1, source_target_pairs={{0,3},{1,2},{2,1},{3,0},{4,7},{5,6},{6,5},{7,4},{8,11},{9,10},{10,... | collective-permute-start | bytes 49160 | tf_op jit(solution)/shard_map/ppermute | solution.py:536
  23.7 0.0 collective-permute-start.6
  23.7 0.0 collective-permute-done.3.came_ref
  23.7 0.8 %prepare.1 = (f32[177,8,128]{2,1,0:T(8,128)S(1)}, f32[77,8,128]{2,1,0:T(8,128)S(1)}, f32[9,8,128]{2,1,0:T(8,128)S(1)}) custom-call(s32[2,8,128]{2,1,0:T(8,128)S(1)} %get-tuple-element.21.mine_ref, f32[16]{0:T(128)} %basis_hbm.3, f32[177,8,128]{2,1,0:T(8,128)S(1)} %get-tuple-element.22.state_ref, f32[178,4,128]{2,1,0:T(4,128)S(1)} %collective-permute-done.3.came_ref, ...), custom_call_target="tpu_custom_call" | custom-call | tf_op jit(solution)/shard_map/prepare/pallas_call | solution.py:592
  24.5 0.0 collective-permute-done.7.refs_2_
  24.5 1.3 %collective-permute-done.5.refs_0_ = f32[2,16,128]{2,1,0:T(8,128)S(1)} collective-permute-done((f32[2,16,128]{2,1,0:T(8,128)S(1)}, f32[2,16,128]{2,1,0:T(8,128)S(1)}, u32[]{:S(2)}, u32[]{:S(2)}) %collective-permute-start.5) | collective-permute-done | bytes 16416 | tf_op jit(solution)/shard_map/ppermute | solution.py:536
  25.8 2.5 %collective-permute-done.6.refs_1_ = f32[2,16,128]{2,1,0:T(8,128)S(1)} collective-permute-done((f32[2,16,128]{2,1,0:T(8,128)S(1)}, f32[2,16,128]{2,1,0:T(8,128)S(1)}, u32[]{:S(2)}, u32[]{:S(2)}) %collective-permute-start.6) | collective-permute-done | bytes 16416 | tf_op jit(solution)/shard_map/ppermute | solution.py:536
  28.3 1.0 %update.1 = (f32[59,8,128]{2,1,0:T(8,128)}, f32[59,8,128]{2,1,0:T(8,128)}, f32[59,8,128]{2,1,0:T(8,128)}, f32[3,8,128]{2,1,0:T(8,128)}) custom-call(f32[177,8,128]{2,1,0:T(8,128)S(1)} %get-tuple-element.30.mixed_ref, f32[77,8,128]{2,1,0:T(8,128)S(1)} %get-tuple-element.31.slope_ref, f32[9,8,128]{2,1,0:T(8,128)S(1)} %get-tuple-element.32.early_ref, ...), custom_call_target="tpu_custom_call" | custom-call | tf_op jit(solution)/shard_map/update/pallas_call | solution.py:604
  (1 shorter events, 0.0 us)
Async XLA Ops:
  1.7 7.1 %collective-permute-start.2 = (f32[9,8,128]{2,1,0:T(8,128)S(1)}, f32[9,8,128]{2,1,0:T(8,128)S(1)}, u32[]{:S(2)}, u32[]{:S(2)}) collective-permute-start(f32[9,8,128]{2,1,0:T(8,128)S(1)} %project.1.refs_3_), channel_id=1, source_target_pairs={{0,3},{1,2},{2,1},{3,0},{4,7},{5,6},{6,5},{7,4},{8,11},{9,10},{10,... | collective-permute-start | bytes 110600 | tf_op jit(solution)/shard_map/ppermute | solution.py:536
  6.8 4.9 %collective-permute-start.1 = (f32[9,8,128]{2,1,0:T(8,128)S(1)}, f32[9,8,128]{2,1,0:T(8,128)S(1)}, u32[]{:S(2)}, u32[]{:S(2)}) collective-permute-start(f32[9,8,128]{2,1,0:T(8,128)S(1)} %project.1.refs_3_), channel_id=1, source_target_pairs={{0,2},{1,3},{2,0},{3,1},{4,6},{5,7},{6,4},{7,5},{8,10},{9,11},{10,... | collective-permute-start | bytes 110600 | tf_op jit(solution)/shard_map/ppermute | solution.py:536
  6.8 4.9 %collective-permute-start = (f32[9,8,128]{2,1,0:T(8,128)S(1)}, f32[9,8,128]{2,1,0:T(8,128)S(1)}, u32[]{:S(2)}, u32[]{:S(2)}) collective-permute-start(f32[9,8,128]{2,1,0:T(8,128)S(1)} %project.1.refs_3_), channel_id=1, source_target_pairs={{0,1},{1,0},{2,3},{3,2},{4,5},{5,4},{6,7},{7,6},{8,9},{9,8},{10,11... | collective-permute-start | bytes 110600 | tf_op jit(solution)/shard_map/ppermute | solution.py:536
  7.4 4.2 %copy-start = (f32[1,3,1024]{2,0,1:T(1,128)S(1)}, f32[1,3,1024]{2,0,1:T(1,128)}, u32[]{:S(2)}) copy-start(f32[1,3,1024]{2,0,1:T(1,128)} %param.11) | copy-start | bytes 36868
  11.6 12.1 %collective-permute-start.3 = (f32[178,4,128]{2,1,0:T(4,128)S(1)}, f32[178,4,128]{2,1,0:T(4,128)S(1)}, u32[]{:S(2)}, u32[]{:S(2)}) collective-permute-start(f32[178,4,128]{2,1,0:T(4,128)S(1)} %get-tuple-element.24), channel_id=1, source_target_pairs={{0,4},{4,8},{8,12},{12,16},{16,20},{20,24},{24,28},{28,0},{1,5},{5... | collective-permute-start | bytes 1093640 | tf_op jit(solution)/shard_map/ppermute | solution.py:539
  15.9 4.3 %collective-permute-start.4 = (f32[4,16,128]{2,1,0:T(8,128)S(1)}, f32[4,16,128]{2,1,0:T(8,128)S(1)}, u32[]{:S(2)}, u32[]{:S(2)}) collective-permute-start(f32[4,16,128]{2,1,0:T(8,128)S(1)} %get-tuple-element.29), channel_id=1, source_target_pairs={{0,4},{4,8},{8,12},{12,16},{16,20},{20,24},{24,28},{28,0},{1,5},{5... | collective-permute-start | bytes 98312 | tf_op jit(solution)/shard_map/ppermute | solution.py:539
  20.2 4.3 %collective-permute-start.7 = (f32[2,16,128]{2,1,0:T(8,128)S(1)}, f32[2,16,128]{2,1,0:T(8,128)S(1)}, u32[]{:S(2)}, u32[]{:S(2)}) collective-permute-start(f32[2,16,128]{2,1,0:T(8,128)S(1)} %get-tuple-element.46), channel_id=1, source_target_pairs={{0,1},{1,0},{2,3},{3,2},{4,5},{5,4},{6,7},{7,6},{8,9},{9,8},{10,11... | collective-permute-start | bytes 49160 | tf_op jit(solution)/shard_map/ppermute | solution.py:536
  20.2 5.6 %collective-permute-start.5 = (f32[2,16,128]{2,1,0:T(8,128)S(1)}, f32[2,16,128]{2,1,0:T(8,128)S(1)}, u32[]{:S(2)}, u32[]{:S(2)}) collective-permute-start(f32[2,16,128]{2,1,0:T(8,128)S(1)} %get-tuple-element.48), channel_id=1, source_target_pairs={{0,3},{1,2},{2,1},{3,0},{4,7},{5,6},{6,5},{7,4},{8,11},{9,10},{10,... | collective-permute-start | bytes 49160 | tf_op jit(solution)/shard_map/ppermute | solution.py:536
  23.7 4.6 %collective-permute-start.6 = (f32[2,16,128]{2,1,0:T(8,128)S(1)}, f32[2,16,128]{2,1,0:T(8,128)S(1)}, u32[]{:S(2)}, u32[]{:S(2)}) collective-permute-start(f32[2,16,128]{2,1,0:T(8,128)S(1)} %get-tuple-element.49), channel_id=1, source_target_pairs={{0,2},{1,3},{2,0},{3,1},{4,6},{5,7},{6,4},{7,5},{8,10},{9,11},{10,... | collective-permute-start | bytes 49160 | tf_op jit(solution)/shard_map/ppermute | solution.py:536
